TPU v7x, 128 devices: a whole 4x4x4 slice. The times are simulated.
128 devices in a mesh: seq: 8 (over z, core), head: 16 (over x, y).
Axes of the slice: x: 4, y: 4, z: 4, core: 2. Of those that a mesh axis runs over, the one named last changes fastest.
Arguments:
- query_raw: bfloat16 [8192, 8192], P('seq', 'head'), may hold values from -12 to 12
- key_raw: bfloat16 [8192, 8192], P('seq', 'head'), may hold values from -6 to 6
- value_raw: bfloat16 [8192, 8192], P('seq', 'head'), may hold values from -6 to 6
- query_gain: float32 [8192], P('head'), may hold values from 0.1 to 1.9
- log_decay: float32 [64, 8192], P('head', 'seq'), may hold values from -1.5 to 0
- out_grad: bfloat16 [8192, 8192], P('seq', 'head'), may hold values from -0.75 to 0.75
Outputs:
- query_raw_grad: bfloat16 [8192, 8192], P(('seq', 'head'))
- key_raw_grad: bfloat16 [8192, 8192], P(('seq', 'head'))
- value_raw_grad: bfloat16 [8192, 8192], P(('seq', 'head'))
All inputs are finite; a program needn't handle non-finite values.
Results may differ from a plain program's by a relative error of at most 0.0021.
Values may be sent and summed in bfloat16 or wider, within the bound.
No kernel may reach another device: no remote copies, remote signals or barrier semaphores. Data moves between devices by JAX's collectives and lax.ppermute only.
A program may use at most 128 MiB of HBM per device.

v0:
```python
import functools

import jax
import jax.numpy as jnp
from jax import lax
from jax.sharding import Mesh
from jax.sharding import PartitionSpec as P

D = 8192
BLOCK = 128
HEAD = ("head_0", "head_1")
SEQ = ("seq_0", "seq_1")
SEQ_HEAD = ("seq_0", "seq_1", "head_0", "head_1")


epsilon = 1e-06


def from_everyone(value, axis):
    length = lax.axis_size(axis)
    return lax.all_to_all(
        jnp.broadcast_to(value[None], (length, *value.shape)), axis, 0, 0, tiled=True
    )


def taken_together(value, axis):
    return from_everyone(value, axis).sum(axis=0)


def carried_in(value, axis, combine, identity):
    length, mine = (lax.axis_size(axis), lax.axis_index(axis))
    everything = jax.tree.map(lambda part: lax.all_gather(part, axis), value)
    start = jax.tree.map(
        lambda part, zero: jnp.broadcast_to(jnp.asarray(zero, part.dtype), part.shape),
        value,
        identity,
    )

    def lap(k, before):
        reached = k < mine
        new = combine(before, jax.tree.map(lambda part: part[k], everything))
        return jax.tree.map(lambda a, b: jnp.where(reached, a, b), new, before)

    return lax.fori_loop(0, length, lap, start)


def nothing_yet(value, identity):
    return jax.tree.map(
        lambda part, zero: jnp.zeros_like(part) + jnp.asarray(zero, part.dtype), value, identity
    )


def carried_in_2(value, axes, combine, identity):
    before = start = nothing_yet(value, identity)
    subtotal = value
    for axis in reversed(axes):
        length, mine = (lax.axis_size(axis), lax.axis_index(axis))
        pieces = jax.tree.map(lambda part: lax.all_gather(part, axis), subtotal)
        inside, subtotal = (start, start)
        for k in reversed(range(length)):
            passed = k > mine
            subtotal = combine(subtotal, jax.tree.map(lambda part: part[k], pieces))
            inside = jax.tree.map(lambda new, old: jnp.where(passed, new, old), subtotal, inside)
        before = combine(inside, before)
    return before


def by_axis(value, axes):
    return functools.reduce(lax.psum, axes, value)


def exact_prod(form, left, right):
    return jnp.einsum(form, left, right, precision=lax.Precision.HIGHEST)


def block_parts(queries, keys, gates):
    size = gates.shape[0]
    cumul = jnp.cumsum(gates)
    element_slot = lax.broadcasted_iota(jnp.int32, (size, size), 0)
    column = lax.broadcasted_iota(jnp.int32, (size, size), 1)
    causal = element_slot >= column
    strict = element_slot > column
    spread = jnp.where(causal, cumul[:, None] - cumul[None, :], 0.0)
    weights = jnp.where(causal, jnp.exp(spread), 0.0)
    lower = jnp.where(strict, 2.0 * weights * exact_prod("ik,jk->ij", keys, keys), 0.0)
    system = lower + jnp.eye(size, dtype=jnp.float32)
    mixing = 2.0 * weights * exact_prod("ik,jk->ij", queries, keys)
    start_decay = jnp.exp(cumul)
    end_decay = jnp.exp(cumul[-1] - cumul)
    return (system, mixing, start_decay, end_decay, start_decay[-1])


def solve_lower(system, target):
    return lax.linalg.triangular_solve(
        system, target, left_side=True, lower=True, unit_diagonal=True
    )


def block_forward(queries, keys, values, start_state, gates):
    system, mixing, start_decay, end_decay, total = block_parts(queries, keys, gates)
    target = values - start_decay[:, None] * exact_prod("ik,kv->iv", keys, start_state)
    fresh = solve_lower(system, target)
    outputs = start_decay[:, None] * exact_prod("ik,kv->iv", queries, start_state) + exact_prod(
        "ij,jv->iv", mixing, fresh
    )
    end_state = total * start_state + 2.0 * exact_prod(
        "ik,iv->kv", keys, end_decay[:, None] * fresh
    )
    return (outputs, end_state)


def block_maps(queries, keys, values, gates, grad_out):
    system, mixing, start_decay, end_decay, total = block_parts(queries, keys, gates)
    width = keys.shape[1]
    both = solve_lower(system, jnp.concatenate([values, start_decay[:, None] * keys], axis=1))
    initial_amount = both[:, : values.shape[1]]
    weight = both[:, values.shape[1] :]
    transition = total * jnp.eye(width, dtype=jnp.float32) - 2.0 * exact_prod(
        "ik,ij->kj", keys, end_decay[:, None] * weight
    )
    displacement = 2.0 * exact_prod("ik,iv->kv", keys, end_decay[:, None] * initial_amount)
    inner = exact_prod("ij,iv->jv", mixing, grad_out)
    adjoint = exact_prod("ik,iv->kv", start_decay[:, None] * queries, grad_out) - exact_prod(
        "jk,jv->kv", weight, inner
    )
    return (transition, displacement, adjoint)


def block_grads(queries, keys, values, start_state, gates, grad_out, end_grad):

    def forward(query_part, key_part, value_part):
        return block_forward(query_part, key_part, value_part, start_state, gates)

    _, pullback = jax.vjp(forward, queries, keys, values)
    return pullback((grad_out, end_grad))


def batched(function):
    return jax.vmap(jax.vmap(function))


def compose(earlier, later):
    return (
        exact_prod("hij,hjk->hik", later[0], earlier[0]),
        exact_prod("hij,hjk->hik", later[0], earlier[1]) + later[1],
    )


def per_device(query_raw, key_raw, value_raw, query_gain, log_decay, out_grad):
    rows, width = query_raw.shape
    heads = log_decay.shape[0]
    head_dim = width // heads
    blocks = rows // BLOCK
    raw_query = query_raw.astype(jnp.float32)
    squares = taken_together(jnp.sum(raw_query * raw_query, axis=1), HEAD)
    inv_rms = lax.rsqrt(squares / D + epsilon)
    normed = raw_query * inv_rms[:, None]
    scale = head_dim ** (-0.5)
    queries = normed * query_gain * scale
    raw_key = key_raw.astype(jnp.float32).reshape(rows, heads, head_dim)
    key_scale = lax.rsqrt(jnp.sum(raw_key * raw_key, axis=2, keepdims=True) + epsilon)
    keys = raw_key * key_scale

    def to_blocks(array):
        return array.reshape(blocks, BLOCK, heads, head_dim).transpose(2, 0, 1, 3)

    query_blocks = to_blocks(queries)
    key_blocks = to_blocks(keys)
    value_blocks = to_blocks(value_raw.astype(jnp.float32))
    grad_blocks = to_blocks(out_grad.astype(jnp.float32))
    gate_blocks = log_decay.reshape(heads, blocks, BLOCK)
    transitions, displacements, adjoints = batched(block_maps)(
        query_blocks, key_blocks, value_blocks, gate_blocks, grad_blocks
    )
    trans_seq = jnp.moveaxis(transitions, 1, 0)
    offset_seq = jnp.moveaxis(displacements, 1, 0)
    adjoint_seq = jnp.moveaxis(adjoints, 1, 0)
    identity = jnp.broadcast_to(jnp.eye(head_dim, dtype=jnp.float32), (heads, head_dim, head_dim))
    zeros = jnp.zeros((heads, head_dim, head_dim), jnp.float32)

    def gather_step(carry, item):
        return (compose(carry, item), None)

    (device_map, device_offset), _ = lax.scan(
        gather_step, (identity, zeros), (trans_seq, offset_seq)
    )

    def collect_adjoint(carry, item):
        matrix, term = item
        return (exact_prod("hji,hjk->hik", matrix, carry) + term, None)

    device_adjoint, _ = lax.scan(collect_adjoint, zeros, (trans_seq, adjoint_seq), reverse=True)
    _, incoming = carried_in((device_map, device_offset), SEQ, compose, (identity, zeros))
    back_map = jnp.swapaxes(device_map, 1, 2)
    _, outgoing = carried_in_2((back_map, device_adjoint), SEQ, compose, (identity, zeros))

    def advance(state_matrix, item):
        matrix, shift = item
        return (exact_prod("hij,hjk->hik", matrix, state_matrix) + shift, state_matrix)

    def retreat(adjoint_state, item):
        matrix, term = item
        return (exact_prod("hji,hjk->hik", matrix, adjoint_state) + term, adjoint_state)

    _, starts = lax.scan(advance, incoming, (trans_seq, offset_seq))
    _, ends = lax.scan(retreat, outgoing, (trans_seq, adjoint_seq), reverse=True)
    query_grad, key_grad, value_grad = batched(block_grads)(
        query_blocks,
        key_blocks,
        value_blocks,
        jnp.moveaxis(starts, 0, 1),
        gate_blocks,
        grad_blocks,
        jnp.moveaxis(ends, 0, 1),
    )

    def from_blocks(array):
        return array.transpose(1, 2, 0, 3).reshape(rows, width)

    key_grad_rows = key_grad.transpose(1, 2, 0, 3).reshape(rows, heads, head_dim)
    key_raw_grad = key_scale * (
        key_grad_rows - keys * jnp.sum(keys * key_grad_rows, axis=2, keepdims=True)
    )
    key_raw_grad = key_raw_grad.reshape(rows, width).astype(jnp.bfloat16)
    value_raw_grad = from_blocks(value_grad).astype(jnp.bfloat16)
    scaled = from_blocks(query_grad) * query_gain * scale
    correction = by_axis(jnp.sum(scaled * normed, axis=1), HEAD) / D
    query_raw_grad = (inv_rms[:, None] * (scaled - normed * correction[:, None])).astype(
        jnp.bfloat16
    )
    return (
        lax.all_to_all(query_raw_grad, HEAD, split_axis=0, concat_axis=1, tiled=True),
        lax.all_to_all(key_raw_grad, HEAD, split_axis=0, concat_axis=1, tiled=True),
        lax.all_to_all(value_raw_grad, HEAD, split_axis=0, concat_axis=1, tiled=True),
    )


def solution(mesh):
    split = Mesh(mesh.devices.reshape(4, 2, 4, 4), ("seq_0", "seq_1", "head_0", "head_1"))
    return jax.shard_map(
        per_device,
        mesh=split,
        in_specs=(P(SEQ, HEAD), P(SEQ, HEAD), P(SEQ, HEAD), P(HEAD), P(HEAD, SEQ), P(SEQ, HEAD)),
        out_specs=(P(SEQ_HEAD, None), P(SEQ_HEAD, None), P(SEQ_HEAD, None)),
        check_vma=False,
    )
```

profile of v0, /device:TPU:0, one launch (start us, length us, event | category | flops | bytes accessed | tf_op | source)
XLA Modules:
  0.0 694.1 jit_solution(8259316048077969374)
XLA Ops:
  24.6 6.5 add_bitcast_fusion.2
  31.1 315.8 %custom-call.8 = f32[4,8,1,128,128]{3,4,2,1,0:T(8,128)} custom-call(f32[4,8,1,128,128]{4,3,2,1,0:T(8,128)} %add_bitcast_fusion.2), custom_call_target="InvertDiagBlocksLowerTriangular" | custom-call | tf_op jit(solution)/shard_map/vmap(vmap())/triangular_solve | solution.py:94
  346.9 6.6 fusion.32
  353.5 5.4 multiply_bitcast_fusion.1
  359.0 4.7 bitcast_subtract_fusion
  367.2 22.9 %while.72 = (s32[]{:T(128)}, f32[4,128,128]{2,1,0:T(8,128)S(1)}, f32[4,128,128]{2,1,0:T(8,128)S(1)}, f32[8,4,128,128]{3,2,1,0:T(8,128)}, f32[8,4,128,128]{3,2,1,0:T(8,128)}, /*index=5*/s32[]{:T(128)}, s32[]{:T(128)}) while((s32[]{:T(128)}, f32[4,128,128]{2,1,0:T(8,128)S(1)}, f32[4,128,128]{2,1,0:T(8,128)S(1)}, ...), condition=%wide.region_5.6_spmd.clone, body=%wide.region_4.5_spmd.clone.sunk | while | flops 201457664 | bytes 2885218 | solution.py:184
  396.0 7.2 %all-to-all-start = ((f32[16,1,1024]{2,1,0:T(1,128)}), f32[16,1,1024]{2,1,0:T(1,128)}, u32[]{:S(2)}, u32[]{:S(2)}) async-start(f32[16,1,1024]{2,1,0:T(1,128)} %broadcast_in_dim.86), calls=%async_computation | async-start | bytes 131072 | tf_op jit(solution)/shard_map/all_to_all | solution.py:21
  415.5 3.4 all-gather.13.cloned.1.call-done
  419.0 27.4 %all-gather.11.cloned.1.call-done = f32[32,128,128]{2,1,0:T(8,128)} async-done(((f32[4,128,128]{2,1,0:T(8,128)}), f32[32,128,128]{2,1,0:T(8,128)}) %all-gather.11.cloned.1.call-update) | async-done | bytes 2097168 | tf_op jit(solution)/shard_map/all_gather | solution.py:32
  446.4 11.9 %while.73 = (s32[]{:T(128)}, f32[4,128,128]{2,1,0:T(8,128)S(1)}, s32[]{:T(128)}, f32[8,4,128,128]{3,2,1,0:T(8,128)}, f32[8,4,128,128]{3,2,1,0:T(8,128)}, /*index=5*/s32[]{:T(128)}, s32[]{:T(128)}) while((s32[]{:T(128)}, f32[4,128,128]{2,1,0:T(8,128)S(1)}, s32[]{:T(128)}, f32[8,4,128,128]{3,2,1,0:T(8,128)}, ...), condition=%wide.region_7.8_spmd.clone, body=%wide.region_6.7_spmd.clone.sunk | while | flops 100925440 | bytes 1837671 | solution.py:44
  459.9 18.0 %while.70 = (s32[]{:T(128)}, f32[4,128,128]{2,1,0:T(8,128)S(1)}, f32[8,4,128,128]{3,2,1,0:T(8,128)}, f32[8,4,128,128]{3,2,1,0:T(8,128)}, f32[8,4,128,128]{3,2,1,0:T(8,128)}, /*index=5*/s32[]{:T(128)}) while((s32[]{:T(128)}, f32[4,128,128]{2,1,0:T(8,128)S(1)}, f32[8,4,128,128]{3,2,1,0:T(8,128)}, f32[8,4,128,128]{3,2,1,0:T(8,128)}, ...), condition=%wide.region_9.10_spmd, body=%wide.region_8.9_spmd.sunk | while | flops 100728832 | bytes 2098257 | solution.py:205
  477.9 4.0 fusion.72
  481.9 4.0 fusion.60
  490.8 5.9 add_bitcast_fusion.1
  502.0 10.4 %psum.14 = f32[1024]{0:T(1024)S(1)} all-reduce(f32[1024]{0:T(1024)S(1)} %fusion.39), channel_id=1, replica_groups=mesh['seq_0'=4,'seq_1'=2,'head_0'=4,'head_1'=4] {'head_0'}, use_global_device_ids=true, to_apply=%region_11.12 | all-reduce | flops 1024 | bytes 8192 | tf_op jit(solution)/shard_map/psum | solution.py:69
  512.4 10.5 %psum.15 = f32[1024]{0:T(1024)S(1)} all-reduce(f32[1024]{0:T(1024)S(1)} %psum.14), channel_id=1, replica_groups=mesh['seq_0'=4,'seq_1'=2,'head_0'=4,'head_1'=4] {'head_1'}, use_global_device_ids=true, to_apply=%region_12.13 | all-reduce | flops 1024 | bytes 8192 | tf_op jit(solution)/shard_map/psum | solution.py:69
  531.0 6.2 fusion.53
  542.4 3.7 subtract_bitcast_fusion
  547.8 11.9 %while.74 = (s32[]{:T(128)}, f32[4,128,128]{2,1,0:T(8,128)S(1)}, f32[8,4,128,128]{2,3,1,0:T(8,128)}, f32[8,4,128,128]{3,2,1,0:T(8,128)}, s32[]{:T(128)}, /*index=5*/s32[]{:T(128)}, s32[]{:T(128)}) while((s32[]{:T(128)}, f32[4,128,128]{2,1,0:T(8,128)S(1)}, f32[8,4,128,128]{2,3,1,0:T(8,128)}, f32[8,4,128,128]{3,2,1,0:T(8,128)}, ...), condition=%wide.region_14.15_spmd.clone, body=%wide.region_13.14_spmd.clone.sunk | while | flops 100794368 | bytes 1574506 | solution.py:192
  567.3 4.4 all-to-all-start.1
  571.6 7.1 %fusion.51 = f32[4,8,128,128]{3,2,1,0:T(8,128)} fusion(f32[4,8,128,128]{3,2,1,0:T(8,128)} %copy-done.27, f32[4,8,128,128]{2,1,3,0:T(8,128)} %bitcast.275), kind=kOutput, calls=%fused_computation.66 | convolution fusion | flops 805306368 | bytes 6291456 | tf_op jit(solution)/shard_map/vmap(vmap(transpose(jvp(ik,jk->ij))))/dot_general | solution.py:73
  578.8 5.5 all-gather.17.cloned.1.call-done
  590.5 17.6 %while.71 = (s32[]{:T(128)}, f32[4,128,128]{2,1,0:T(8,128)S(1)}, f32[8,4,128,128]{3,2,1,0:T(8,128)}, f32[8,4,128,128]{2,3,1,0:T(8,128)}, f32[8,4,128,128]{3,2,1,0:T(8,128)}, /*index=5*/s32[]{:T(128)}, s32[]{:T(128)}) while((s32[]{:T(128)}, f32[4,128,128]{2,1,0:T(8,128)S(1)}, f32[8,4,128,128]{3,2,1,0:T(8,128)}, ...), condition=%wide.region_16.17_spmd, body=%wide.region_15.16_spmd.sunk | while | flops 100728832 | bytes 2098269 | solution.py:206
  608.1 4.4 multiply_add_fusion
  618.5 6.9 fusion.169
  625.4 5.8 fusion.84
  631.2 4.3 select_multiply_fusion
  635.5 7.0 %all-to-all-start.3 = ((bf16[16,64,512]{2,1,0:T(8,128)(2,1)}), bf16[16,64,512]{2,1,0:T(8,128)(2,1)S(1)}, u32[]{:S(2)}, u32[]{:S(2)}) async-start(bf16[16,64,512]{2,1,0:T(8,128)(2,1)} %convert_element_type.53), calls=%async_computation.3 | async-start | bytes 2097152 | tf_op jit(solution)/shard_map/all_to_all | solution.py:234
  642.5 6.7 fusion.79
  651.5 6.1 multiply_reduce_fusion
  664.2 7.3 %all-to-all-start.2 = ((bf16[16,64,512]{2,1,0:T(8,128)(2,1)}), bf16[16,64,512]{2,1,0:T(8,128)(2,1)S(1)}, u32[]{:S(2)}, u32[]{:S(2)}) async-start(bf16[16,64,512]{2,1,0:T(8,128)(2,1)} %bitcast.36), calls=%async_computation.2 | async-start | bytes 2097152 | tf_op jit(solution)/shard_map/all_to_all | solution.py:233
  674.9 11.3 %all-to-all-done.2 = bf16[16,64,512]{2,1,0:T(8,128)(2,1)S(1)} async-done(((bf16[16,64,512]{2,1,0:T(8,128)(2,1)}), bf16[16,64,512]{2,1,0:T(8,128)(2,1)S(1)}, u32[]{:S(2)}, u32[]{:S(2)}) %all-to-all-start.2) | async-done | bytes 1048608 | tf_op jit(solution)/shard_map/all_to_all | solution.py:233
  (306 shorter events, 178.7 us)
Async XLA Ops:
  7.2 411.8 %all-gather.13.cloned.1.call-start = ((), (), s32[]{:S(2)}) async-start(), calls=%async_computation.5 | async-start | bytes 2359296 | tf_op jit(solution)/shard_map/all_gather | solution.py:32
  10.0 4.7 copy-start.39
  15.4 4.9 copy-start.13
  353.5 5.5 copy-start.1
  353.5 5.5 copy-start.53
  390.8 55.6 %all-gather.11.cloned.1.call-start = ((), (), s32[]{:S(2)}) async-start(), calls=%async_computation.4 | async-start | bytes 2359296 | tf_op jit(solution)/shard_map/all_gather | solution.py:32
  391.6 11.7 %copy-start.16 = (f32[4,128,128]{2,1,0:T(8,128)S(1)}, f32[4,128,128]{2,1,0:T(8,128)}, u32[]{:S(2)}) copy-start(f32[4,128,128]{2,1,0:T(8,128)} %copy-done.15) | copy-start | bytes 786436
  396.0 16.7 %all-to-all-start = ((f32[16,1,1024]{2,1,0:T(1,128)}), f32[16,1,1024]{2,1,0:T(1,128)}, u32[]{:S(2)}, u32[]{:S(2)}) async-start(f32[16,1,1024]{2,1,0:T(1,128)} %broadcast_in_dim.86), calls=%async_computation | async-start | bytes 131072 | tf_op jit(solution)/shard_map/all_to_all | solution.py:21
  403.2 175.5 %all-gather.15.cloned.1.call-start = ((), (), s32[]{:S(2)}) async-start(), calls=%async_computation.6 | async-start | bytes 1310720 | tf_op jit(solution)/shard_map/all_gather | solution.py:58
  408.2 176.1 %all-gather.17.cloned.1.call-start = ((), (), s32[]{:S(2)}) async-start(), calls=%async_computation.7 | async-start | bytes 1310720 | tf_op jit(solution)/shard_map/all_gather | solution.py:58
  412.7 78.0 %copy-start.22 = (bf16[8,128,4,128]{3,2,1,0:T(4,128)(2,1)}, bf16[8,128,4,128]{3,2,1,0:T(4,128)(2,1)S(1)}, u32[]{:S(2)}) copy-start(bf16[8,128,4,128]{3,2,1,0:T(4,128)(2,1)S(1)} %reshape.159) | copy-start | bytes 3145732
  477.9 4.1 copy-start.4
  477.9 4.1 copy-start.14
  481.9 4.1 copy-start.48
  531.0 6.2 copy-start.10
  531.0 6.2 copy-start.23
  547.8 14.6 %copy-start.21 = (f32[8,128,128]{2,1,0:T(8,128)S(1)}, f32[8,128,128]{2,1,0:T(8,128)}, u32[]{:S(2)}) copy-start(f32[8,128,128]{2,1,0:T(8,128)} %copy-done.20) | copy-start | bytes 1572868
  559.6 4.3 copy-start.36
  559.7 4.3 copy-start.38
  562.7 4.5 copy-start.34
  567.3 68.2 %all-to-all-start.1 = ((bf16[16,64,512]{2,1,0:T(8,128)(2,1)}), bf16[16,64,512]{2,1,0:T(8,128)(2,1)}, u32[]{:S(2)}, u32[]{:S(2)}) async-start(bf16[16,64,512]{2,1,0:T(8,128)(2,1)} %bitcast.21), calls=%async_computation.1 | async-start | bytes 2097152 | tf_op jit(solution)/shard_map/all_to_all | solution.py:232
  578.8 8.4 %copy-start.32 = (f32[16,128,128]{2,1,0:T(8,128)S(1)}, f32[16,128,128]{2,1,0:T(8,128)}, u32[]{:S(2)}) copy-start(f32[16,128,128]{2,1,0:T(8,128)} %all-gather.15.cloned.1.call-done) | copy-start | bytes 3145732
  608.1 4.4 copy-start.5
  618.5 6.9 copy-start.8
  618.5 6.9 copy-start.12
  625.4 5.8 copy-start.6
  625.4 5.8 copy-start.45
  625.4 5.8 copy-start.50
  625.4 5.8 copy-start.52
  635.5 28.8 %all-to-all-start.3 = ((bf16[16,64,512]{2,1,0:T(8,128)(2,1)}), bf16[16,64,512]{2,1,0:T(8,128)(2,1)S(1)}, u32[]{:S(2)}, u32[]{:S(2)}) async-start(bf16[16,64,512]{2,1,0:T(8,128)(2,1)} %convert_element_type.53), calls=%async_computation.3 | async-start | bytes 2097152 | tf_op jit(solution)/shard_map/all_to_all | solution.py:234
  642.5 6.7 copy-start.29
  664.2 22.0 %all-to-all-start.2 = ((bf16[16,64,512]{2,1,0:T(8,128)(2,1)}), bf16[16,64,512]{2,1,0:T(8,128)(2,1)S(1)}, u32[]{:S(2)}, u32[]{:S(2)}) async-start(bf16[16,64,512]{2,1,0:T(8,128)(2,1)} %bitcast.36), calls=%async_computation.2 | async-start | bytes 2097152 | tf_op jit(solution)/shard_map/all_to_all | solution.py:233
  (31 other events, 65.3 us)
Sparse Core Ops, SparseCore 0:
  390.9 27.9 all-gather.12
  420.7 25.6 all-gather.10
  448.1 24.5 all-gather.14
  564.0 20.2 all-gather.16
where the time goes:
time: 704 us; the launch traced here: 694 us
  other arithmetic  335 us (48%)
  matrix products  179 us (25%)
  local copies, waits for them, and re-layouts  62.9 us (9%)
  waiting for transfers between devices  48.4 us (7%)
  starting transfers between devices  26.1 us (4%)
  blocking collectives  25.8 us (4%)
  between operations  15 us (2%)
    another operation x4, other arithmetic, solve_lower(): lax.linalg.triangular_solve(system, target, left_side=True, lower=True, u...  317 us
    dot_general x76, matrix products, exact_prod(): return jnp.einsum(form, left, right, precision=lax.Precision.HIGHEST)  155 us
    all_gather x2, waiting for transfers between devices, carried_in(): everything = jax.tree.map(lambda part: lax.all_gather(part, axis), value)  30.9 us
    psum x2, blocking collectives, by_axis(): return functools.reduce(lax.psum, axes, value)  20.9 us
    unnamed x121, local copies, waits for them, and re-layouts  20.6 us
    another operation x4, matrix products, solve_lower(): lax.linalg.triangular_solve(system, target, left_side=True, lower=True, u...  17.1 us
  transfers between devices with their start and end apart: 8, of which 4 were waited for; matrix products, arithmetic and copies ran while one was open for 27% of the time, Pallas kernels for 0%

commit v1 on v0

v1 whole, which is shorter than its diff:
```python
import functools

import jax
import jax.numpy as jnp
from jax import lax
from jax.experimental import pallas as pl
from jax.experimental.pallas import tpu as pltpu
from jax.sharding import Mesh
from jax.sharding import PartitionSpec as P

D = 8192
C = 128
PAIR = 2
HEAD = ("head_0", "head_1")
SEQ = ("seq_0", "seq_1")
SEQ_HEAD = ("seq_0", "seq_1", "head_0", "head_1")
EPS = 1e-06
SCALE = C ** (-0.5)

f32 = jnp.float32
bf16 = jnp.bfloat16


def halves(x):
    high = x.astype(bf16)
    return high, (x - high.astype(f32)).astype(bf16)


def nn(a, b):
    return lax.dot_general(a, b, (((1,), (0,)), ((), ())), preferred_element_type=f32)


def nt(a, b):
    return lax.dot_general(a, b, (((1,), (1,)), ((), ())), preferred_element_type=f32)


def mul3(form, a, b):
    return form(a[0], b[0]) + (form(a[0], b[1]) + form(a[1], b[0]))


def mul_left(form, a, b):
    return form(a[0], b) + form(a[1], b)


def mul_right(form, a, b):
    return form(a, b[0]) + form(a, b[1])


def iotas():
    return (
        lax.broadcasted_iota(jnp.int32, (C, C), 0),
        lax.broadcasted_iota(jnp.int32, (C, C), 1),
    )


def columns_of(rows):
    missing = C - rows.shape[0]
    return jnp.concatenate([rows, jnp.zeros((missing, C), f32)], axis=0).T


def tile(ref, b, h):
    return ref[b * C : (b + 1) * C, h * C : (h + 1) * C]


def prep_keys(heads, steps, key, value, decay, inv, weight, trans, shift, cols, rows, send, whole, offset):
    step = pl.program_id(0)
    units = [(b, h) for b in range(PAIR) for h in range(heads)]
    count = len(units)
    row, col = iotas()
    lane = lax.broadcasted_iota(jnp.int32, (C, C), 1)

    @pl.when(step == 0)
    def _():
        eye = jnp.where(row == col, 1.0, 0.0)
        for h in range(heads):
            whole[h] = eye
            offset[h] = jnp.zeros((C, C), f32)

    upto = jnp.where(row <= col, 1.0, 0.0)
    logs = jnp.concatenate([decay[:, b * C : (b + 1) * C] for b in range(PAIR)], axis=0)
    cumul_rows = jnp.dot(logs, upto, precision=lax.Precision.HIGHEST, preferred_element_type=f32)
    cumul_cols = columns_of(cumul_rows)

    raw = [tile(key, b, h) for b, h in units]
    scale_cols = []
    gathered = jnp.zeros((C, C), f32)
    for u in range(count):
        wide = raw[u].astype(f32)
        scale_cols.append(lax.rsqrt(jnp.sum(wide * wide, axis=1, keepdims=True) + EPS))
        gathered = jnp.where(lane == u, scale_cols[u], gathered)
    scale_rows = gathered.T

    rows[0, :count] = cumul_rows
    rows[0, count:] = scale_rows[:count]
    for b in range(PAIR):
        packed = jnp.zeros((C, C), f32)
        for h in range(heads):
            u = b * heads + h
            packed = jnp.where(lane == h, cumul_cols[:, u : u + 1], packed)
            packed = jnp.where(lane == heads + h, scale_cols[u], packed)
        cols[b * C : (b + 1) * C] = packed

    g_col = [cumul_cols[:, u : u + 1] for u in range(count)]
    g_row = [cumul_rows[u : u + 1] for u in range(count)]
    s_row = [scale_rows[u : u + 1] for u in range(count)]
    last = [g_row[u][:, C - 1 :] for u in range(count)]

    lower = []
    for u in range(count):
        gram = nt(raw[u], raw[u])
        decayed = jnp.exp(jnp.where(row > col, g_col[u] - g_row[u], 0.0))
        lower.append(
            jnp.where(row > col, 2.0 * decayed * (scale_cols[u] * s_row[u]) * gram, 0.0)
        )

    apart = row ^ col
    result = [
        jnp.where(row == col, 1.0, 0.0) - jnp.where(apart == 1, lower[u], 0.0) for u in range(count)
    ]
    size = 2
    while size < C:
        here = (apart >= size) & (apart < 2 * size)
        split = [halves(x) for x in result]
        below = [halves(jnp.where(here, lower[u], 0.0)) for u in range(count)]
        inner = [halves(mul3(nn, below[u], split[u])) for u in range(count)]
        result = [result[u] - mul3(nn, split[u], inner[u]) for u in range(count)]
        size *= 2

    for u in range(count):
        inv[u] = result[u]
    split = [halves(x) for x in result]
    scaled = []
    for u in range(count):
        end = jnp.exp(last[u] - g_row[u])
        turned = tile(value, *units[u]).T
        amount = mul_right(nt, turned, split[u]) * (2.0 * end * s_row[u])
        shift[u] = mul_left(nn, halves(amount), raw[u])
        start = jnp.exp(g_row[u]) * s_row[u]
        scaled.append(mul_left(nn, halves(result[u] * start), raw[u]))
        weight[u] = scaled[u]
    for u in range(count):
        end = jnp.exp(last[u] - g_col[u]) * (2.0 * scale_cols[u])
        drop = mul_right(nn, raw[u].T, halves(scaled[u] * end))
        trans[u] = jnp.where(row == col, jnp.exp(last[u]), 0.0) - drop

    for b in range(PAIR):
        for h in range(heads):
            u = b * heads + h
            step_map = halves(trans[u])
            whole[h] = mul3(nn, step_map, halves(whole[h]))
            offset[h] = mul3(nt, halves(offset[h]), step_map) + shift[u]

    @pl.when(step == steps - 1)
    def _():
        half = C // 2
        for h in range(heads):
            for part in range(2):
                send[2 * h + part, :C] = whole[h]
                send[2 * h + part, C:] = offset[h, part * half : (part + 1) * half]


def prep_queries(heads, query, key, grad, gain, sums, weight, trans, cols, rows, inner, adjoint, norm_cols, norm_rows, send, total):
    step = pl.program_id(0)
    units = [(b, h) for b in range(PAIR) for h in range(heads)]
    count = len(units)
    row, col = iotas()

    @pl.when(step == 0)
    def _():
        for h in range(heads):
            total[h] = jnp.zeros((C, C), f32)

    squares = jnp.sum(sums[...], axis=0, keepdims=True)
    norm = lax.rsqrt(squares * (1.0 / D) + EPS)
    per_block = jnp.concatenate([norm[:, b * C : (b + 1) * C] for b in range(PAIR)], axis=0)
    n_cols = columns_of(per_block)
    norm_rows[0] = jnp.concatenate([per_block, jnp.zeros((8 - PAIR, C), f32)], axis=0)
    for b in range(PAIR):
        norm_cols[b * C : (b + 1) * C] = jnp.broadcast_to(n_cols[:, b : b + 1], (C, C))

    scaled_query, mixing = [], []
    for u, (b, h) in enumerate(units):
        here = cols[b * C : (b + 1) * C]
        g_col = here[:, h : h + 1]
        g_row = rows[0, u : u + 1]
        s_row = rows[0, count + u : count + u + 1]
        n_col = n_cols[:, b : b + 1]
        wide = tile(query, b, h).astype(f32) * (gain[:, h * C : (h + 1) * C] * SCALE)
        decayed = jnp.exp(jnp.where(row >= col, g_col - g_row, 0.0))
        scores = mul_left(nt, halves(wide), tile(key, b, h))
        mixing.append(
            halves(jnp.where(row >= col, 2.0 * decayed * (n_col * s_row) * scores, 0.0))
        )
        scaled_query.append(halves(wide * (jnp.exp(g_col) * n_col)))
    turned = [tile(grad, b, h).T for b, h in units]
    for u in range(count):
        inner[u] = mul_right(nn, turned[u], mixing[u])
    for u in range(count):
        adjoint[u] = mul_right(nn, turned[u], scaled_query[u]) - mul3(
            nn, halves(inner[u]), halves(weight[u])
        )
    for b in reversed(range(PAIR)):
        for h in range(heads):
            u = b * heads + h
            total[h] = mul3(nn, halves(total[h]), halves(trans[u])) + adjoint[u]

    half = C // 2
    for h in range(heads):
        for part in range(2):
            send[2 * h + part] = total[h, part * half : (part + 1) * half]


def scan_states(received, out):
    count = received.shape[0]
    state = jnp.zeros(out.shape[1:], f32)
    for k in range(count):
        out[k] = state
        if k < count - 1:
            state = mul3(nt, halves(state), halves(received[k, :C])) + received[k, C:]


def scan_adjoints(maps, received, out):
    count = received.shape[0]
    state = jnp.zeros(out.shape[1:], f32)
    for k in reversed(range(count)):
        out[k] = state
        if k:
            state = mul3(nn, halves(state), halves(maps[k, :C])) + received[k]


def query_grads(heads, query, key, value, grad, gain, incoming, inv, weight, trans, shift, cols, rows, norm_cols, scaled, fresh, starts, part, state):
    step = pl.program_id(0)
    units = [(b, h) for b in range(PAIR) for h in range(heads)]
    count = len(units)
    row, col = iotas()
    lane = lax.broadcasted_iota(jnp.int32, (C, C), 1)

    @pl.when(step == 0)
    def _():
        state[...] = incoming[...]

    for b in range(PAIR):
        for h in range(heads):
            u = b * heads + h
            starts[u] = state[h]
            state[h] = mul3(nt, halves(state[h]), halves(trans[u])) + shift[u]
    begin = [halves(starts[u]) for u in range(count)]
    amounts = []
    for u, (b, h) in enumerate(units):
        amount = mul_left(nn, halves(inv[u]), tile(value, b, h)) - mul3(
            nt, halves(weight[u]), begin[u]
        )
        fresh[u] = amount
        amounts.append(halves(amount))
    cross = [mul_right(nt, tile(grad, b, h), amounts[u]) for u, (b, h) in enumerate(units)]
    sums = [jnp.zeros((C, 1), f32) for _ in range(PAIR)]
    for u, (b, h) in enumerate(units):
        here = cols[b * C : (b + 1) * C]
        g_col = here[:, h : h + 1]
        g_row = rows[0, u : u + 1]
        s_row = rows[0, count + u : count + u + 1]
        decayed = jnp.exp(jnp.where(row >= col, g_col - g_row, 0.0))
        mixed = jnp.where(row >= col, 2.0 * decayed * s_row * cross[u], 0.0)
        result = mul_left(nn, halves(mixed), tile(key, b, h)) + jnp.exp(g_col) * mul_right(
            nn, tile(grad, b, h), begin[u]
        )
        result = result * (gain[:, h * C : (h + 1) * C] * SCALE)
        scaled[b * C : (b + 1) * C, h * C : (h + 1) * C] = result
        sums[b] = sums[b] + jnp.sum(result * tile(query, b, h).astype(f32), axis=1, keepdims=True)
    for b in range(PAIR):
        full = sums[b] * norm_cols[b * C : (b + 1) * C]
        part[:, b * C : (b + 1) * C] = full.T[: part.shape[0]]


def finish_queries(query, scaled, norm_cols, sums, out):
    total = jnp.sum(sums[...], axis=0, keepdims=True) * (1.0 / D)
    blocks = total.shape[1] // C
    per_block = jnp.concatenate([total[:, b * C : (b + 1) * C] for b in range(blocks)], axis=0)
    corrections = columns_of(per_block)
    for b in range(blocks):
        part = slice(b * C, (b + 1) * C)
        norm = norm_cols[part][:, :1]
        normed = query[part].astype(f32) * norm
        out[part] = (norm * (scaled[part] - normed * corrections[:, b : b + 1])).astype(bf16)


def key_grads(heads, query, key, grad, gain, outgoing, inv, trans, adjoint, inner, fresh, starts, cols, rows, norm_rows, key_out, value_out, state):
    step = pl.program_id(0)
    units = [(b, h) for b in range(PAIR) for h in range(heads)]
    count = len(units)
    row, col = iotas()

    @pl.when(step == 0)
    def _():
        state[...] = outgoing[...]

    ends = [None] * count
    for b in reversed(range(PAIR)):
        for h in range(heads):
            u = b * heads + h
            ends[u] = halves(state[h])
            state[h] = mul3(nn, ends[u], halves(trans[u])) + adjoint[u]
    g_row = [rows[0, u : u + 1] for u in range(count)]
    s_row = [rows[0, count + u : count + u + 1] for u in range(count)]
    keys = [tile(key, b, h) for b, h in units]
    amounts = [halves(fresh[u]) for u in range(count)]
    turned = []
    for u in range(count):
        end = jnp.exp(g_row[u][:, C - 1 :] - g_row[u]) * (2.0 * s_row[u])
        turned.append(halves(inner[u] + mul_left(nt, ends[u], keys[u]) * end))
    results = [mul3(nn, turned[u], halves(inv[u])).T for u in range(count)]
    for u, (b, h) in enumerate(units):
        value_out[b * C : (b + 1) * C, h * C : (h + 1) * C] = results[u].astype(bf16)
    results = [halves(x) for x in results]
    against = [mul3(nt, results[u], amounts[u]) for u in range(count)]
    across = [mul_left(nt, amounts[u], tile(grad, b, h)) for u, (b, h) in enumerate(units)]
    for u, (b, h) in enumerate(units):
        here = cols[b * C : (b + 1) * C]
        g_col = here[:, h : h + 1]
        s_col = here[:, heads + h : heads + h + 1]
        n_row = norm_rows[0, b : b + 1]
        below = jnp.exp(jnp.where(row > col, g_col - g_row[u], 0.0))
        pulled = jnp.where(row > col, -2.0 * below * against[u], 0.0)
        both = (pulled + pulled.T) * s_row[u]
        above = jnp.exp(jnp.where(row <= col, g_row[u] - g_col, 0.0))
        mixed = jnp.where(row <= col, 2.0 * above * n_row * across[u], 0.0)
        total = mul_left(nn, halves(both), keys[u])
        total += mul_left(nn, halves(mixed), tile(query, b, h)) * (
            gain[:, h * C : (h + 1) * C] * SCALE
        )
        total -= jnp.exp(g_col) * mul3(nn, results[u], halves(starts[u]))
        end = 2.0 * jnp.exp(g_row[u][:, C - 1 :] - g_col)
        total += end * mul3(nn, amounts[u], ends[u])
        unit = keys[u].astype(f32) * s_col
        along = jnp.sum(unit * total, axis=1, keepdims=True)
        key_out[b * C : (b + 1) * C, h * C : (h + 1) * C] = (
            s_col * (total - unit * along)
        ).astype(bf16)


def from_everyone(value, axis):
    length = lax.axis_size(axis)
    return lax.all_to_all(
        jnp.broadcast_to(value[None], (length, *value.shape)), axis, 0, 0, tiled=True
    )


def per_device(query_raw, key_raw, value_raw, query_gain, log_decay, out_grad):
    rows, width = query_raw.shape
    heads = log_decay.shape[0]
    blocks = rows // C
    steps = blocks // PAIR
    count = PAIR * heads
    tokens = PAIR * C
    group = lax.axis_size(HEAD)
    chain = lax.axis_size(SEQ)
    gain = query_gain.reshape(1, width)
    shape = jax.ShapeDtypeStruct

    def forward(*block):
        return pl.BlockSpec(block, lambda i: (i,) + (0,) * (len(block) - 1))

    def backward(*block):
        return pl.BlockSpec(block, lambda i: (steps - 1 - i,) + (0,) * (len(block) - 1))

    def fixed(*block):
        return pl.BlockSpec(block, lambda i: (0,) * len(block))

    def lanes(order, *block):
        return pl.BlockSpec(block, lambda i: (0, order(i)))

    def ahead(i):
        return i

    def back(i):
        return steps - 1 - i

    matrices = shape((blocks * heads, C, C), f32)
    matrix = (count, C, C)
    carry = pltpu.VMEM((heads, C, C), f32)

    wide = query_raw.astype(f32)
    squares = from_everyone(jnp.sum(wide * wide, axis=1)[None], HEAD).reshape(group, rows)

    inv, weight, trans, shift, cols, row_info, send = pl.pallas_call(
        functools.partial(prep_keys, heads, steps),
        grid=(steps,),
        in_specs=[forward(tokens, width), forward(tokens, width), lanes(ahead, heads, tokens)],
        out_specs=[forward(*matrix)] * 4
        + [forward(tokens, C), forward(1, 2 * count, C), fixed(2 * heads, C + C // 2, C)],
        out_shape=[matrices] * 4
        + [
            shape((rows, C), f32),
            shape((steps, 2 * count, C), f32),
            shape((2 * heads, C + C // 2, C), f32),
        ],
        scratch_shapes=[carry, carry],
        name="prep_keys",
    )(key_raw, value_raw, log_decay)
    maps = lax.all_to_all(send, SEQ, 0, 0, tiled=True)

    inner, adjoint, norm_cols, norm_rows, send_back = pl.pallas_call(
        functools.partial(prep_queries, heads),
        grid=(steps,),
        in_specs=[
            backward(tokens, width),
            backward(tokens, width),
            backward(tokens, width),
            fixed(1, width),
            lanes(back, group, tokens),
            backward(*matrix),
            backward(*matrix),
            backward(tokens, C),
            backward(1, 2 * count, C),
        ],
        out_specs=[
            backward(*matrix),
            backward(*matrix),
            backward(tokens, C),
            backward(1, 8, C),
            fixed(2 * heads, C // 2, C),
        ],
        out_shape=[
            matrices,
            matrices,
            shape((rows, C), f32),
            shape((steps, 8, C), f32),
            shape((2 * heads, C // 2, C), f32),
        ],
        scratch_shapes=[carry],
        name="prep_queries",
    )(query_raw, key_raw, out_grad, gain, squares, weight, trans, cols, row_info)
    late = lax.all_to_all(send_back, SEQ, 0, 0, tiled=True)

    pieces = shape((chain, C // 2, C), f32)
    incoming = lax.all_to_all(
        pl.pallas_call(scan_states, out_shape=pieces, name="scan_states")(maps),
        SEQ,
        0,
        0,
        tiled=True,
    ).reshape(heads, C, C)
    outgoing = lax.all_to_all(
        pl.pallas_call(scan_adjoints, out_shape=pieces, name="scan_adjoints")(maps, late),
        SEQ,
        0,
        0,
        tiled=True,
    ).reshape(heads, C, C)

    scaled, fresh, starts, part = pl.pallas_call(
        functools.partial(query_grads, heads),
        grid=(steps,),
        in_specs=[forward(tokens, width)] * 4
        + [fixed(1, width), fixed(heads, C, C)]
        + [forward(*matrix)] * 4
        + [forward(tokens, C), forward(1, 2 * count, C), forward(tokens, C)],
        out_specs=[
            forward(tokens, width),
            forward(*matrix),
            forward(*matrix),
            lanes(ahead, 8, tokens),
        ],
        out_shape=[shape((rows, width), f32), matrices, matrices, shape((8, rows), f32)],
        scratch_shapes=[carry],
        name="query_grads",
    )(
        query_raw, key_raw, value_raw, out_grad, gain, incoming,
        inv, weight, trans, shift, cols, row_info, norm_cols,
    )
    corrections = from_everyone(part[:1], HEAD).reshape(group, rows)

    key_raw_grad, value_raw_grad = pl.pallas_call(
        functools.partial(key_grads, heads),
        grid=(steps,),
        in_specs=[backward(tokens, width)] * 3
        + [fixed(1, width), fixed(heads, C, C)]
        + [backward(*matrix)] * 6
        + [backward(tokens, C), backward(1, 2 * count, C), backward(1, 8, C)],
        out_specs=[backward(tokens, width)] * 2,
        out_shape=[shape((rows, width), bf16)] * 2,
        scratch_shapes=[carry],
        name="key_grads",
    )(
        query_raw, key_raw, out_grad, gain, outgoing,
        inv, trans, adjoint, inner, fresh, starts, cols, row_info, norm_rows,
    )

    query_raw_grad = pl.pallas_call(
        finish_queries,
        grid=(steps,),
        in_specs=[
            forward(tokens, width),
            forward(tokens, width),
            forward(tokens, C),
            lanes(ahead, group, tokens),
        ],
        out_specs=forward(tokens, width),
        out_shape=shape((rows, width), bf16),
        name="finish_queries",
    )(query_raw, scaled, norm_cols, corrections)

    def owned(array):
        return lax.all_to_all(array, HEAD, split_axis=0, concat_axis=1, tiled=True)

    return owned(query_raw_grad), owned(key_raw_grad), owned(value_raw_grad)


def solution(mesh):
    split = Mesh(mesh.devices.reshape(4, 2, 4, 4), ("seq_0", "seq_1", "head_0", "head_1"))
    return jax.shard_map(
        per_device,
        mesh=split,
        in_specs=(P(SEQ, HEAD), P(SEQ, HEAD), P(SEQ, HEAD), P(HEAD), P(HEAD, SEQ), P(SEQ, HEAD)),
        out_specs=(P(SEQ_HEAD, None), P(SEQ_HEAD, None), P(SEQ_HEAD, None)),
        check_vma=False,
    )
```

time: 704 us -> 180 us (0.26); the launches traced: 694 us -> 179 us
  other arithmetic: 335 us -> 1.5 us
  matrix products: 179 us -> 0 us
  Pallas kernels: 0 us -> 71.1 us
  local copies, waits for them, and re-layouts: 62.9 us -> 6.68 us
  between operations: 15 us -> 0.77 us
  starting transfers between devices: 26.1 us -> 37.4 us
  waiting for transfers between devices: 48.4 us -> 37.3 us
    another operation x5 -> x0, other arithmetic: 318 us -> none  [the longest x4 317 us: solve_lower(): lax.linalg.triangular_solve(system, target, left_side=True, lower=True, u...]
    dot_general x77 -> x0, matrix products: 162 us -> none  [the longest x76 155 us: exact_prod(): return jnp.einsum(form, left, right, precision=lax.Precision.HIGHEST)]
    pallas_call x0 -> x7, Pallas kernels: none -> 71.1 us  [the longest x1 23.4 us: per_device(): pl.pallas_call(functools.partial(prep_keys, heads, steps), grid=(steps,),...]
    all_gather x4 -> x0, waiting for transfers between devices: 36.4 us -> none  [the longest x2 30.9 us: carried_in(): everything = jax.tree.map(lambda part: lax.all_gather(part, axis), value)]
    all_to_all x3 -> x6, waiting for transfers between devices: 11.3 us -> 37.3 us  [the longest x2 24.5 us: owned(): return lax.all_to_all(array, HEAD, split_axis=0, concat_axis=1, tiled=True)]
    all_to_all x0 -> x1, blocking collectives: none -> 24 us  [owned(): return lax.all_to_all(array, HEAD, split_axis=0, concat_axis=1, tiled=True)]
    psum x2 -> x0, blocking collectives: 20.9 us -> none  [by_axis(): return functools.reduce(lax.psum, axes, value)]
    unnamed x121 -> x10, local copies, waits for them, and re-layouts: 20.6 us -> 1.3 us
  transfers between devices with their start and end apart: 8 -> 8, of which waited for: 4 -> 5; matrix products, arithmetic and copies ran while one was open for 27% -> 2% of each run, Pallas kernels for 0% -> 40%
where the time goes in v1:
time: 180 us; the launch traced here: 179 us
  Pallas kernels  71.1 us (39%)
  starting transfers between devices  37.4 us (21%)
  waiting for transfers between devices  37.3 us (21%)
  blocking collectives  24 us (13%)
  local copies, waits for them, and re-layouts  6.68 us (4%)
    all_to_all x2, waiting for transfers between devices, owned(): return lax.all_to_all(array, HEAD, split_axis=0, concat_axis=1, tiled=True)  24.5 us
    all_to_all x1, blocking collectives, owned(): return lax.all_to_all(array, HEAD, split_axis=0, concat_axis=1, tiled=True)  24 us
    pallas_call x1, Pallas kernels, per_device(): pl.pallas_call(functools.partial(prep_keys, heads, steps), grid=(steps,),...  23.4 us
    pallas_call x1, Pallas kernels, per_device(): pl.pallas_call(functools.partial(key_grads, heads), grid=(steps,), in_spe...  16.4 us
    all_to_all x2, starting transfers between devices, from_everyone(): lax.all_to_all(jnp.broadcast_to(value[None], (length, *value.shape)), axi...  14.4 us
    pallas_call x1, Pallas kernels, per_device(): pl.pallas_call(functools.partial(query_grads, heads), grid=(steps,), in_s...  12.4 us
    pallas_call x1, Pallas kernels, per_device(): pl.pallas_call(functools.partial(prep_queries, heads), grid=(steps,), in_...  8.4 us
    all_to_all x2, starting transfers between devices, owned(): return lax.all_to_all(array, HEAD, split_axis=0, concat_axis=1, tiled=True)  7.5 us
  transfers between devices with their start and end apart: 8, of which 5 were waited for; matrix products, arithmetic and copies ran while one was open for 2% of the time, Pallas kernels for 40%

profile of v1, /device:TPU:0, one launch (start us, length us, event | category | flops | bytes accessed | tf_op | source)
XLA Modules:
  0.0 178.8 jit_solution(1654207077691893370)
XLA Ops:
  0.6 1.5 multiply_reduce_fusion
  2.1 0.7 broadcast_in_dim.6
  2.8 7.1 %all-to-all-start.2 = ((f32[16,1,1024]{2,1,0:T(1,128)}), f32[16,1,1024]{2,1,0:T(1,128)S(1)}, u32[]{:S(2)}, u32[]{:S(2)}) async-start(f32[16,1,1024]{2,1,0:T(1,128)} %broadcast_in_dim.6), calls=%async_computation.2 | async-start | bytes 131072 | tf_op jit(solution)/shard_map/all_to_all | solution.py:343
  10.0 23.4 %prep_keys.1 = (f32[32,128,128]{2,1,0:T(8,128)}, f32[32,128,128]{2,1,0:T(8,128)}, f32[32,128,128]{2,1,0:T(8,128)}, f32[32,128,128]{2,1,0:T(8,128)}, f32[1024,128...) custom-call(bf16[1024,512]{1,0:T(8,128)(2,1)} %key.7, bf16[1024,512]{1,0:T(8,128)(2,1)} %value.3, ...), custom_call_target="tpu_custom_call" | custom-call | tf_op jit(solution)/shard_map/prep_keys/pallas_call | solution.py:385
  33.4 0.0 all-to-all-done.2
  33.4 5.3 %all-to-all-start = ((f32[8,192,128]{2,1,0:T(8,128)}), f32[8,192,128]{2,1,0:T(8,128)S(1)}, u32[]{:S(2)}, u32[]{:S(2)}) async-start(f32[8,192,128]{2,1,0:T(8,128)} %get-tuple-element.21), calls=%async_computation | async-start | bytes 1572864 | tf_op jit(solution)/shard_map/all_to_all | solution.py:400
  38.7 0.6 copy.23
  39.4 8.4 %prep_queries.1 = (f32[32,128,128]{2,1,0:T(8,128)}, f32[32,128,128]{2,1,0:T(8,128)}, f32[1024,128]{1,0:T(8,128)}, f32[4,8,128]{2,1,0:T(8,128)}, f32[8,64,128]{2,1,0:T(8,128)}) custom-call(bf16[1024,512]{1,0:T(8,128)(2,1)} %query.7, bf16[1024,512]{1,0:T(8,128)(2,1)} %key.7, bf16[1024,512]{1,0:T(8,128)(2,1)} %grad.5, f32[1,512]{1,0:T(1,128)} %bitcast.34, ...), custom_call_target="tpu_custom_call" | custom-call | tf_op jit(solution)/shard_map/prep_queries/pallas_call | solution.py:402
  47.8 4.1 %all-to-all-done.received.maps = f32[8,192,128]{2,1,0:T(8,128)S(1)} async-done(((f32[8,192,128]{2,1,0:T(8,128)}), f32[8,192,128]{2,1,0:T(8,128)S(1)}, u32[]{:S(2)}, u32[]{:S(2)}) %all-to-all-start) | async-done | bytes 786464 | tf_op jit(solution)/shard_map/all_to_all | solution.py:400
  51.8 3.4 %all-to-all-start.5 = ((f32[8,64,128]{2,1,0:T(8,128)}), f32[8,64,128]{2,1,0:T(8,128)S(1)}, u32[]{:S(2)}, u32[]{:S(2)}) async-start(f32[8,64,128]{2,1,0:T(8,128)} %get-tuple-element.31), calls=%async_computation.5 | async-start | bytes 524288 | tf_op jit(solution)/shard_map/all_to_all | solution.py:433
  55.3 3.2 %scan_states.1 = f32[8,64,128]{2,1,0:T(8,128)} custom-call(f32[8,192,128]{2,1,0:T(8,128)} %copy-done), custom_call_target="tpu_custom_call" | custom-call | tf_op jit(solution)/shard_map/scan_states/pallas_call | solution.py:437
  58.4 4.3 %all-to-all-done.5.received = f32[8,64,128]{2,1,0:T(8,128)S(1)} async-done(((f32[8,64,128]{2,1,0:T(8,128)}), f32[8,64,128]{2,1,0:T(8,128)S(1)}, u32[]{:S(2)}, u32[]{:S(2)}) %all-to-all-start.5) | async-done | bytes 262176 | tf_op jit(solution)/shard_map/all_to_all | solution.py:433
  62.7 3.4 %all-to-all-start.1 = ((f32[8,64,128]{2,1,0:T(8,128)}), f32[8,64,128]{2,1,0:T(8,128)S(1)}, u32[]{:S(2)}, u32[]{:S(2)}) async-start(f32[8,64,128]{2,1,0:T(8,128)} %scan_states.1), calls=%async_computation.1 | async-start | bytes 524288 | tf_op jit(solution)/shard_map/all_to_all | solution.py:436
  66.1 3.0 %scan_adjoints.1 = f32[8,64,128]{2,1,0:T(8,128)} custom-call(f32[8,192,128]{2,1,0:T(8,128)} %copy-done, f32[8,64,128]{2,1,0:T(8,128)} %copy-done.3), custom_call_target="tpu_custom_call" | custom-call | tf_op jit(solution)/shard_map/scan_adjoints/pallas_call | solution.py:444
  69.1 4.4 %all-to-all-done.1 = f32[8,64,128]{2,1,0:T(8,128)S(1)} async-done(((f32[8,64,128]{2,1,0:T(8,128)}), f32[8,64,128]{2,1,0:T(8,128)S(1)}, u32[]{:S(2)}, u32[]{:S(2)}) %all-to-all-start.1) | async-done | bytes 262176 | tf_op jit(solution)/shard_map/all_to_all | solution.py:436
  73.5 3.4 %all-to-all-start.6 = ((f32[8,64,128]{2,1,0:T(8,128)}), f32[8,64,128]{2,1,0:T(8,128)S(1)}, u32[]{:S(2)}, u32[]{:S(2)}) async-start(f32[8,64,128]{2,1,0:T(8,128)} %scan_adjoints.1), calls=%async_computation.6 | async-start | bytes 524288 | tf_op jit(solution)/shard_map/all_to_all | solution.py:443
  77.0 12.4 %query_grads.1 = (f32[1024,512]{1,0:T(8,128)}, f32[32,128,128]{2,1,0:T(8,128)}, f32[32,128,128]{2,1,0:T(8,128)}, f32[8,1024]{1,0:T(8,128)}) custom-call(bf16[1024,512]{1,0:T(8,128)(2,1)} %query.7, bf16[1024,512]{1,0:T(8,128)(2,1)} %key.7, bf16[1024,512]{1,0:T(8,128)(2,1)} %value.3, bf16[1024,512]{1,0:T(8,128)(2,1)} %grad.5, f32[1,512]{1,0:T(1,128)} %bitcast.35, ...), custom_call_target="tpu_custom_call" | custom-call | tf_op jit(solution)/shard_map/query_grads/pallas_call | solution.py:451
  89.4 0.8 slice.3
  90.2 0.0 all-to-all-done.6
  90.2 0.7 broadcast_in_dim.15
  90.9 7.2 %all-to-all-start.3 = ((f32[16,1,1024]{2,1,0:T(1,128)}), f32[16,1,1024]{2,1,0:T(1,128)S(1)}, u32[]{:S(2)}, u32[]{:S(2)}) async-start(f32[16,1,1024]{2,1,0:T(1,128)} %broadcast_in_dim.15), calls=%async_computation.3 | async-start | bytes 131072 | tf_op jit(solution)/shard_map/all_to_all | solution.py:343
  98.1 16.4 %key_grads.1 = (bf16[1024,512]{1,0:T(8,128)(2,1)}, bf16[1024,512]{1,0:T(8,128)(2,1)}) custom-call(bf16[1024,512]{1,0:T(8,128)(2,1)} %query.7, bf16[1024,512]{1,0:T(8,128)(2,1)} %key.7, bf16[1024,512]{1,0:T(8,128)(2,1)} %grad.5, f32[1,512]{1,0:T(1,128)} %bitcast.36, f32[4,128,128]{2,1,0:T(8,128)} %bitcast.26, f32[32,128,128]{2,1,0:T(8,128)} %get-tuple-element.22.inv, ...), custom_call_target="tpu_custom_call" | custom-call | tf_op jit(solution)/shard_map/key_grads/pallas_call | solution.py:473
  114.6 24.0 %all_to_all.87 = bf16[16,64,512]{2,1,0:T(8,128)(2,1)S(1)} all-to-all(bf16[16,64,512]{2,1,0:T(8,128)(2,1)} %bitcast.28), channel_id=1, replica_groups=mesh['seq_0'=4,'seq_1'=2,'head_0'=4,'head_1'=4] {'head_0','head_1'}, dimensions={0} | all-to-all | bytes 2097152 | tf_op jit(solution)/shard_map/all_to_all | solution.py:504
  138.6 3.8 %all-to-all-start.7 = ((bf16[16,64,512]{2,1,0:T(8,128)(2,1)}), bf16[16,64,512]{2,1,0:T(8,128)(2,1)S(1)}, u32[]{:S(2)}, u32[]{:S(2)}) async-start(bf16[16,64,512]{2,1,0:T(8,128)(2,1)} %bitcast.6), calls=%async_computation.7 | async-start | bytes 2097152 | tf_op jit(solution)/shard_map/all_to_all | solution.py:504
  142.5 0.6 copy.22
  143.1 4.3 %finish_queries.1 = bf16[1024,512]{1,0:T(8,128)(2,1)} custom-call(bf16[1024,512]{1,0:T(8,128)(2,1)} %query.7, f32[1024,512]{1,0:T(8,128)} %get-tuple-element.29.scaled, f32[1024,128]{1,0:T(8,128)} %get-tuple-element.28.norm_cols, f32[16,1024]{1,0:T(8,128)} %bitcast.33), custom_call_target="tpu_custom_call" | custom-call | tf_op jit(solution)/shard_map/finish_queries/pallas_call | solution.py:489
  147.4 11.1 %all-to-all-done.7 = bf16[16,64,512]{2,1,0:T(8,128)(2,1)S(1)} async-done(((bf16[16,64,512]{2,1,0:T(8,128)(2,1)}), bf16[16,64,512]{2,1,0:T(8,128)(2,1)S(1)}, u32[]{:S(2)}, u32[]{:S(2)}) %all-to-all-start.7) | async-done | bytes 1048608 | tf_op jit(solution)/shard_map/all_to_all | solution.py:504
  158.5 3.7 %all-to-all-start.4 = ((bf16[16,64,512]{2,1,0:T(8,128)(2,1)}), bf16[16,64,512]{2,1,0:T(8,128)(2,1)S(1)}, u32[]{:S(2)}, u32[]{:S(2)}) async-start(bf16[16,64,512]{2,1,0:T(8,128)(2,1)} %bitcast.25), calls=%async_computation.4 | async-start | bytes 2097152 | tf_op jit(solution)/shard_map/all_to_all | solution.py:504
  162.1 1.1 copy.19
  163.2 1.1 copy.18
  164.3 13.5 %all-to-all-done.4 = bf16[16,64,512]{2,1,0:T(8,128)(2,1)S(1)} async-done(((bf16[16,64,512]{2,1,0:T(8,128)(2,1)}), bf16[16,64,512]{2,1,0:T(8,128)(2,1)S(1)}, u32[]{:S(2)}, u32[]{:S(2)}) %all-to-all-start.4) | async-done | bytes 1048608 | tf_op jit(solution)/shard_map/all_to_all | solution.py:504
  177.7 1.1 copy.17
  (9 shorter events, 0.0 us)
Async XLA Ops:
  2.8 30.6 %all-to-all-start.2 = ((f32[16,1,1024]{2,1,0:T(1,128)}), f32[16,1,1024]{2,1,0:T(1,128)S(1)}, u32[]{:S(2)}, u32[]{:S(2)}) async-start(f32[16,1,1024]{2,1,0:T(1,128)} %broadcast_in_dim.6), calls=%async_computation.2 | async-start | bytes 131072 | tf_op jit(solution)/shard_map/all_to_all | solution.py:343
  33.4 18.4 %all-to-all-start = ((f32[8,192,128]{2,1,0:T(8,128)}), f32[8,192,128]{2,1,0:T(8,128)S(1)}, u32[]{:S(2)}, u32[]{:S(2)}) async-start(f32[8,192,128]{2,1,0:T(8,128)} %get-tuple-element.21), calls=%async_computation | async-start | bytes 1572864 | tf_op jit(solution)/shard_map/all_to_all | solution.py:400
  51.8 3.4 %copy-start = (f32[8,192,128]{2,1,0:T(8,128)}, f32[8,192,128]{2,1,0:T(8,128)S(1)}, u32[]{:S(2)}) copy-start(f32[8,192,128]{2,1,0:T(8,128)S(1)} %all-to-all-done.received.maps) | copy-start | bytes 2359300
  51.8 10.8 %all-to-all-start.5 = ((f32[8,64,128]{2,1,0:T(8,128)}), f32[8,64,128]{2,1,0:T(8,128)S(1)}, u32[]{:S(2)}, u32[]{:S(2)}) async-start(f32[8,64,128]{2,1,0:T(8,128)} %get-tuple-element.31), calls=%async_computation.5 | async-start | bytes 524288 | tf_op jit(solution)/shard_map/all_to_all | solution.py:433
  62.7 3.4 %copy-start.3 = (f32[8,64,128]{2,1,0:T(8,128)}, f32[8,64,128]{2,1,0:T(8,128)S(1)}, u32[]{:S(2)}) copy-start(f32[8,64,128]{2,1,0:T(8,128)S(1)} %all-to-all-done.5.received) | copy-start | bytes 786436
  62.7 10.9 %all-to-all-start.1 = ((f32[8,64,128]{2,1,0:T(8,128)}), f32[8,64,128]{2,1,0:T(8,128)S(1)}, u32[]{:S(2)}, u32[]{:S(2)}) async-start(f32[8,64,128]{2,1,0:T(8,128)} %scan_states.1), calls=%async_computation.1 | async-start | bytes 524288 | tf_op jit(solution)/shard_map/all_to_all | solution.py:436
  73.5 3.4 %copy-start.2 = (f32[8,64,128]{2,1,0:T(8,128)}, f32[8,64,128]{2,1,0:T(8,128)S(1)}, u32[]{:S(2)}) copy-start(f32[8,64,128]{2,1,0:T(8,128)S(1)} %all-to-all-done.1) | copy-start | bytes 786436
  73.5 16.6 %all-to-all-start.6 = ((f32[8,64,128]{2,1,0:T(8,128)}), f32[8,64,128]{2,1,0:T(8,128)S(1)}, u32[]{:S(2)}, u32[]{:S(2)}) async-start(f32[8,64,128]{2,1,0:T(8,128)} %scan_adjoints.1), calls=%async_computation.6 | async-start | bytes 524288 | tf_op jit(solution)/shard_map/all_to_all | solution.py:443
  90.2 8.0 %copy-start.1 = (f32[8,64,128]{2,1,0:T(8,128)}, f32[8,64,128]{2,1,0:T(8,128)S(1)}, u32[]{:S(2)}) copy-start(f32[8,64,128]{2,1,0:T(8,128)S(1)} %all-to-all-done.6) | copy-start | bytes 786436
  90.9 23.7 %all-to-all-start.3 = ((f32[16,1,1024]{2,1,0:T(1,128)}), f32[16,1,1024]{2,1,0:T(1,128)S(1)}, u32[]{:S(2)}, u32[]{:S(2)}) async-start(f32[16,1,1024]{2,1,0:T(1,128)} %broadcast_in_dim.15), calls=%async_computation.3 | async-start | bytes 131072 | tf_op jit(solution)/shard_map/all_to_all | solution.py:343
  138.6 19.8 %all-to-all-start.7 = ((bf16[16,64,512]{2,1,0:T(8,128)(2,1)}), bf16[16,64,512]{2,1,0:T(8,128)(2,1)S(1)}, u32[]{:S(2)}, u32[]{:S(2)}) async-start(bf16[16,64,512]{2,1,0:T(8,128)(2,1)} %bitcast.6), calls=%async_computation.7 | async-start | bytes 2097152 | tf_op jit(solution)/shard_map/all_to_all | solution.py:504
  158.5 19.3 %all-to-all-start.4 = ((bf16[16,64,512]{2,1,0:T(8,128)(2,1)}), bf16[16,64,512]{2,1,0:T(8,128)(2,1)S(1)}, u32[]{:S(2)}, u32[]{:S(2)}) async-start(bf16[16,64,512]{2,1,0:T(8,128)(2,1)} %bitcast.25), calls=%async_computation.4 | async-start | bytes 2097152 | tf_op jit(solution)/shard_map/all_to_all | solution.py:504

commit v2 on v1

v2 whole, which is shorter than its diff:
```python
import functools

import jax
import jax.numpy as jnp
from jax import lax
from jax.experimental import pallas as pl
from jax.experimental.pallas import tpu as pltpu
from jax.sharding import Mesh
from jax.sharding import PartitionSpec as P

D = 8192
C = 128
PAIRS = (2, 2, 2, 2, 2)
HEAD = ("head_0", "head_1")
SEQ = ("seq_0", "seq_1")
SEQ_HEAD = ("seq_0", "seq_1", "head_0", "head_1")
EPS = 1e-06
SCALE = C ** (-0.5)

f32 = jnp.float32
bf16 = jnp.bfloat16


def halves(x):
    high = x.astype(bf16)
    return high, (x - high.astype(f32)).astype(bf16)


def nn(a, b):
    return lax.dot_general(a, b, (((1,), (0,)), ((), ())), preferred_element_type=f32)


def nt(a, b):
    return lax.dot_general(a, b, (((1,), (1,)), ((), ())), preferred_element_type=f32)


def mul3(form, a, b):
    return form(a[0], b[0]) + (form(a[0], b[1]) + form(a[1], b[0]))


def mul_left(form, a, b):
    return form(a[0], b) + form(a[1], b)


def mul_right(form, a, b):
    return form(a, b[0]) + form(a, b[1])


def iotas():
    return (
        lax.broadcasted_iota(jnp.int32, (C, C), 0),
        lax.broadcasted_iota(jnp.int32, (C, C), 1),
    )


def columns_of(rows):
    missing = C - rows.shape[0]
    return jnp.concatenate([rows, jnp.zeros((missing, C), f32)], axis=0).T


def tile(ref, b, h):
    return ref[b * C : (b + 1) * C, h * C : (h + 1) * C]


def square_sums(query, out):
    blocks = query.shape[0] // C
    ones = jnp.full((out.shape[0], query.shape[1]), 1.0, bf16)
    wide = query[...].astype(f32)
    sums = mul_right(nt, ones, halves(wide * wide))
    for b in range(blocks):
        out[:, b] = sums[:, b * C : (b + 1) * C]


def all_units(pair, heads):
    return [(b, h) for b in range(pair) for h in range(heads)]


def prep_keys(pair, heads, steps, key, value, decay, inv, weight, trans, shift, cols, rows, send, whole, offset):
    step = pl.program_id(0)
    units = all_units(pair, heads)
    count = len(units)
    row, col = iotas()

    @pl.when(step == 0)
    def _():
        eye = jnp.where(row == col, 1.0, 0.0)
        for h in range(heads):
            whole[h] = eye
            offset[h] = jnp.zeros((C, C), f32)

    upto = jnp.where(row <= col, 1.0, 0.0)
    logs = jnp.concatenate([decay[:, b * C : (b + 1) * C] for b in range(pair)], axis=0)
    cumul_rows = jnp.dot(logs, upto, precision=lax.Precision.HIGHEST, preferred_element_type=f32)
    cumul_cols = columns_of(cumul_rows)

    raw = [tile(key, b, h) for b, h in units]
    scale_cols = []
    gathered = jnp.zeros((C, C), f32)
    for u in range(count):
        wide = raw[u].astype(f32)
        scale_cols.append(lax.rsqrt(jnp.sum(wide * wide, axis=1, keepdims=True) + EPS))
        gathered = jnp.where(col == u, scale_cols[u], gathered)
    scale_rows = gathered.T

    for b in range(pair):
        mine = slice(b * heads, (b + 1) * heads)
        rows[b] = jnp.concatenate([cumul_rows[mine], scale_rows[mine]], axis=0)
        packed = jnp.zeros((C, C), f32)
        for h in range(heads):
            u = b * heads + h
            packed = jnp.where(col == h, cumul_cols[:, u : u + 1], packed)
            packed = jnp.where(col == heads + h, scale_cols[u], packed)
        cols[b * C : (b + 1) * C] = packed

    g_col = [cumul_cols[:, u : u + 1] for u in range(count)]
    g_row = [cumul_rows[u : u + 1] for u in range(count)]
    s_row = [scale_rows[u : u + 1] for u in range(count)]
    last = [g_row[u][:, C - 1 :] for u in range(count)]

    lower = []
    for u in range(count):
        gram = nt(raw[u], raw[u])
        decayed = jnp.exp(jnp.where(row > col, g_col[u] - g_row[u], 0.0))
        lower.append(
            jnp.where(row > col, 2.0 * decayed * (scale_cols[u] * s_row[u]) * gram, 0.0)
        )

    apart = row ^ col
    result = [
        jnp.where(row == col, 1.0, 0.0) - jnp.where(apart == 1, lower[u], 0.0) for u in range(count)
    ]
    size = 2
    while size < C:
        here = (apart >= size) & (apart < 2 * size)
        split = [halves(x) for x in result]
        below = [halves(jnp.where(here, lower[u], 0.0)) for u in range(count)]
        inner = [halves(mul3(nn, below[u], split[u])) for u in range(count)]
        result = [result[u] - mul3(nn, split[u], inner[u]) for u in range(count)]
        size *= 2

    split = [halves(x) for x in result]
    scaled, moved = [], []
    for u, (b, h) in enumerate(units):
        inv[b, h] = result[u]
        end = jnp.exp(last[u] - g_row[u])
        turned = tile(value, b, h).T
        amount = mul_right(nt, turned, split[u]) * (2.0 * end * s_row[u])
        moved.append(mul_left(nn, halves(amount), raw[u]))
        shift[b, h] = moved[u]
        start = jnp.exp(g_row[u]) * s_row[u]
        scaled.append(mul_left(nn, halves(result[u] * start), raw[u]))
        weight[b, h] = scaled[u]
    maps = []
    for u, (b, h) in enumerate(units):
        end = jnp.exp(last[u] - g_col[u]) * (2.0 * scale_cols[u])
        drop = mul_right(nn, raw[u].T, halves(scaled[u] * end))
        maps.append(jnp.where(row == col, jnp.exp(last[u]), 0.0) - drop)
        trans[b, h] = maps[u]

    for b in range(pair):
        for h in range(heads):
            u = b * heads + h
            step_map = halves(maps[u])
            whole[h] = mul3(nn, step_map, halves(whole[h]))
            offset[h] = mul3(nt, halves(offset[h]), step_map) + moved[u]

    @pl.when(step == steps - 1)
    def _():
        half = C // 2
        for h in range(heads):
            for part in range(2):
                send[2 * h + part, :C] = whole[h]
                send[2 * h + part, C:] = offset[h, part * half : (part + 1) * half]


def prep_queries(pair, heads, steps, query, key, grad, gain, sums, weight, trans, cols, rows, inner, adjoint, norm_cols, norm_rows, send, total, norms):
    step = pl.program_id(0)
    units = all_units(pair, heads)
    count = len(units)
    row, col = iotas()

    @pl.when(step == 0)
    def _():
        for h in range(heads):
            total[h] = jnp.zeros((C, C), f32)
        norms[...] = lax.rsqrt(jnp.sum(sums[...], axis=0) * (1.0 / D) + EPS)

    first = (steps - 1 - step) * pair
    n_rows = [norms[pl.ds(first + b, 1)] for b in range(pair)]
    n_cols = columns_of(jnp.concatenate(n_rows, axis=0))
    for b in range(pair):
        norm_rows[b] = jnp.broadcast_to(n_rows[b], (8, C))
        norm_cols[b * C : (b + 1) * C] = jnp.broadcast_to(n_cols[:, b : b + 1], (C, C))

    scaled_query, mixing = [], []
    for u, (b, h) in enumerate(units):
        here = cols[b * C : (b + 1) * C]
        g_col = here[:, h : h + 1]
        g_row = rows[b, h : h + 1]
        s_row = rows[b, heads + h : heads + h + 1]
        n_col = n_cols[:, b : b + 1]
        wide = tile(query, b, h).astype(f32) * (gain[:, h * C : (h + 1) * C] * SCALE)
        decayed = jnp.exp(jnp.where(row >= col, g_col - g_row, 0.0))
        scores = mul_left(nt, halves(wide), tile(key, b, h))
        mixing.append(
            halves(jnp.where(row >= col, 2.0 * decayed * (n_col * s_row) * scores, 0.0))
        )
        scaled_query.append(halves(wide * (jnp.exp(g_col) * n_col)))
    turned = [tile(grad, b, h).T for b, h in units]
    mixed = [mul_right(nn, turned[u], mixing[u]) for u in range(count)]
    terms = []
    for u, (b, h) in enumerate(units):
        inner[b, h] = mixed[u]
        terms.append(
            mul_right(nn, turned[u], scaled_query[u])
            - mul3(nn, halves(mixed[u]), halves(weight[b, h]))
        )
        adjoint[b, h] = terms[u]
    for b in reversed(range(pair)):
        for h in range(heads):
            u = b * heads + h
            total[h] = mul3(nn, halves(total[h]), halves(trans[b, h])) + terms[u]

    half = C // 2
    for h in range(heads):
        for part in range(2):
            send[2 * h + part] = total[h, part * half : (part + 1) * half]


def scan_states(received, late, out):
    count = received.shape[0]
    half = C // 2
    state = jnp.zeros((half, C), f32)
    for k in range(count):
        out[k, :half] = state
        out[k, half:] = late[k]
        if k < count - 1:
            state = mul3(nt, halves(state), halves(received[k, :C])) + received[k, C:]


def scan_adjoints(maps, received, out):
    count = received.shape[0]
    half = C // 2
    state = jnp.zeros((half, C), f32)
    for k in reversed(range(count)):
        out[k] = state
        if k:
            state = mul3(nn, halves(state), halves(maps[k, :C])) + received[k, half:]


def query_grads(pair, heads, steps, query, key, value, grad, gain, incoming, inv, weight, trans, shift, cols, rows, norm_cols, scaled, fresh, starts, part, state, sums_so_far):
    step = pl.program_id(0)
    units = all_units(pair, heads)
    row, col = iotas()
    half = C // 2

    @pl.when(step == 0)
    def _():
        for h in range(heads):
            for side in range(2):
                state[h, side * half : (side + 1) * half] = incoming[2 * h + side, :half]

    for b in range(pair):
        for h in range(heads):
            starts[b, h] = state[h]
            state[h] = mul3(nt, halves(state[h]), halves(trans[b, h])) + shift[b, h]
    begin = [halves(starts[b, h]) for b, h in units]
    amounts = []
    for u, (b, h) in enumerate(units):
        amount = mul_left(nn, halves(inv[b, h]), tile(value, b, h)) - mul3(
            nt, halves(weight[b, h]), begin[u]
        )
        fresh[b, h] = amount
        amounts.append(halves(amount))
    cross = [mul_right(nt, tile(grad, b, h), amounts[u]) for u, (b, h) in enumerate(units)]
    sums = [jnp.zeros((C, 1), f32) for _ in range(pair)]
    for u, (b, h) in enumerate(units):
        here = cols[b * C : (b + 1) * C]
        g_col = here[:, h : h + 1]
        g_row = rows[b, h : h + 1]
        s_row = rows[b, heads + h : heads + h + 1]
        decayed = jnp.exp(jnp.where(row >= col, g_col - g_row, 0.0))
        mixed = jnp.where(row >= col, 2.0 * decayed * s_row * cross[u], 0.0)
        result = mul_left(nn, halves(mixed), tile(key, b, h)) + jnp.exp(g_col) * mul_right(
            nn, tile(grad, b, h), begin[u]
        )
        result = result * (gain[:, h * C : (h + 1) * C] * SCALE)
        scaled[b * C : (b + 1) * C, h * C : (h + 1) * C] = result
        sums[b] = sums[b] + jnp.sum(result * tile(query, b, h).astype(f32), axis=1, keepdims=True)
    for b in range(pair):
        full = sums[b] * norm_cols[b * C : (b + 1) * C]
        sums_so_far[pl.ds(step * pair + b, 1)] = full.T[:1]

    @pl.when(step == steps - 1)
    def _():
        part[...] = jnp.broadcast_to(sums_so_far[...][None], part.shape)


def finish_queries(pair, query, scaled, norm_cols, sums, others, out, corrections):
    step = pl.program_id(0)

    @pl.when(step == 0)
    def _():
        corrections[...] = jnp.sum(sums[...], axis=0) * (1.0 / D)

    lines = [corrections[pl.ds(step * pair + b, 1)] for b in range(pair)]
    columns = columns_of(jnp.concatenate(lines, axis=0))
    for b in range(pair):
        part = slice(b * C, (b + 1) * C)
        norm = norm_cols[part][:, :1]
        factor = norm * norm * columns[:, b : b + 1]
        out[part] = (norm * scaled[part] - query[part].astype(f32) * factor).astype(bf16)


def key_grads(pair, heads, query, key, grad, gain, outgoing, inv, trans, adjoint, inner, fresh, starts, cols, rows, norm_rows, out, state):
    step = pl.program_id(0)
    units = all_units(pair, heads)
    count = len(units)
    row, col = iotas()
    half = C // 2
    width = heads * C

    @pl.when(step == 0)
    def _():
        for h in range(heads):
            for side in range(2):
                state[h, side * half : (side + 1) * half] = outgoing[2 * h + side]

    ends = [None] * count
    for b in reversed(range(pair)):
        for h in range(heads):
            u = b * heads + h
            ends[u] = halves(state[h])
            state[h] = mul3(nn, ends[u], halves(trans[b, h])) + adjoint[b, h]
    g_row = [rows[b, h : h + 1] for b, h in units]
    s_row = [rows[b, heads + h : heads + h + 1] for b, h in units]
    keys = [tile(key, b, h) for b, h in units]
    amounts = [halves(fresh[b, h]) for b, h in units]
    turned = []
    for u, (b, h) in enumerate(units):
        end = jnp.exp(g_row[u][:, C - 1 :] - g_row[u]) * (2.0 * s_row[u])
        turned.append(halves(inner[b, h] + mul_left(nt, ends[u], keys[u]) * end))
    results = [mul3(nn, turned[u], halves(inv[b, h])).T for u, (b, h) in enumerate(units)]
    for u, (b, h) in enumerate(units):
        out[b * C : (b + 1) * C, 2 * width + h * C : 2 * width + (h + 1) * C] = results[u].astype(bf16)
    results = [halves(x) for x in results]
    against = [mul3(nt, results[u], amounts[u]) for u in range(count)]
    across = [mul_left(nt, amounts[u], tile(grad, b, h)) for u, (b, h) in enumerate(units)]
    for u, (b, h) in enumerate(units):
        here = cols[b * C : (b + 1) * C]
        g_col = here[:, h : h + 1]
        s_col = here[:, heads + h : heads + h + 1]
        n_row = norm_rows[b, :1]
        below = jnp.exp(jnp.where(row > col, g_col - g_row[u], 0.0))
        pulled = jnp.where(row > col, -2.0 * below * against[u], 0.0)
        both = (pulled + pulled.T) * s_row[u]
        above = jnp.exp(jnp.where(row <= col, g_row[u] - g_col, 0.0))
        mixed = jnp.where(row <= col, 2.0 * above * n_row * across[u], 0.0)
        total = mul_left(nn, halves(both), keys[u])
        total += mul_left(nn, halves(mixed), tile(query, b, h)) * (
            gain[:, h * C : (h + 1) * C] * SCALE
        )
        total -= jnp.exp(g_col) * mul3(nn, results[u], halves(starts[b, h]))
        end = 2.0 * jnp.exp(g_row[u][:, C - 1 :] - g_col)
        total += end * mul3(nn, amounts[u], ends[u])
        unit = keys[u].astype(f32) * s_col
        along = jnp.sum(unit * total, axis=1, keepdims=True)
        out[b * C : (b + 1) * C, width + h * C : width + (h + 1) * C] = (
            s_col * (total - unit * along)
        ).astype(bf16)


def per_device(query_raw, key_raw, value_raw, query_gain, log_decay, out_grad):
    rows, width = query_raw.shape
    heads = log_decay.shape[0]
    blocks = rows // C
    group = lax.axis_size(HEAD)
    chain = lax.axis_size(SEQ)
    gain = query_gain.reshape(1, width)
    shape = jax.ShapeDtypeStruct

    def specs(pair, reverse=False):
        steps = blocks // pair

        def at(i):
            return steps - 1 - i if reverse else i

        return (
            steps,
            pl.BlockSpec((pair * C, width), lambda i: (at(i), 0)),
            pl.BlockSpec((pair, heads, C, C), lambda i: (at(i), 0, 0, 0)),
            pl.BlockSpec((pair * C, C), lambda i: (at(i), 0)),
            pl.BlockSpec((pair, 8, C), lambda i: (at(i), 0, 0)),
        )

    def fixed(*block):
        return pl.BlockSpec(block, lambda i: (0,) * len(block))

    def exchange(value, axis):
        return lax.all_to_all(value, axis, 0, 0, tiled=True)

    matrices = shape((blocks, heads, C, C), f32)
    columns = shape((rows, C), f32)
    lines = shape((blocks, 8, C), f32)
    sums = shape((group, blocks, C), f32)
    carry = pltpu.VMEM((heads, C, C), f32)
    line_scratch = pltpu.VMEM((blocks, C), f32)
    half = C // 2

    squares = exchange(
        pl.pallas_call(square_sums, out_shape=sums, name="square_sums")(query_raw), HEAD
    )

    steps, tokens, matrix, column, line = specs(PAIRS[0])
    inv, weight, trans, shift, cols, row_info, send = pl.pallas_call(
        functools.partial(prep_keys, PAIRS[0], heads, steps),
        grid=(steps,),
        in_specs=[tokens, tokens, pl.BlockSpec((heads, PAIRS[0] * C), lambda i: (0, i))],
        out_specs=[matrix] * 4 + [column, line, fixed(2 * heads, C + half, C)],
        out_shape=[matrices] * 4 + [columns, lines, shape((2 * heads, C + half, C), f32)],
        scratch_shapes=[carry, carry],
        name="prep_keys",
    )(key_raw, value_raw, log_decay)
    maps = exchange(send, SEQ)

    steps, tokens, matrix, column, line = specs(PAIRS[1], reverse=True)
    inner, adjoint, norm_cols, norm_rows, late = pl.pallas_call(
        functools.partial(prep_queries, PAIRS[1], heads, steps),
        grid=(steps,),
        in_specs=[tokens] * 3
        + [fixed(1, width), fixed(group, blocks, C)]
        + [matrix, matrix, column, line],
        out_specs=[matrix, matrix, column, line, fixed(2 * heads, half, C)],
        out_shape=[matrices, matrices, columns, lines, shape((2 * heads, half, C), f32)],
        scratch_shapes=[carry, line_scratch],
        name="prep_queries",
    )(query_raw, key_raw, out_grad, gain, squares, weight, trans, cols, row_info)

    incoming = exchange(
        pl.pallas_call(scan_states, out_shape=shape((chain, C, C), f32), name="scan_states")(
            maps, late
        ),
        SEQ,
    )
    outgoing = exchange(
        pl.pallas_call(
            scan_adjoints, out_shape=shape((chain, half, C), f32), name="scan_adjoints"
        )(maps, incoming),
        SEQ,
    )

    steps, tokens, matrix, column, line = specs(PAIRS[2])
    scaled, fresh, starts, part = pl.pallas_call(
        functools.partial(query_grads, PAIRS[2], heads, steps),
        grid=(steps,),
        in_specs=[tokens] * 4
        + [fixed(1, width), fixed(2 * heads, C, C)]
        + [matrix] * 4
        + [column, line, column],
        out_specs=[tokens, matrix, matrix, fixed(group, blocks, C)],
        out_shape=[shape((rows, width), f32), matrices, matrices, sums],
        scratch_shapes=[carry, line_scratch],
        name="query_grads",
    )(
        query_raw, key_raw, value_raw, out_grad, gain, incoming,
        inv, weight, trans, shift, cols, row_info, norm_cols,
    )
    corrections = exchange(part, HEAD)

    steps, tokens, matrix, column, line = specs(PAIRS[4], reverse=True)
    key_value = pl.pallas_call(
        functools.partial(key_grads, PAIRS[4], heads),
        grid=(steps,),
        in_specs=[tokens] * 3
        + [fixed(1, width), fixed(2 * heads, half, C)]
        + [matrix] * 6
        + [column, line, line],
        out_specs=pl.BlockSpec((PAIRS[4] * C, 3 * width), lambda i: (steps - 1 - i, 0)),
        out_shape=shape((rows, 3 * width), bf16),
        scratch_shapes=[carry],
        name="key_grads",
    )(
        query_raw, key_raw, out_grad, gain, outgoing,
        inv, trans, adjoint, inner, fresh, starts, cols, row_info, norm_rows,
    )

    steps, tokens, matrix, column, line = specs(PAIRS[3])
    grads = pl.pallas_call(
        functools.partial(finish_queries, PAIRS[3]),
        grid=(steps,),
        in_specs=[tokens, tokens, column, fixed(group, blocks, C), pl.BlockSpec(memory_space=pl.ANY)],
        out_specs=tokens,
        out_shape=shape((rows, 3 * width), bf16),
        input_output_aliases={4: 0},
        scratch_shapes=[line_scratch],
        name="finish_queries",
    )(query_raw, scaled, norm_cols, corrections, key_value)

    pieces = exchange(grads.reshape(group, rows // group, 3 * width), HEAD)
    return tuple(
        pieces[:, :, at : at + width].transpose(1, 0, 2).reshape(rows // group, group * width)
        for at in range(0, 3 * width, width)
    )


def solution(mesh):
    split = Mesh(mesh.devices.reshape(4, 2, 4, 4), ("seq_0", "seq_1", "head_0", "head_1"))
    return jax.shard_map(
        per_device,
        mesh=split,
        in_specs=(P(SEQ, HEAD), P(SEQ, HEAD), P(SEQ, HEAD), P(HEAD), P(HEAD, SEQ), P(SEQ, HEAD)),
        out_specs=(P(SEQ_HEAD, None), P(SEQ_HEAD, None), P(SEQ_HEAD, None)),
        check_vma=False,
    )
```

time: 180 us -> 171 us (0.950)
  blocking collectives: 24 us -> 61.2 us
  waiting for transfers between devices: 37.3 us -> 4.3 us
  starting transfers between devices: 37.4 us -> 23.1 us
  Pallas kernels: 71.1 us -> 75.4 us
    all_to_all x1 -> x2, blocking collectives: 24 us -> 61.2 us  [exchange(): return lax.all_to_all(value, axis, 0, 0, tiled=True)]
    all_to_all x8 -> x4, waiting for transfers between devices: 37.3 us -> 4.3 us  [exchange(): return lax.all_to_all(value, axis, 0, 0, tiled=True)]
    all_to_all x8 -> x4, starting transfers between devices: 37.4 us -> 23.1 us  [exchange(): return lax.all_to_all(value, axis, 0, 0, tiled=True)]
    pallas_call x7 -> x8, Pallas kernels: 71.1 us -> 75.4 us  [the longest x1 23.4 us: per_device(): pl.pallas_call(functools.partial(prep_keys, PAIRS[0], heads, steps), grid...]
    all_to_all x3 -> x0, local copies, waits for them, and re-layouts: 3.21 us -> none  [owned(): return lax.all_to_all(array, HEAD, split_axis=0, concat_axis=1, tiled=True)]
    reshape x0 -> x3, local copies, waits for them, and re-layouts: none -> 3.19 us  [per_device(): pieces[:, :, at:at + width].transpose(1, 0, 2)]
  transfers between devices with their start and end apart: 8 -> 4, of which waited for: 5 -> 1; matrix products, arithmetic and copies ran while one was open for 2% -> 0% of each run, Pallas kernels for 40% -> 36%
where the time goes in v2:
time: 171 us; the launch traced here: 170 us
  Pallas kernels  75.4 us (44%)
  blocking collectives  61.2 us (36%)
  starting transfers between devices  23.1 us (14%)
  local copies, waits for them, and re-layouts  5.08 us (3%)
  waiting for transfers between devices  4.3 us (3%)
    all_to_all x2, blocking collectives, exchange(): return lax.all_to_all(value, axis, 0, 0, tiled=True)  61.2 us
    pallas_call x1, Pallas kernels, per_device(): pl.pallas_call(functools.partial(prep_keys, PAIRS[0], heads, steps), grid...  23.4 us
    all_to_all x4, starting transfers between devices, exchange(): return lax.all_to_all(value, axis, 0, 0, tiled=True)  23.1 us
    pallas_call x1, Pallas kernels, per_device(): pl.pallas_call(functools.partial(key_grads, PAIRS[4], heads), grid=(steps...  16.7 us
    pallas_call x1, Pallas kernels, per_device(): pl.pallas_call(functools.partial(query_grads, PAIRS[2], heads, steps), gr...  12.9 us
    pallas_call x1, Pallas kernels, per_device(): pl.pallas_call(functools.partial(prep_queries, PAIRS[1], heads, steps), g...  8.82 us
    pallas_call x1, Pallas kernels, per_device(): pl.pallas_call(functools.partial(finish_queries, PAIRS[3]), grid=(steps,)...  4.57 us
    all_to_all x4, waiting for transfers between devices, exchange(): return lax.all_to_all(value, axis, 0, 0, tiled=True)  4.3 us
  transfers between devices with their start and end apart: 4, of which 1 were waited for; matrix products, arithmetic and copies ran while one was open for 0% of the time, Pallas kernels for 36%

profile of v2, /device:TPU:0, one launch (start us, length us, event | category | flops | bytes accessed | tf_op | source)
XLA Modules:
  0.0 169.8 jit_solution(16204920946709246478)
XLA Ops:
  0.6 2.6 %square_sums.1 = f32[16,8,128]{2,1,0:T(8,128)} custom-call(bf16[1024,512]{1,0:T(8,128)(2,1)} %query.9), custom_call_target="tpu_custom_call" | custom-call | tf_op jit(solution)/shard_map/square_sums/pallas_call | solution.py:411
  3.2 7.1 %all-to-all-start.1 = ((f32[16,8,128]{2,1,0:T(8,128)}), f32[16,8,128]{2,1,0:T(8,128)S(1)}, u32[]{:S(2)}, u32[]{:S(2)}) async-start(f32[16,8,128]{2,1,0:T(8,128)} %square_sums.1), calls=%async_computation.1 | async-start | bytes 131072 | tf_op jit(solution)/shard_map/all_to_all | solution.py:400
  10.4 23.4 %prep_keys.1 = (f32[8,4,128,128]{3,2,1,0:T(8,128)}, f32[8,4,128,128]{3,2,1,0:T(8,128)}, f32[8,4,128,128]{3,2,1,0:T(8,128)}, f32[8,4,128,128]{3,2,1,0:T(8,128)}, ...) custom-call(bf16[1024,512]{1,0:T(8,128)(2,1)} %key.7, bf16[1024,512]{1,0:T(8,128)(2,1)} %value.3, ...), custom_call_target="tpu_custom_call" | custom-call | tf_op jit(solution)/shard_map/prep_keys/pallas_call | solution.py:415
  33.8 0.0 all-to-all-done.1.sums
  33.8 0.0 copy-start.2
  33.8 5.3 %all-to-all-start = ((f32[8,192,128]{2,1,0:T(8,128)}), f32[8,192,128]{2,1,0:T(8,128)S(1)}, u32[]{:S(2)}, u32[]{:S(2)}) async-start(f32[8,192,128]{2,1,0:T(8,128)} %get-tuple-element.19), calls=%async_computation | async-start | bytes 1572864 | tf_op jit(solution)/shard_map/all_to_all | solution.py:400
  39.1 0.0 copy-done.2
  39.1 8.8 %prep_queries.1 = (f32[8,4,128,128]{3,2,1,0:T(8,128)}, f32[8,4,128,128]{3,2,1,0:T(8,128)}, f32[1024,128]{1,0:T(8,128)}, f32[8,8,128]{2,1,0:T(8,128)}, f32[8,64,128]{2,1,0:T(8,128)}) custom-call(bf16[1024,512]{1,0:T(8,128)(2,1)} %query.9, bf16[1024,512]{1,0:T(8,128)(2,1)} %key.7, bf16[1024,512]{1,0:T(8,128)(2,1)} %grad.5, f32[1,512]{1,0:T(1,128)} %bitcast.18, ...), custom_call_target="tpu_custom_call" | custom-call | tf_op jit(solution)/shard_map/prep_queries/pallas_call | solution.py:427
  48.0 4.3 %all-to-all-done.received.maps = f32[8,192,128]{2,1,0:T(8,128)S(1)} async-done(((f32[8,192,128]{2,1,0:T(8,128)}), f32[8,192,128]{2,1,0:T(8,128)S(1)}, u32[]{:S(2)}, u32[]{:S(2)}) %all-to-all-start) | async-done | bytes 786464 | tf_op jit(solution)/shard_map/all_to_all | solution.py:400
  52.3 0.0 copy-start
  52.3 0.9 copy-done
  53.1 3.3 %scan_states.1 = f32[8,128,128]{2,1,0:T(8,128)} custom-call(f32[8,192,128]{2,1,0:T(8,128)} %copy-done, f32[8,64,128]{2,1,0:T(8,128)} %get-tuple-element.24.late), custom_call_target="tpu_custom_call" | custom-call | tf_op jit(solution)/shard_map/scan_states/pallas_call | solution.py:440
  56.5 14.5 %all_to_all.30.incoming.received = f32[8,128,128]{2,1,0:T(8,128)} all-to-all(f32[8,128,128]{2,1,0:T(8,128)} %scan_states.1), channel_id=1, replica_groups=mesh['seq_0'=4,'seq_1'=2,'head_0'=4,'head_1'=4] {'seq_0','seq_1'}, dimensions={0} | all-to-all | bytes 1048576 | tf_op jit(solution)/shard_map/all_to_all | solution.py:400
  71.0 3.1 %scan_adjoints.1 = f32[8,64,128]{2,1,0:T(8,128)} custom-call(f32[8,192,128]{2,1,0:T(8,128)} %copy-done, f32[8,128,128]{2,1,0:T(8,128)} %all_to_all.30.incoming.received), custom_call_target="tpu_custom_call" | custom-call | tf_op jit(solution)/shard_map/scan_adjoints/pallas_call | solution.py:446
  74.0 3.4 %all-to-all-start.4 = ((f32[8,64,128]{2,1,0:T(8,128)}), f32[8,64,128]{2,1,0:T(8,128)S(1)}, u32[]{:S(2)}, u32[]{:S(2)}) async-start(f32[8,64,128]{2,1,0:T(8,128)} %scan_adjoints.1), calls=%async_computation.4 | async-start | bytes 524288 | tf_op jit(solution)/shard_map/all_to_all | solution.py:400
  77.5 12.9 %query_grads.1 = (f32[1024,512]{1,0:T(8,128)}, f32[8,4,128,128]{3,2,1,0:T(8,128)}, f32[8,4,128,128]{3,2,1,0:T(8,128)}, f32[16,8,128]{2,1,0:T(8,128)}) custom-call(bf16[1024,512]{1,0:T(8,128)(2,1)} %query.9, bf16[1024,512]{1,0:T(8,128)(2,1)} %key.7, bf16[1024,512]{1,0:T(8,128)(2,1)} %value.3, bf16[1024,512]{1,0:T(8,128)(2,1)} %grad.5, f32[1,512]{1,0:T(1,128)} %bitcast.19, ...), custom_call_target="tpu_custom_call" | custom-call | tf_op jit(solution)/shard_map/query_grads/pallas_call | solution.py:453
  90.4 0.0 all-to-all-done.4.outgoing
  90.4 0.0 copy-start.1
  90.4 7.2 %all-to-all-start.3 = ((f32[16,8,128]{2,1,0:T(8,128)}), f32[16,8,128]{2,1,0:T(8,128)S(1)}, u32[]{:S(2)}, u32[]{:S(2)}) async-start(f32[16,8,128]{2,1,0:T(8,128)} %get-tuple-element.29), calls=%async_computation.3 | async-start | bytes 131072 | tf_op jit(solution)/shard_map/all_to_all | solution.py:400
  97.6 0.0 copy-done.1
  97.6 16.7 %key_grads.1.others = bf16[1024,1536]{1,0:T(8,128)(2,1)} custom-call(bf16[1024,512]{1,0:T(8,128)(2,1)} %query.9, bf16[1024,512]{1,0:T(8,128)(2,1)} %key.7, bf16[1024,512]{1,0:T(8,128)(2,1)} %grad.5, f32[1,512]{1,0:T(1,128)} %bitcast.20, f32[8,64,128]{2,1,0:T(8,128)} %copy-done.1, f32[8,4,128,128]{3,2,1,0:T(8,128)} %get-tuple-element.25.inv, ...), custom_call_target="tpu_custom_call" | custom-call | tf_op jit(solution)/shard_map/key_grads/pallas_call | solution.py:471
  114.3 0.0 all-to-all-done.3.sums
  114.3 0.0 copy-start.3
  114.3 0.6 copy-done.3
  115.0 4.6 %finish_queries.1 = bf16[1024,1536]{1,0:T(8,128)(2,1)} custom-call(bf16[1024,512]{1,0:T(8,128)(2,1)} %query.9, f32[1024,512]{1,0:T(8,128)} %get-tuple-element.28.scaled, f32[1024,128]{1,0:T(8,128)} %get-tuple-element.27.norm_cols, f32[16,8,128]{2,1,0:T(8,128)} %copy-done.3, bf16[1024,1536]{1,0:T(8,128)(2,1)} %key_grads.1.others), custom_call_target="tpu_custom_call", output_to_operand_aliasing={{}: (4, {})} | custom-call | tf_op jit(solution)/shard_map/finish_queries/pallas_call | solution.py:488
  119.5 46.7 %all_to_all.31 = bf16[16,64,1536]{2,1,0:T(8,128)(2,1)S(1)} all-to-all(bf16[16,64,1536]{2,1,0:T(8,128)(2,1)} %bitcast.14), channel_id=1, replica_groups=mesh['seq_0'=4,'seq_1'=2,'head_0'=4,'head_1'=4] {'head_0','head_1'}, dimensions={0} | all-to-all | bytes 6291456 | tf_op jit(solution)/shard_map/all_to_all | solution.py:400
  166.2 0.4 slice_bitcast_fusion
  166.6 1.1 copy.15
  167.7 1.1 copy.14
  168.7 1.1 copy.13
Async XLA Ops:
  3.2 30.6 %all-to-all-start.1 = ((f32[16,8,128]{2,1,0:T(8,128)}), f32[16,8,128]{2,1,0:T(8,128)S(1)}, u32[]{:S(2)}, u32[]{:S(2)}) async-start(f32[16,8,128]{2,1,0:T(8,128)} %square_sums.1), calls=%async_computation.1 | async-start | bytes 131072 | tf_op jit(solution)/shard_map/all_to_all | solution.py:400
  33.8 5.3 %copy-start.2 = (f32[16,8,128]{2,1,0:T(8,128)}, f32[16,8,128]{2,1,0:T(8,128)S(1)}, u32[]{:S(2)}) copy-start(f32[16,8,128]{2,1,0:T(8,128)S(1)} %all-to-all-done.1.sums) | copy-start | bytes 196612
  33.8 18.4 %all-to-all-start = ((f32[8,192,128]{2,1,0:T(8,128)}), f32[8,192,128]{2,1,0:T(8,128)S(1)}, u32[]{:S(2)}, u32[]{:S(2)}) async-start(f32[8,192,128]{2,1,0:T(8,128)} %get-tuple-element.19), calls=%async_computation | async-start | bytes 1572864 | tf_op jit(solution)/shard_map/all_to_all | solution.py:400
  52.3 0.9 copy-start
  74.0 16.3 %all-to-all-start.4 = ((f32[8,64,128]{2,1,0:T(8,128)}), f32[8,64,128]{2,1,0:T(8,128)S(1)}, u32[]{:S(2)}, u32[]{:S(2)}) async-start(f32[8,64,128]{2,1,0:T(8,128)} %scan_adjoints.1), calls=%async_computation.4 | async-start | bytes 524288 | tf_op jit(solution)/shard_map/all_to_all | solution.py:400
  90.4 7.3 %copy-start.1 = (f32[8,64,128]{2,1,0:T(8,128)}, f32[8,64,128]{2,1,0:T(8,128)S(1)}, u32[]{:S(2)}) copy-start(f32[8,64,128]{2,1,0:T(8,128)S(1)} %all-to-all-done.4.outgoing) | copy-start | bytes 786436
  90.4 23.9 %all-to-all-start.3 = ((f32[16,8,128]{2,1,0:T(8,128)}), f32[16,8,128]{2,1,0:T(8,128)S(1)}, u32[]{:S(2)}, u32[]{:S(2)}) async-start(f32[16,8,128]{2,1,0:T(8,128)} %get-tuple-element.29), calls=%async_computation.3 | async-start | bytes 131072 | tf_op jit(solution)/shard_map/all_to_all | solution.py:400
  114.3 0.6 copy-start.3

commit v3 on v2

--- a/solution.py
+++ b/solution.py
@@ -8,9 +8,10 @@
 from jax.sharding import Mesh
 from jax.sharding import PartitionSpec as P
 
+
 D = 8192
 C = 128
-PAIRS = (2, 2, 2, 2, 2)
+PAIRS = (2, 2, 2, 4, 4)
 HEAD = ("head_0", "head_1")
 SEQ = ("seq_0", "seq_1")
 SEQ_HEAD = ("seq_0", "seq_1", "head_0", "head_1")
@@ -75,7 +76,7 @@
     return [(b, h) for b in range(pair) for h in range(heads)]
 
 
-def prep_keys(pair, heads, steps, key, value, decay, inv, weight, trans, shift, cols, rows, send, whole, offset):
+def prep_keys(pair, heads, steps, place, key, value, decay, inv, weight, trans, shift, cols, rows, mine, other, whole, offset):
     step = pl.program_id(0)
     units = all_units(pair, heads)
     count = len(units)
@@ -103,8 +104,8 @@
     scale_rows = gathered.T
 
     for b in range(pair):
-        mine = slice(b * heads, (b + 1) * heads)
-        rows[b] = jnp.concatenate([cumul_rows[mine], scale_rows[mine]], axis=0)
+        these = slice(b * heads, (b + 1) * heads)
+        rows[b] = jnp.concatenate([cumul_rows[these], scale_rows[these]], axis=0)
         packed = jnp.zeros((C, C), f32)
         for h in range(heads):
             u = b * heads + h
@@ -166,14 +167,57 @@
 
     @pl.when(step == steps - 1)
     def _():
-        half = C // 2
-        for h in range(heads):
-            for part in range(2):
-                send[2 * h + part, :C] = whole[h]
-                send[2 * h + part, C:] = offset[h, part * half : (part + 1) * half]
-
-
-def prep_queries(pair, heads, steps, query, key, grad, gain, sums, weight, trans, cols, rows, inner, adjoint, norm_cols, norm_rows, send, total, norms):
+        half = heads // 2
+        first = place[1] * half
+        for j in range(half):
+            mine[j, 0] = whole[first + j]
+            mine[j, 1] = offset[first + j]
+            other[j, 0] = whole[half - first + j]
+            other[j, 1] = offset[half - first + j]
+
+
+def chip_maps(place, mine, other, out):
+    first = place[1] == 0
+    for j in range(mine.shape[0]):
+        early = [jnp.where(first, mine[j, i], other[j, i]) for i in range(2)]
+        late = [jnp.where(first, other[j, i], mine[j, i]) for i in range(2)]
+        step_map = halves(late[0])
+        out[j, 0] = mul3(nn, step_map, halves(early[0]))
+        out[j, 1] = mul3(nt, halves(early[1]), step_map) + late[1]
+
+
+def chip_states(place, mine, other, one, two, three, mine_back, other_back, stay, leave, back):
+    first = place[1] == 0
+    for j in range(mine.shape[0]):
+        state = jnp.zeros((C, C), f32)
+        for k, behind in ((3, three), (2, two), (1, one)):
+            moved = mul3(nt, halves(state), halves(behind[j, 0])) + behind[j, 1]
+            state = jnp.where(place[0] >= k, moved, state)
+        early = [jnp.where(first, mine[j, i], other[j, i]) for i in range(2)]
+        step_map = halves(early[0])
+        after = mul3(nt, halves(state), step_map) + early[1]
+        stay[j] = jnp.where(first, state, after)
+        leave[j] = jnp.where(first, after, state)
+        early_back = jnp.where(first, mine_back[j], other_back[j])
+        late_back = jnp.where(first, other_back[j], mine_back[j])
+        back[j] = mul3(nn, halves(late_back), step_map) + early_back
+
+
+def chip_adjoints(last, place, mine, other, one, two, three, one_back, two_back, three_back, mine_back, other_back, stay, leave):
+    first = place[1] == 0
+    for j in range(mine.shape[0]):
+        state = jnp.zeros((C, C), f32)
+        for k, ahead, term in ((3, one, one_back), (2, two, two_back), (1, three, three_back)):
+            moved = mul3(nn, halves(state), halves(ahead[j, 0])) + term[j]
+            state = jnp.where(place[0] + k <= last, moved, state)
+        late = jnp.where(first, other[j, 0], mine[j, 0])
+        late_back = jnp.where(first, other_back[j], mine_back[j])
+        before = mul3(nn, halves(state), halves(late)) + late_back
+        stay[j] = jnp.where(first, before, state)
+        leave[j] = jnp.where(first, state, before)
+
+
+def prep_queries(pair, heads, steps, place, query, key, grad, gain, sums, weight, trans, cols, rows, inner, adjoint, norm_cols, norm_rows, mine, other, total, norms):
     step = pl.program_id(0)
     units = all_units(pair, heads)
     count = len(units)
@@ -221,44 +265,27 @@
             u = b * heads + h
             total[h] = mul3(nn, halves(total[h]), halves(trans[b, h])) + terms[u]
 
-    half = C // 2
-    for h in range(heads):
-        for part in range(2):
-            send[2 * h + part] = total[h, part * half : (part + 1) * half]
-
-
-def scan_states(received, late, out):
-    count = received.shape[0]
-    half = C // 2
-    state = jnp.zeros((half, C), f32)
-    for k in range(count):
-        out[k, :half] = state
-        out[k, half:] = late[k]
-        if k < count - 1:
-            state = mul3(nt, halves(state), halves(received[k, :C])) + received[k, C:]
-
-
-def scan_adjoints(maps, received, out):
-    count = received.shape[0]
-    half = C // 2
-    state = jnp.zeros((half, C), f32)
-    for k in reversed(range(count)):
-        out[k] = state
-        if k:
-            state = mul3(nn, halves(state), halves(maps[k, :C])) + received[k, half:]
-
-
-def query_grads(pair, heads, steps, query, key, value, grad, gain, incoming, inv, weight, trans, shift, cols, rows, norm_cols, scaled, fresh, starts, part, state, sums_so_far):
+    @pl.when(step == steps - 1)
+    def _():
+        half = heads // 2
+        begin = place[1] * half
+        for j in range(half):
+            mine[j] = total[begin + j]
+            other[j] = total[half - begin + j]
+
+
+def query_grads(pair, heads, steps, place, query, key, value, grad, gain, mine, other, inv, weight, trans, shift, cols, rows, norm_cols, scaled, fresh, starts, part, state, sums_so_far):
     step = pl.program_id(0)
     units = all_units(pair, heads)
     row, col = iotas()
-    half = C // 2
 
     @pl.when(step == 0)
     def _():
-        for h in range(heads):
-            for side in range(2):
-                state[h, side * half : (side + 1) * half] = incoming[2 * h + side, :half]
+        half = heads // 2
+        first = place[1] * half
+        for j in range(half):
+            state[first + j] = mine[j]
+            state[half - first + j] = other[j]
 
     for b in range(pair):
         for h in range(heads):
@@ -312,28 +339,29 @@
         out[part] = (norm * scaled[part] - query[part].astype(f32) * factor).astype(bf16)
 
 
-def key_grads(pair, heads, query, key, grad, gain, outgoing, inv, trans, adjoint, inner, fresh, starts, cols, rows, norm_rows, out, state):
+def key_grads(pair, heads, part, place, query, key, grad, gain, mine, other, inv, trans, adjoint, inner, fresh, starts, cols, rows, norm_rows, ready, out, state):
     step = pl.program_id(0)
-    units = all_units(pair, heads)
+    taken = heads // 2
+    begin = part * taken
+    units = all_units(pair, taken)
     count = len(units)
     row, col = iotas()
-    half = C // 2
-    width = heads * C
+    width = taken * C
 
     @pl.when(step == 0)
     def _():
-        for h in range(heads):
-            for side in range(2):
-                state[h, side * half : (side + 1) * half] = outgoing[2 * h + side]
+        own = place[1] == part
+        for h in range(taken):
+            state[h] = jnp.where(own, mine[h], other[h])
 
     ends = [None] * count
     for b in reversed(range(pair)):
-        for h in range(heads):
-            u = b * heads + h
+        for h in range(taken):
+            u = b * taken + h
             ends[u] = halves(state[h])
             state[h] = mul3(nn, ends[u], halves(trans[b, h])) + adjoint[b, h]
-    g_row = [rows[b, h : h + 1] for b, h in units]
-    s_row = [rows[b, heads + h : heads + h + 1] for b, h in units]
+    g_row = [rows[b, begin + h : begin + h + 1] for b, h in units]
+    s_row = [rows[b, heads + begin + h : heads + begin + h + 1] for b, h in units]
     keys = [tile(key, b, h) for b, h in units]
     amounts = [halves(fresh[b, h]) for b, h in units]
     turned = []
@@ -342,14 +370,14 @@
         turned.append(halves(inner[b, h] + mul_left(nt, ends[u], keys[u]) * end))
     results = [mul3(nn, turned[u], halves(inv[b, h])).T for u, (b, h) in enumerate(units)]
     for u, (b, h) in enumerate(units):
-        out[b * C : (b + 1) * C, 2 * width + h * C : 2 * width + (h + 1) * C] = results[u].astype(bf16)
+        out[b * C : (b + 1) * C, width + h * C : width + (h + 1) * C] = results[u].astype(bf16)
     results = [halves(x) for x in results]
     against = [mul3(nt, results[u], amounts[u]) for u in range(count)]
     across = [mul_left(nt, amounts[u], tile(grad, b, h)) for u, (b, h) in enumerate(units)]
     for u, (b, h) in enumerate(units):
         here = cols[b * C : (b + 1) * C]
-        g_col = here[:, h : h + 1]
-        s_col = here[:, heads + h : heads + h + 1]
+        g_col = here[:, begin + h : begin + h + 1]
+        s_col = here[:, heads + begin + h : heads + begin + h + 1]
         n_row = norm_rows[b, :1]
         below = jnp.exp(jnp.where(row > col, g_col - g_row[u], 0.0))
         pulled = jnp.where(row > col, -2.0 * below * against[u], 0.0)
@@ -365,7 +393,7 @@
         total += end * mul3(nn, amounts[u], ends[u])
         unit = keys[u].astype(f32) * s_col
         along = jnp.sum(unit * total, axis=1, keepdims=True)
-        out[b * C : (b + 1) * C, width + h * C : width + (h + 1) * C] = (
+        out[b * C : (b + 1) * C, h * C : (h + 1) * C] = (
             s_col * (total - unit * along)
         ).astype(bf16)
 
@@ -375,7 +403,6 @@
     heads = log_decay.shape[0]
     blocks = rows // C
     group = lax.axis_size(HEAD)
-    chain = lax.axis_size(SEQ)
     gain = query_gain.reshape(1, width)
     shape = jax.ShapeDtypeStruct
 
@@ -405,56 +432,79 @@
     sums = shape((group, blocks, C), f32)
     carry = pltpu.VMEM((heads, C, C), f32)
     line_scratch = pltpu.VMEM((blocks, C), f32)
-    half = C // 2
+
+    cores = lax.axis_size("seq_1")
+    chips = lax.axis_size("seq_0")
+    assert (chips, cores) == (4, 2) and heads % 2 == 0
+    some = heads // 2
+    place = jnp.stack([lax.axis_index("seq_0"), lax.axis_index("seq_1")]).astype(jnp.int32)
+    scalar = pl.BlockSpec(memory_space=pltpu.SMEM)
+    pair_maps = shape((some, 2, C, C), f32)
+    pair_states = shape((some, C, C), f32)
+
+    def to_other_core(value):
+        return lax.ppermute(value, "seq_1", [(0, 1), (1, 0)])
+
+    def from_chips_behind(value):
+        pieces = []
+        for k in range(1, chips):
+            pieces.append(
+                lax.ppermute(value, "seq_0", [(i, (i + k) % chips) for i in range(chips)])
+            )
+        return pieces
+
+    def small(kernel, out_shape, *operands):
+        return pl.pallas_call(
+            kernel,
+            in_specs=[scalar] + [pl.BlockSpec(memory_space=pltpu.VMEM)] * (len(operands) - 1),
+            out_shape=out_shape,
+        )(*operands)
 
     squares = exchange(
         pl.pallas_call(square_sums, out_shape=sums, name="square_sums")(query_raw), HEAD
     )
 
     steps, tokens, matrix, column, line = specs(PAIRS[0])
-    inv, weight, trans, shift, cols, row_info, send = pl.pallas_call(
+    inv, weight, trans, shift, cols, row_info, mine, other = pl.pallas_call(
         functools.partial(prep_keys, PAIRS[0], heads, steps),
         grid=(steps,),
-        in_specs=[tokens, tokens, pl.BlockSpec((heads, PAIRS[0] * C), lambda i: (0, i))],
-        out_specs=[matrix] * 4 + [column, line, fixed(2 * heads, C + half, C)],
-        out_shape=[matrices] * 4 + [columns, lines, shape((2 * heads, C + half, C), f32)],
+        in_specs=[scalar, tokens, tokens, pl.BlockSpec((heads, PAIRS[0] * C), lambda i: (0, i))],
+        out_specs=[matrix] * 4 + [column, line] + [fixed(some, 2, C, C)] * 2,
+        out_shape=[matrices] * 4 + [columns, lines, pair_maps, pair_maps],
         scratch_shapes=[carry, carry],
         name="prep_keys",
-    )(key_raw, value_raw, log_decay)
-    maps = exchange(send, SEQ)
+    )(place, key_raw, value_raw, log_decay)
+    other = to_other_core(other)
+    behind = from_chips_behind(small(chip_maps, pair_maps, place, mine, other))
 
     steps, tokens, matrix, column, line = specs(PAIRS[1], reverse=True)
-    inner, adjoint, norm_cols, norm_rows, late = pl.pallas_call(
+    inner, adjoint, norm_cols, norm_rows, mine_back, other_back = pl.pallas_call(
         functools.partial(prep_queries, PAIRS[1], heads, steps),
         grid=(steps,),
-        in_specs=[tokens] * 3
+        in_specs=[scalar]
+        + [tokens] * 3
         + [fixed(1, width), fixed(group, blocks, C)]
         + [matrix, matrix, column, line],
-        out_specs=[matrix, matrix, column, line, fixed(2 * heads, half, C)],
-        out_shape=[matrices, matrices, columns, lines, shape((2 * heads, half, C), f32)],
+        out_specs=[matrix, matrix, column, line] + [fixed(some, C, C)] * 2,
+        out_shape=[matrices, matrices, columns, lines, pair_states, pair_states],
         scratch_shapes=[carry, line_scratch],
         name="prep_queries",
-    )(query_raw, key_raw, out_grad, gain, squares, weight, trans, cols, row_info)
-
-    incoming = exchange(
-        pl.pallas_call(scan_states, out_shape=shape((chain, C, C), f32), name="scan_states")(
-            maps, late
-        ),
-        SEQ,
-    )
-    outgoing = exchange(
-        pl.pallas_call(
-            scan_adjoints, out_shape=shape((chain, half, C), f32), name="scan_adjoints"
-        )(maps, incoming),
-        SEQ,
-    )
+    )(place, query_raw, key_raw, out_grad, gain, squares, weight, trans, cols, row_info)
+    other_back = to_other_core(other_back)
+    stay, leave, back = small(
+        chip_states, [pair_states] * 3,
+        place, mine, other, *behind, mine_back, other_back,
+    )
+    arrived = to_other_core(leave)
+    ahead = from_chips_behind(back)
 
     steps, tokens, matrix, column, line = specs(PAIRS[2])
     scaled, fresh, starts, part = pl.pallas_call(
         functools.partial(query_grads, PAIRS[2], heads, steps),
         grid=(steps,),
-        in_specs=[tokens] * 4
-        + [fixed(1, width), fixed(2 * heads, C, C)]
+        in_specs=[scalar]
+        + [tokens] * 4
+        + [fixed(1, width), fixed(some, C, C), fixed(some, C, C)]
         + [matrix] * 4
         + [column, line, column],
         out_specs=[tokens, matrix, matrix, fixed(group, blocks, C)],
@@ -462,44 +512,72 @@
         scratch_shapes=[carry, line_scratch],
         name="query_grads",
     )(
-        query_raw, key_raw, value_raw, out_grad, gain, incoming,
+        place, query_raw, key_raw, value_raw, out_grad, gain, stay, arrived,
         inv, weight, trans, shift, cols, row_info, norm_cols,
     )
     corrections = exchange(part, HEAD)
 
-    steps, tokens, matrix, column, line = specs(PAIRS[4], reverse=True)
-    key_value = pl.pallas_call(
-        functools.partial(key_grads, PAIRS[4], heads),
-        grid=(steps,),
-        in_specs=[tokens] * 3
-        + [fixed(1, width), fixed(2 * heads, half, C)]
-        + [matrix] * 6
-        + [column, line, line],
-        out_specs=pl.BlockSpec((PAIRS[4] * C, 3 * width), lambda i: (steps - 1 - i, 0)),
-        out_shape=shape((rows, 3 * width), bf16),
-        scratch_shapes=[carry],
-        name="key_grads",
-    )(
-        query_raw, key_raw, out_grad, gain, outgoing,
-        inv, trans, adjoint, inner, fresh, starts, cols, row_info, norm_rows,
-    )
+    stay, leave = small(
+        functools.partial(chip_adjoints, chips - 1), [pair_states] * 2,
+        place, mine, other, *behind, *ahead, mine_back, other_back,
+    )
+    arrived = to_other_core(leave)
+
+    def key_half(index, out_shape, at, ready):
+        pair = PAIRS[4]
+        steps, _, _, column, line = specs(pair, reverse=True)
+        tokens = pl.BlockSpec((pair * C, some * C), lambda i: (steps - 1 - i, index))
+        matrix = pl.BlockSpec((pair, some, C, C), lambda i: (steps - 1 - i, index, 0, 0))
+        return pl.pallas_call(
+            functools.partial(key_grads, pair, heads, index),
+            grid=(steps,),
+            in_specs=[scalar]
+            + [tokens] * 3
+            + [pl.BlockSpec((1, some * C), lambda i: (0, index))]
+            + [fixed(some, C, C)] * 2
+            + [matrix] * 6
+            + [column, line, line, pl.BlockSpec(memory_space=pl.ANY)],
+            out_specs=pl.BlockSpec((pair * C, 2 * some * C), lambda i: (steps - 1 - i, at)),
+            out_shape=shape((rows, out_shape), bf16),
+            scratch_shapes=[pltpu.VMEM((some, C, C), f32)],
+        )(
+            place, query_raw, key_raw, out_grad, gain, stay, arrived,
+            inv, trans, adjoint, inner, fresh, starts, cols, row_info, norm_rows, ready,
+        )
+
+    def owned(array):
+        return exchange(array.reshape(group, rows // group, array.shape[1]), HEAD)
+
+    first_half = key_half(0, width, 0, part)
+    first = owned(first_half)
+    second_half = key_half(1, 2 * width, 1, first_half)
 
     steps, tokens, matrix, column, line = specs(PAIRS[3])
-    grads = pl.pallas_call(
-        functools.partial(finish_queries, PAIRS[3]),
-        grid=(steps,),
-        in_specs=[tokens, tokens, column, fixed(group, blocks, C), pl.BlockSpec(memory_space=pl.ANY)],
-        out_specs=tokens,
-        out_shape=shape((rows, 3 * width), bf16),
-        input_output_aliases={4: 0},
-        scratch_shapes=[line_scratch],
-        name="finish_queries",
-    )(query_raw, scaled, norm_cols, corrections, key_value)
-
-    pieces = exchange(grads.reshape(group, rows // group, 3 * width), HEAD)
-    return tuple(
-        pieces[:, :, at : at + width].transpose(1, 0, 2).reshape(rows // group, group * width)
-        for at in range(0, 3 * width, width)
+    second = owned(
+        pl.pallas_call(
+            functools.partial(finish_queries, PAIRS[3]),
+            grid=(steps,),
+            in_specs=[
+                tokens, tokens, column, fixed(group, blocks, C),
+                pl.BlockSpec(memory_space=pl.ANY),
+            ],
+            out_specs=tokens,
+            out_shape=shape((rows, 2 * width), bf16),
+            input_output_aliases={4: 0},
+            scratch_shapes=[line_scratch],
+            name="finish_queries",
+        )(query_raw, scaled, norm_cols, corrections, second_half),
+    )
+
+    def lay(*pieces):
+        whole = pieces[0] if len(pieces) == 1 else jnp.concatenate(pieces, axis=2)
+        return whole.transpose(1, 0, 2).reshape(rows // group, group * width)
+
+    side = some * C
+    return (
+        lay(second[:, :, :width]),
+        lay(first[:, :, :side], second[:, :, width : width + side]),
+        lay(first[:, :, side:], second[:, :, width + side :]),
     )
 
 

time: 171 us -> 173 us (1.012)
  blocking collectives: 61.2 us -> 14.8 us
  waiting for transfers between devices: 4.3 us -> 42.9 us
  Pallas kernels: 75.4 us -> 80.6 us
  local copies, waits for them, and re-layouts: 5.08 us -> 8.48 us
    all_to_all x2 -> x1, blocking collectives: 61.2 us -> 14.8 us  [exchange(): return lax.all_to_all(value, axis, 0, 0, tiled=True)]
    all_to_all x4 -> x3, waiting for transfers between devices: 4.3 us -> 32.1 us  [exchange(): return lax.all_to_all(value, axis, 0, 0, tiled=True)]
    ppermute x0 -> x10, waiting for transfers between devices: none -> 10.8 us  [the longest x6 7.5 us: from_chips_behind(): lax.ppermute(value, 'seq_0', [(i, (i + k) % chips) for i in range(chips)])]
    ppermute x0 -> x10, starting transfers between devices: none -> 9.84 us  [the longest x6 9.66 us: from_chips_behind(): lax.ppermute(value, 'seq_0', [(i, (i + k) % chips) for i in range(chips)])]
    all_to_all x4 -> x3, starting transfers between devices: 23.1 us -> 14.4 us  [exchange(): return lax.all_to_all(value, axis, 0, 0, tiled=True)]
    pallas_call x3 -> x5, Pallas kernels: 23.1 us -> 28.9 us  [the longest x2 20 us: key_half(): pl.pallas_call(functools.partial(key_grads, pair, heads, index), grid=(st...]
    unnamed x9 -> x27, local copies, waits for them, and re-layouts: 1.89 us -> 4.05 us
  transfers between devices with their start and end apart: 4 -> 13, of which waited for: 1 -> 7; matrix products, arithmetic and copies ran while one was open for 0% -> 1% of each run, Pallas kernels for 36% -> 30%
where the time goes in v3:
time: 173 us
  Pallas kernels  80.6 us (47%)
  waiting for transfers between devices  42.9 us (25%)
  starting transfers between devices  24.2 us (14%)
  blocking collectives  14.8 us (9%)
  local copies, waits for them, and re-layouts  8.48 us (5%)
    all_to_all x3, waiting for transfers between devices, exchange(): return lax.all_to_all(value, axis, 0, 0, tiled=True)  32.1 us
    pallas_call x1, Pallas kernels, per_device(): pl.pallas_call(functools.partial(prep_keys, PAIRS[0], heads, steps), grid...  23.3 us
    pallas_call x2, Pallas kernels, key_half(): pl.pallas_call(functools.partial(key_grads, pair, heads, index), grid=(st...  20 us
    all_to_all x1, blocking collectives, exchange(): return lax.all_to_all(value, axis, 0, 0, tiled=True)  14.8 us
    all_to_all x3, starting transfers between devices, exchange(): return lax.all_to_all(value, axis, 0, 0, tiled=True)  14.4 us
    pallas_call x1, Pallas kernels, per_device(): pl.pallas_call(functools.partial(query_grads, PAIRS[2], heads, steps), gr...  12.9 us
    ppermute x6, starting transfers between devices, from_chips_behind(): lax.ppermute(value, 'seq_0', [(i, (i + k) % chips) for i in range(chips)])  9.66 us
    pallas_call x1, Pallas kernels, per_device(): pl.pallas_call(functools.partial(prep_queries, PAIRS[1], heads, steps), g...  9.5 us
  transfers between devices with their start and end apart: 13, of which 7 were waited for; matrix products, arithmetic and copies ran while one was open for 1% of the time, Pallas kernels for 30%

profile of v3, /device:TPU:0, one launch (start us, length us, event | category | flops | bytes accessed | tf_op | source)
XLA Modules:
  0.0 172.6 jit_solution(18435298299761313481)
XLA Ops:
  1.2 23.3 %prep_keys.1 = (f32[8,4,128,128]{3,2,1,0:T(8,128)}, f32[8,4,128,128]{3,2,1,0:T(8,128)}, f32[8,4,128,128]{3,2,1,0:T(8,128)}, f32[8,4,128,128]{3,2,1,0:T(8,128)}, ...) custom-call(s32[2]{0:T(128)} %pad_add_fusion.place, ...), custom_call_target="tpu_custom_call" | custom-call | tf_op jit(solution)/shard_map/prep_keys/pallas_call | solution.py:468
  24.6 1.7 %collective-permute-done.other = f32[2,2,128,128]{3,2,1,0:T(8,128)S(1)} collective-permute-done((f32[2,2,128,128]{3,2,1,0:T(8,128)}, f32[2,2,128,128]{3,2,1,0:T(8,128)S(1)}, u32[]{:S(2)}, u32[]{:S(2)}) %collective-permute-start) | collective-permute-done | bytes 262176 | tf_op jit(solution)/shard_map/ppermute | solution.py:446
  26.4 0.7 copy-done
  27.1 2.1 %shard_map.85 = f32[2,2,128,128]{3,2,1,0:T(8,128)} custom-call(s32[2]{0:T(128)} %pad_add_fusion.place, f32[2,2,128,128]{3,2,1,0:T(8,128)} %get-tuple-element.26.mine, f32[2,2,128,128]{3,2,1,0:T(8,128)} %copy-done), custom_call_target="tpu_custom_call" | custom-call | tf_op jit(solution)/shard_map/pallas_call | solution.py:457
  29.1 4.1 %collective-permute-start.3 = (f32[2,2,128,128]{3,2,1,0:T(8,128)}, f32[2,2,128,128]{3,2,1,0:T(8,128)S(1)}, u32[]{:S(2)}, u32[]{:S(2)}) collective-permute-start(f32[2,2,128,128]{3,2,1,0:T(8,128)} %shard_map.85), channel_id=1, source_target_pairs={{0,96},{32,0},{64,32},{96,64},{1,97},{33,1},{65,33},{97,65},{2,98}... | collective-permute-start | bytes 786440 | tf_op jit(solution)/shard_map/ppermute | solution.py:452
  33.3 1.3 collective-permute-start.1
  34.6 2.6 %square_sums.1 = f32[16,8,128]{2,1,0:T(8,128)} custom-call(bf16[1024,512]{1,0:T(8,128)(2,1)} %query.11), custom_call_target="tpu_custom_call" | custom-call | tf_op jit(solution)/shard_map/square_sums/pallas_call | solution.py:464
  37.2 14.8 %all_to_all.20.sums = f32[16,8,128]{2,1,0:T(8,128)} all-to-all(f32[16,8,128]{2,1,0:T(8,128)} %square_sums.1), channel_id=1, replica_groups=mesh['seq_0'=4,'seq_1'=2,'head_0'=4,'head_1'=4] {'head_0','head_1'}, dimensions={0} | all-to-all | bytes 131072 | tf_op jit(solution)/shard_map/all_to_all | solution.py:427
  52.0 9.5 %prep_queries.1 = (f32[8,4,128,128]{3,2,1,0:T(8,128)}, f32[8,4,128,128]{3,2,1,0:T(8,128)}, f32[1024,128]{1,0:T(8,128)}, f32[8,8,128]{2,1,0:T(8,128)}, f32[2,128,128]{2,1,0:T(8,128)}, /*index=5*/f32[2,128,128]{2,1,0:T(8,128)}) custom-call(s32[2]{0:T(128)} %pad_add_fusion.place, bf16[1024,512]{1,0:T(8,128)(2,1)} %query.11, bf16[1024,512]{1,0:T(8,128)(2,1)} %key.9, ...), custom_call_target="tpu_custom_call" | custom-call | tf_op jit(solution)/shard_map/prep_queries/pallas_call | solution.py:481
  61.6 1.5 collective-permute-done.4.other_back
  64.0 3.6 %shard_map.86 = (f32[2,128,128]{2,1,0:T(8,128)}, f32[2,128,128]{2,1,0:T(8,128)}, f32[2,128,128]{2,1,0:T(8,128)}) custom-call(s32[2]{0:T(128)} %pad_add_fusion.place, f32[2,2,128,128]{3,2,1,0:T(8,128)} %get-tuple-element.26.mine, f32[2,2,128,128]{3,2,1,0:T(8,128)} %copy-done, f32[2,2,128,128]{3,2,1,0:T(8,128)} %copy-done.5, f32[2,2,128,128]{3,2,1,0:T(8,128)} %copy-done.4, ...), custom_call_target="tpu_custom_call" | custom-call | tf_op jit(solution)/shard_map/pallas_call | solution.py:457
  67.6 2.0 %collective-permute-start.8 = (f32[2,128,128]{2,1,0:T(8,128)}, f32[2,128,128]{2,1,0:T(8,128)S(1)}, u32[]{:S(2)}, u32[]{:S(2)}) collective-permute-start(f32[2,128,128]{2,1,0:T(8,128)} %get-tuple-element.41), channel_id=1, source_target_pairs={{0,96},{32,0},{64,32},{96,64},{1,97},{33,1},{65,33},{97,65},{2,98}... | collective-permute-start | bytes 393224 | tf_op jit(solution)/shard_map/ppermute | solution.py:452
  69.6 2.3 %collective-permute-start.7 = (f32[2,128,128]{2,1,0:T(8,128)}, f32[2,128,128]{2,1,0:T(8,128)S(1)}, u32[]{:S(2)}, u32[]{:S(2)}) collective-permute-start(f32[2,128,128]{2,1,0:T(8,128)} %get-tuple-element.41), channel_id=1, source_target_pairs={{0,64},{32,96},{64,0},{96,32},{1,65},{33,97},{65,1},{97,33},{2,66}... | collective-permute-start | bytes 393224 | tf_op jit(solution)/shard_map/ppermute | solution.py:452
  71.9 2.5 %collective-permute-done.8.three_back = f32[2,128,128]{2,1,0:T(8,128)S(1)} collective-permute-done((f32[2,128,128]{2,1,0:T(8,128)}, f32[2,128,128]{2,1,0:T(8,128)S(1)}, u32[]{:S(2)}, u32[]{:S(2)}) %collective-permute-start.8) | collective-permute-done | bytes 131104 | tf_op jit(solution)/shard_map/ppermute | solution.py:452
  74.4 3.3 %collective-permute-done.7.two_back = f32[2,128,128]{2,1,0:T(8,128)S(1)} collective-permute-done((f32[2,128,128]{2,1,0:T(8,128)}, f32[2,128,128]{2,1,0:T(8,128)S(1)}, u32[]{:S(2)}, u32[]{:S(2)}) %collective-permute-start.7) | collective-permute-done | bytes 131104 | tf_op jit(solution)/shard_map/ppermute | solution.py:452
  77.7 1.7 collective-permute-done.6.one_back
  79.4 0.7 copy-done.12
  80.1 3.2 %shard_map.87 = (f32[2,128,128]{2,1,0:T(8,128)}, f32[2,128,128]{2,1,0:T(8,128)}) custom-call(s32[2]{0:T(128)} %pad_add_fusion.place, f32[2,2,128,128]{3,2,1,0:T(8,128)} %get-tuple-element.26.mine, f32[2,2,128,128]{3,2,1,0:T(8,128)} %copy-done, f32[2,2,128,128]{3,2,1,0:T(8,128)} %copy-done.5, f32[2,2,128,128]{3,2,1,0:T(8,128)} %copy-done.4, ...), custom_call_target="tpu_custom_call" | custom-call | tf_op jit(solution)/shard_map/pallas_call | solution.py:457
  84.0 12.9 %query_grads.1 = (f32[1024,512]{1,0:T(8,128)}, f32[8,4,128,128]{3,2,1,0:T(8,128)}, f32[8,4,128,128]{3,2,1,0:T(8,128)}, f32[16,8,128]{2,1,0:T(8,128)}) custom-call(s32[2]{0:T(128)} %pad_add_fusion.place, bf16[1024,512]{1,0:T(8,128)(2,1)} %query.11, bf16[1024,512]{1,0:T(8,128)(2,1)} %key.9, bf16[1024,512]{1,0:T(8,128)(2,1)} %value.3, bf16[1024,512]{1,0:T(8,128)(2,1)} %grad.7, ...), custom_call_target="tpu_custom_call" | custom-call | tf_op jit(solution)/shard_map/query_grads/pallas_call | solution.py:502
  96.8 3.5 %all-to-all-start.1 = ((f32[16,8,128]{2,1,0:T(8,128)}), f32[16,8,128]{2,1,0:T(8,128)S(1)}, u32[]{:S(2)}, u32[]{:S(2)}) async-start(f32[16,8,128]{2,1,0:T(8,128)} %get-tuple-element.40.ready), calls=%async_computation.1 | async-start | bytes 131072 | tf_op jit(solution)/shard_map/all_to_all | solution.py:427
  100.3 0.6 copy-done.6
  101.0 10.0 %shard_map.88.ready = bf16[1024,512]{1,0:T(8,128)(2,1)} custom-call(s32[2]{0:T(128)} %pad_add_fusion.place, bf16[1024,512]{1,0:T(8,128)(2,1)} %query.11, bf16[1024,512]{1,0:T(8,128)(2,1)} %key.9, bf16[1024,512]{1,0:T(8,128)(2,1)} %grad.7, f32[1,512]{1,0:T(1,128)} %bitcast.24, f32[2,128,128]{2,1,0:T(8,128)} %get-tuple-element.42.mine, ...), custom_call_target="tpu_custom_call" | custom-call | tf_op jit(solution)/shard_map/pallas_call | solution.py:531
  111.0 7.2 %all-to-all-start.3 = ((bf16[16,64,512]{2,1,0:T(8,128)(2,1)}), bf16[16,64,512]{2,1,0:T(8,128)(2,1)S(1)}, u32[]{:S(2)}, u32[]{:S(2)}) async-start(bf16[16,64,512]{2,1,0:T(8,128)(2,1)} %bitcast.18), calls=%async_computation.3 | async-start | bytes 2097152 | tf_op jit(solution)/shard_map/all_to_all | solution.py:427
  118.2 10.0 %shard_map.89.others = bf16[1024,1024]{1,0:T(8,128)(2,1)} custom-call(s32[2]{0:T(128)} %pad_add_fusion.place, bf16[1024,512]{1,0:T(8,128)(2,1)} %query.11, bf16[1024,512]{1,0:T(8,128)(2,1)} %key.9, bf16[1024,512]{1,0:T(8,128)(2,1)} %grad.7, f32[1,512]{1,0:T(1,128)} %bitcast.25, f32[2,128,128]{2,1,0:T(8,128)} %get-tuple-element.42.mine, ...), custom_call_target="tpu_custom_call" | custom-call | tf_op jit(solution)/shard_map/pallas_call | solution.py:531
  128.2 3.5 %finish_queries.1 = bf16[1024,1024]{1,0:T(8,128)(2,1)} custom-call(bf16[1024,512]{1,0:T(8,128)(2,1)} %query.11, f32[1024,512]{1,0:T(8,128)} %get-tuple-element.39.scaled, f32[1024,128]{1,0:T(8,128)} %get-tuple-element.38.norm_cols, f32[16,8,128]{2,1,0:T(8,128)} %copy-done.8, bf16[1024,1024]{1,0:T(8,128)(2,1)} %shard_map.89.others), custom_call_target="tpu_custom_call", output_to_operand_aliasing={{}: (4, {})} | custom-call | tf_op jit(solution)/shard_map/finish_queries/pallas_call | solution.py:557
  131.7 4.7 %all-to-all-done.3 = bf16[16,64,512]{2,1,0:T(8,128)(2,1)S(1)} async-done(((bf16[16,64,512]{2,1,0:T(8,128)(2,1)}), bf16[16,64,512]{2,1,0:T(8,128)(2,1)S(1)}, u32[]{:S(2)}, u32[]{:S(2)}) %all-to-all-start.3) | async-done | bytes 1048608 | tf_op jit(solution)/shard_map/all_to_all | solution.py:427
  136.4 3.7 %all-to-all-start.2 = ((bf16[16,64,1024]{2,1,0:T(8,128)(2,1)}), bf16[16,64,1024]{2,1,0:T(8,128)(2,1)S(1)}, u32[]{:S(2)}, u32[]{:S(2)}) async-start(bf16[16,64,1024]{2,1,0:T(8,128)(2,1)} %bitcast.17), calls=%async_computation.2 | async-start | bytes 4194304 | tf_op jit(solution)/shard_map/all_to_all | solution.py:427
  140.1 1.1 fusion.1
  141.2 27.4 %all-to-all-done.2 = bf16[16,64,1024]{2,1,0:T(8,128)(2,1)S(1)} async-done(((bf16[16,64,1024]{2,1,0:T(8,128)(2,1)}), bf16[16,64,1024]{2,1,0:T(8,128)(2,1)S(1)}, u32[]{:S(2)}, u32[]{:S(2)}) %all-to-all-start.2) | async-done | bytes 2097184 | tf_op jit(solution)/shard_map/all_to_all | solution.py:427
  168.7 1.1 copy.13
  170.5 1.1 copy.14
  171.6 1.1 copy.15
  (39 shorter events, 3.1 us)
Async XLA Ops:
  24.5 1.8 %collective-permute-start = (f32[2,2,128,128]{3,2,1,0:T(8,128)}, f32[2,2,128,128]{3,2,1,0:T(8,128)S(1)}, u32[]{:S(2)}, u32[]{:S(2)}) collective-permute-start(f32[2,2,128,128]{3,2,1,0:T(8,128)} %get-tuple-element.27), channel_id=1, source_target_pairs={{0,16},{16,0},{1,17},{17,1},{2,18},{18,2},{3,19},{19,3},{4,20},{20... | collective-permute-start | bytes 786440 | tf_op jit(solution)/shard_map/ppermute | solution.py:446
  26.4 0.7 copy-start
  29.1 34.0 %collective-permute-start.3 = (f32[2,2,128,128]{3,2,1,0:T(8,128)}, f32[2,2,128,128]{3,2,1,0:T(8,128)S(1)}, u32[]{:S(2)}, u32[]{:S(2)}) collective-permute-start(f32[2,2,128,128]{3,2,1,0:T(8,128)} %shard_map.85), channel_id=1, source_target_pairs={{0,96},{32,0},{64,32},{96,64},{1,97},{33,1},{65,33},{97,65},{2,98}... | collective-permute-start | bytes 786440 | tf_op jit(solution)/shard_map/ppermute | solution.py:452
  33.3 29.8 %collective-permute-start.2 = (f32[2,2,128,128]{3,2,1,0:T(8,128)}, f32[2,2,128,128]{3,2,1,0:T(8,128)S(1)}, u32[]{:S(2)}, u32[]{:S(2)}) collective-permute-start(f32[2,2,128,128]{3,2,1,0:T(8,128)} %shard_map.85), channel_id=1, source_target_pairs={{0,64},{32,96},{64,0},{96,32},{1,65},{33,97},{65,1},{97,33},{2,66}... | collective-permute-start | bytes 786440 | tf_op jit(solution)/shard_map/ppermute | solution.py:452
  33.3 29.8 %collective-permute-start.1 = (f32[2,2,128,128]{3,2,1,0:T(8,128)}, f32[2,2,128,128]{3,2,1,0:T(8,128)S(1)}, u32[]{:S(2)}, u32[]{:S(2)}) collective-permute-start(f32[2,2,128,128]{3,2,1,0:T(8,128)} %shard_map.85), channel_id=1, source_target_pairs={{0,32},{32,64},{64,96},{96,0},{1,33},{33,65},{65,97},{97,1},{2,34}... | collective-permute-start | bytes 786440 | tf_op jit(solution)/shard_map/ppermute | solution.py:452
  61.5 1.6 collective-permute-start.4
  63.1 0.7 copy-start.7
  63.1 0.7 copy-start.3
  63.1 0.9 copy-start.4
  63.1 0.9 copy-start.5
  67.6 6.7 %collective-permute-start.8 = (f32[2,128,128]{2,1,0:T(8,128)}, f32[2,128,128]{2,1,0:T(8,128)S(1)}, u32[]{:S(2)}, u32[]{:S(2)}) collective-permute-start(f32[2,128,128]{2,1,0:T(8,128)} %get-tuple-element.41), channel_id=1, source_target_pairs={{0,96},{32,0},{64,32},{96,64},{1,97},{33,1},{65,33},{97,65},{2,98}... | collective-permute-start | bytes 393224 | tf_op jit(solution)/shard_map/ppermute | solution.py:452
  69.6 8.1 %collective-permute-start.7 = (f32[2,128,128]{2,1,0:T(8,128)}, f32[2,128,128]{2,1,0:T(8,128)S(1)}, u32[]{:S(2)}, u32[]{:S(2)}) collective-permute-start(f32[2,128,128]{2,1,0:T(8,128)} %get-tuple-element.41), channel_id=1, source_target_pairs={{0,64},{32,96},{64,0},{96,32},{1,65},{33,97},{65,1},{97,33},{2,66}... | collective-permute-start | bytes 393224 | tf_op jit(solution)/shard_map/ppermute | solution.py:452
  71.9 7.5 %collective-permute-start.6 = (f32[2,128,128]{2,1,0:T(8,128)}, f32[2,128,128]{2,1,0:T(8,128)S(1)}, u32[]{:S(2)}, u32[]{:S(2)}) collective-permute-start(f32[2,128,128]{2,1,0:T(8,128)} %get-tuple-element.41), channel_id=1, source_target_pairs={{0,32},{32,64},{64,96},{96,0},{1,33},{33,65},{65,97},{97,1},{2,34}... | collective-permute-start | bytes 393224 | tf_op jit(solution)/shard_map/ppermute | solution.py:452
  71.9 11.4 %collective-permute-start.5 = (f32[2,128,128]{2,1,0:T(8,128)}, f32[2,128,128]{2,1,0:T(8,128)S(1)}, u32[]{:S(2)}, u32[]{:S(2)}) collective-permute-start(f32[2,128,128]{2,1,0:T(8,128)} %get-tuple-element.35), channel_id=1, source_target_pairs={{0,16},{16,0},{1,17},{17,1},{2,18},{18,2},{3,19},{19,3},{4,20},{20... | collective-permute-start | bytes 393224 | tf_op jit(solution)/shard_map/ppermute | solution.py:446
  74.4 5.0 %copy-start.10 = (f32[2,128,128]{2,1,0:T(8,128)}, f32[2,128,128]{2,1,0:T(8,128)S(1)}, u32[]{:S(2)}) copy-start(f32[2,128,128]{2,1,0:T(8,128)S(1)} %collective-permute-done.8.three_back) | copy-start | bytes 393220
  77.7 1.7 copy-start.11
  79.4 0.7 copy-start.12
  83.3 17.0 %collective-permute-start.9 = (f32[2,128,128]{2,1,0:T(8,128)}, f32[2,128,128]{2,1,0:T(8,128)S(1)}, u32[]{:S(2)}, u32[]{:S(2)}) collective-permute-start(f32[2,128,128]{2,1,0:T(8,128)} %get-tuple-element.43), channel_id=1, source_target_pairs={{0,16},{16,0},{1,17},{17,1},{2,18},{18,2},{3,19},{19,3},{4,20},{20... | collective-permute-start | bytes 393224 | tf_op jit(solution)/shard_map/ppermute | solution.py:446
  83.3 0.7 copy-start.9
  96.8 14.2 %all-to-all-start.1 = ((f32[16,8,128]{2,1,0:T(8,128)}), f32[16,8,128]{2,1,0:T(8,128)S(1)}, u32[]{:S(2)}, u32[]{:S(2)}) async-start(f32[16,8,128]{2,1,0:T(8,128)} %get-tuple-element.40.ready), calls=%async_computation.1 | async-start | bytes 131072 | tf_op jit(solution)/shard_map/all_to_all | solution.py:427
  100.3 0.7 copy-start.6
  111.0 17.2 %copy-start.8 = (f32[16,8,128]{2,1,0:T(8,128)}, f32[16,8,128]{2,1,0:T(8,128)S(1)}, u32[]{:S(2)}) copy-start(f32[16,8,128]{2,1,0:T(8,128)S(1)} %all-to-all-done.1.sums) | copy-start | bytes 196612
  111.0 25.4 %all-to-all-start.3 = ((bf16[16,64,512]{2,1,0:T(8,128)(2,1)}), bf16[16,64,512]{2,1,0:T(8,128)(2,1)S(1)}, u32[]{:S(2)}, u32[]{:S(2)}) async-start(bf16[16,64,512]{2,1,0:T(8,128)(2,1)} %bitcast.18), calls=%async_computation.3 | async-start | bytes 2097152 | tf_op jit(solution)/shard_map/all_to_all | solution.py:427
  136.4 32.2 %all-to-all-start.2 = ((bf16[16,64,1024]{2,1,0:T(8,128)(2,1)}), bf16[16,64,1024]{2,1,0:T(8,128)(2,1)S(1)}, u32[]{:S(2)}, u32[]{:S(2)}) async-start(bf16[16,64,1024]{2,1,0:T(8,128)(2,1)} %bitcast.17), calls=%async_computation.2 | async-start | bytes 4194304 | tf_op jit(solution)/shard_map/all_to_all | solution.py:427
  168.7 1.2 copy-start.1
  168.7 1.6 copy-start.2

commit v4 on v3

--- a/solution.py
+++ b/solution.py
@@ -11,7 +11,7 @@
 
 D = 8192
 C = 128
-PAIRS = (2, 2, 2, 4, 4)
+PAIRS = (4, 2, 2, 4, 2)
 HEAD = ("head_0", "head_1")
 SEQ = ("seq_0", "seq_1")
 SEQ_HEAD = ("seq_0", "seq_1", "head_0", "head_1")
@@ -36,7 +36,16 @@
 
 
 def mul3(form, a, b):
-    return form(a[0], b[0]) + (form(a[0], b[1]) + form(a[1], b[0]))
+    left = jnp.concatenate(a, axis=1)
+    blank = jnp.zeros_like(b[1])
+    if form is nn:
+        upper = jnp.concatenate([b[0], b[1]], axis=1)
+        lower = jnp.concatenate([b[0], blank], axis=1)
+    else:
+        upper = jnp.concatenate([b[0], b[0]], axis=1)
+        lower = jnp.concatenate([b[1], blank], axis=1)
+    both = form(left, jnp.concatenate([upper, lower], axis=0))
+    return both[:, :C] + both[:, C:]
 
 
 def mul_left(form, a, b):
@@ -323,7 +332,7 @@
         part[...] = jnp.broadcast_to(sums_so_far[...][None], part.shape)
 
 
-def finish_queries(pair, query, scaled, norm_cols, sums, others, out, corrections):
+def finish_queries(pair, query, scaled, norm_cols, sums, out, corrections):
     step = pl.program_id(0)
 
     @pl.when(step == 0)
@@ -339,29 +348,29 @@
         out[part] = (norm * scaled[part] - query[part].astype(f32) * factor).astype(bf16)
 
 
-def key_grads(pair, heads, part, place, query, key, grad, gain, mine, other, inv, trans, adjoint, inner, fresh, starts, cols, rows, norm_rows, ready, out, state):
+def key_grads(pair, heads, place, query, key, grad, gain, mine, other, inv, trans, adjoint, inner, fresh, starts, cols, rows, norm_rows, ready, out, state):
     step = pl.program_id(0)
-    taken = heads // 2
-    begin = part * taken
-    units = all_units(pair, taken)
+    units = all_units(pair, heads)
     count = len(units)
     row, col = iotas()
-    width = taken * C
+    width = heads * C
 
     @pl.when(step == 0)
     def _():
-        own = place[1] == part
-        for h in range(taken):
-            state[h] = jnp.where(own, mine[h], other[h])
+        half = heads // 2
+        first = place[1] * half
+        for j in range(half):
+            state[first + j] = mine[j]
+            state[half - first + j] = other[j]
 
     ends = [None] * count
     for b in reversed(range(pair)):
-        for h in range(taken):
-            u = b * taken + h
+        for h in range(heads):
+            u = b * heads + h
             ends[u] = halves(state[h])
             state[h] = mul3(nn, ends[u], halves(trans[b, h])) + adjoint[b, h]
-    g_row = [rows[b, begin + h : begin + h + 1] for b, h in units]
-    s_row = [rows[b, heads + begin + h : heads + begin + h + 1] for b, h in units]
+    g_row = [rows[b, h : h + 1] for b, h in units]
+    s_row = [rows[b, heads + h : heads + h + 1] for b, h in units]
     keys = [tile(key, b, h) for b, h in units]
     amounts = [halves(fresh[b, h]) for b, h in units]
     turned = []
@@ -376,8 +385,8 @@
     across = [mul_left(nt, amounts[u], tile(grad, b, h)) for u, (b, h) in enumerate(units)]
     for u, (b, h) in enumerate(units):
         here = cols[b * C : (b + 1) * C]
-        g_col = here[:, begin + h : begin + h + 1]
-        s_col = here[:, heads + begin + h : heads + begin + h + 1]
+        g_col = here[:, h : h + 1]
+        s_col = here[:, heads + h : heads + h + 1]
         n_row = norm_rows[b, :1]
         below = jnp.exp(jnp.where(row > col, g_col - g_row[u], 0.0))
         pulled = jnp.where(row > col, -2.0 * below * against[u], 0.0)
@@ -523,62 +532,44 @@
     )
     arrived = to_other_core(leave)
 
-    def key_half(index, out_shape, at, ready):
-        pair = PAIRS[4]
-        steps, _, _, column, line = specs(pair, reverse=True)
-        tokens = pl.BlockSpec((pair * C, some * C), lambda i: (steps - 1 - i, index))
-        matrix = pl.BlockSpec((pair, some, C, C), lambda i: (steps - 1 - i, index, 0, 0))
-        return pl.pallas_call(
-            functools.partial(key_grads, pair, heads, index),
-            grid=(steps,),
-            in_specs=[scalar]
-            + [tokens] * 3
-            + [pl.BlockSpec((1, some * C), lambda i: (0, index))]
-            + [fixed(some, C, C)] * 2
-            + [matrix] * 6
-            + [column, line, line, pl.BlockSpec(memory_space=pl.ANY)],
-            out_specs=pl.BlockSpec((pair * C, 2 * some * C), lambda i: (steps - 1 - i, at)),
-            out_shape=shape((rows, out_shape), bf16),
-            scratch_shapes=[pltpu.VMEM((some, C, C), f32)],
-        )(
-            place, query_raw, key_raw, out_grad, gain, stay, arrived,
-            inv, trans, adjoint, inner, fresh, starts, cols, row_info, norm_rows, ready,
-        )
-
     def owned(array):
         return exchange(array.reshape(group, rows // group, array.shape[1]), HEAD)
 
-    first_half = key_half(0, width, 0, part)
-    first = owned(first_half)
-    second_half = key_half(1, 2 * width, 1, first_half)
-
     steps, tokens, matrix, column, line = specs(PAIRS[3])
-    second = owned(
-        pl.pallas_call(
-            functools.partial(finish_queries, PAIRS[3]),
-            grid=(steps,),
-            in_specs=[
-                tokens, tokens, column, fixed(group, blocks, C),
-                pl.BlockSpec(memory_space=pl.ANY),
-            ],
-            out_specs=tokens,
-            out_shape=shape((rows, 2 * width), bf16),
-            input_output_aliases={4: 0},
-            scratch_shapes=[line_scratch],
-            name="finish_queries",
-        )(query_raw, scaled, norm_cols, corrections, second_half),
-    )
-
-    def lay(*pieces):
-        whole = pieces[0] if len(pieces) == 1 else jnp.concatenate(pieces, axis=2)
-        return whole.transpose(1, 0, 2).reshape(rows // group, group * width)
-
-    side = some * C
-    return (
-        lay(second[:, :, :width]),
-        lay(first[:, :, :side], second[:, :, width : width + side]),
-        lay(first[:, :, side:], second[:, :, width + side :]),
-    )
+    query_raw_grad = pl.pallas_call(
+        functools.partial(finish_queries, PAIRS[3]),
+        grid=(steps,),
+        in_specs=[tokens, tokens, column, fixed(group, blocks, C)],
+        out_specs=tokens,
+        out_shape=shape((rows, width), bf16),
+        scratch_shapes=[line_scratch],
+        name="finish_queries",
+    )(query_raw, scaled, norm_cols, corrections)
+    first = owned(query_raw_grad)
+
+    steps, tokens, matrix, column, line = specs(PAIRS[4], reverse=True)
+    key_value = pl.pallas_call(
+        functools.partial(key_grads, PAIRS[4], heads),
+        grid=(steps,),
+        in_specs=[scalar]
+        + [tokens] * 3
+        + [fixed(1, width), fixed(some, C, C), fixed(some, C, C)]
+        + [matrix] * 6
+        + [column, line, line, pl.BlockSpec(memory_space=pl.ANY)],
+        out_specs=pl.BlockSpec((PAIRS[4] * C, 2 * width), lambda i: (steps - 1 - i, 0)),
+        out_shape=shape((rows, 2 * width), bf16),
+        scratch_shapes=[carry],
+        name="key_grads",
+    )(
+        place, query_raw, key_raw, out_grad, gain, stay, arrived,
+        inv, trans, adjoint, inner, fresh, starts, cols, row_info, norm_rows, query_raw_grad,
+    )
+    second = owned(key_value)
+
+    def lay(pieces):
+        return pieces.transpose(1, 0, 2).reshape(rows // group, group * width)
+
+    return lay(first), lay(second[:, :, :width]), lay(second[:, :, width:])
 
 
 def solution(mesh):

time: 173 us -> 169 us (0.977)
  blocking collectives: 14.8 us -> 26.6 us
  Pallas kernels: 80.6 us -> 69.8 us
  starting transfers between devices: 24.2 us -> 20.9 us
    all_to_all x1 -> x2, blocking collectives: 14.8 us -> 26.6 us  [exchange(): return lax.all_to_all(value, axis, 0, 0, tiled=True)]
    pallas_call x2 -> x1, Pallas kernels: 20 us -> 15.4 us  [per_device(): pl.pallas_call(functools.partial(key_grads, PAIRS[4], heads), grid=(steps...]
    pallas_call x1, Pallas kernels: 23.3 us -> 19.2 us  [per_device(): pl.pallas_call(functools.partial(prep_keys, PAIRS[0], heads, steps), grid...]
    all_to_all x3 -> x2, starting transfers between devices: 14.4 us -> 10.7 us  [exchange(): return lax.all_to_all(value, axis, 0, 0, tiled=True)]
    ppermute x4, waiting for transfers between devices: 3.28 us -> 6.25 us  [to_other_core(): return lax.ppermute(value, 'seq_1', [(0, 1), (1, 0)])]
    all_to_all x3 -> x2, waiting for transfers between devices: 32.1 us -> 30.1 us  [exchange(): return lax.all_to_all(value, axis, 0, 0, tiled=True)]
    unnamed x27 -> x23, local copies, waits for them, and re-layouts: 4.05 us -> 3.85 us
  transfers between devices with their start and end apart: 13 -> 12, of which waited for: 7 -> 8; matrix products, arithmetic and copies ran while one was open for 1% -> 1% of each run, Pallas kernels for 30% -> 18%
where the time goes in v4:
time: 169 us
  Pallas kernels  69.8 us (41%)
  waiting for transfers between devices  42.8 us (25%)
  blocking collectives  26.6 us (16%)
  starting transfers between devices  20.9 us (12%)
  local copies, waits for them, and re-layouts  7.07 us (4%)
    all_to_all x2, waiting for transfers between devices, exchange(): return lax.all_to_all(value, axis, 0, 0, tiled=True)  30.1 us
    all_to_all x2, blocking collectives, exchange(): return lax.all_to_all(value, axis, 0, 0, tiled=True)  26.6 us
    pallas_call x1, Pallas kernels, per_device(): pl.pallas_call(functools.partial(prep_keys, PAIRS[0], heads, steps), grid...  19.2 us
    pallas_call x1, Pallas kernels, per_device(): pl.pallas_call(functools.partial(key_grads, PAIRS[4], heads), grid=(steps...  15.4 us
    pallas_call x1, Pallas kernels, per_device(): pl.pallas_call(functools.partial(query_grads, PAIRS[2], heads, steps), gr...  11.7 us
    all_to_all x2, starting transfers between devices, exchange(): return lax.all_to_all(value, axis, 0, 0, tiled=True)  10.7 us
    ppermute x6, starting transfers between devices, from_chips_behind(): lax.ppermute(value, 'seq_0', [(i, (i + k) % chips) for i in range(chips)])  9.77 us
    pallas_call x1, Pallas kernels, per_device(): pl.pallas_call(functools.partial(prep_queries, PAIRS[1], heads, steps), g...  9.28 us
  transfers between devices with their start and end apart: 12, of which 8 were waited for; matrix products, arithmetic and copies ran while one was open for 1% of the time, Pallas kernels for 18%

profile of v4, /device:TPU:0, one launch (start us, length us, event | category | flops | bytes accessed | tf_op | source)
XLA Modules:
  0.0 168.6 jit_solution(8445332073357897493)
XLA Ops:
  0.6 0.6 pad_add_fusion.place
  1.3 19.2 %prep_keys.1 = (f32[8,4,128,128]{3,2,1,0:T(8,128)}, f32[8,4,128,128]{3,2,1,0:T(8,128)}, f32[8,4,128,128]{3,2,1,0:T(8,128)}, f32[8,4,128,128]{3,2,1,0:T(8,128)}, ...) custom-call(s32[2]{0:T(128)} %pad_add_fusion.place, ...), custom_call_target="tpu_custom_call" | custom-call | tf_op jit(solution)/shard_map/prep_keys/pallas_call | solution.py:477
  20.6 1.7 %collective-permute-done.other = f32[2,2,128,128]{3,2,1,0:T(8,128)S(1)} collective-permute-done((f32[2,2,128,128]{3,2,1,0:T(8,128)}, f32[2,2,128,128]{3,2,1,0:T(8,128)S(1)}, u32[]{:S(2)}, u32[]{:S(2)}) %collective-permute-start) | collective-permute-done | bytes 262176 | tf_op jit(solution)/shard_map/ppermute | solution.py:455
  22.3 0.7 copy-done
  23.0 2.0 %shard_map.85 = f32[2,2,128,128]{3,2,1,0:T(8,128)} custom-call(s32[2]{0:T(128)} %pad_add_fusion.place, f32[2,2,128,128]{3,2,1,0:T(8,128)} %get-tuple-element.26.mine, f32[2,2,128,128]{3,2,1,0:T(8,128)} %copy-done), custom_call_target="tpu_custom_call" | custom-call | tf_op jit(solution)/shard_map/pallas_call | solution.py:466
  25.1 4.2 %collective-permute-start.3 = (f32[2,2,128,128]{3,2,1,0:T(8,128)}, f32[2,2,128,128]{3,2,1,0:T(8,128)S(1)}, u32[]{:S(2)}, u32[]{:S(2)}) collective-permute-start(f32[2,2,128,128]{3,2,1,0:T(8,128)} %shard_map.85), channel_id=1, source_target_pairs={{0,96},{32,0},{64,32},{96,64},{1,97},{33,1},{65,33},{97,65},{2,98}... | collective-permute-start | bytes 786440 | tf_op jit(solution)/shard_map/ppermute | solution.py:461
  29.2 1.3 collective-permute-start.1
  30.5 2.6 %square_sums.1 = f32[16,8,128]{2,1,0:T(8,128)} custom-call(bf16[1024,512]{1,0:T(8,128)(2,1)} %query.9), custom_call_target="tpu_custom_call" | custom-call | tf_op jit(solution)/shard_map/square_sums/pallas_call | solution.py:473
  33.1 14.8 %all_to_all.20.sums = f32[16,8,128]{2,1,0:T(8,128)} all-to-all(f32[16,8,128]{2,1,0:T(8,128)} %square_sums.1), channel_id=1, replica_groups=mesh['seq_0'=4,'seq_1'=2,'head_0'=4,'head_1'=4] {'head_0','head_1'}, dimensions={0} | all-to-all | bytes 131072 | tf_op jit(solution)/shard_map/all_to_all | solution.py:436
  47.9 9.3 %prep_queries.1 = (f32[8,4,128,128]{3,2,1,0:T(8,128)}, f32[8,4,128,128]{3,2,1,0:T(8,128)}, f32[1024,128]{1,0:T(8,128)}, f32[8,8,128]{2,1,0:T(8,128)}, f32[2,128,128]{2,1,0:T(8,128)}, /*index=5*/f32[2,128,128]{2,1,0:T(8,128)}) custom-call(s32[2]{0:T(128)} %pad_add_fusion.place, bf16[1024,512]{1,0:T(8,128)(2,1)} %query.9, bf16[1024,512]{1,0:T(8,128)(2,1)} %key.7, ...), custom_call_target="tpu_custom_call" | custom-call | tf_op jit(solution)/shard_map/prep_queries/pallas_call | solution.py:490
  57.4 1.5 collective-permute-done.4.other_back
  59.9 3.1 %shard_map.86 = (f32[2,128,128]{2,1,0:T(8,128)}, f32[2,128,128]{2,1,0:T(8,128)}, f32[2,128,128]{2,1,0:T(8,128)}) custom-call(s32[2]{0:T(128)} %pad_add_fusion.place, f32[2,2,128,128]{3,2,1,0:T(8,128)} %get-tuple-element.26.mine, f32[2,2,128,128]{3,2,1,0:T(8,128)} %copy-done, f32[2,2,128,128]{3,2,1,0:T(8,128)} %copy-done.3, f32[2,2,128,128]{3,2,1,0:T(8,128)} %copy-done.2, ...), custom_call_target="tpu_custom_call" | custom-call | tf_op jit(solution)/shard_map/pallas_call | solution.py:466
  63.2 1.4 collective-permute-done.5.other
  65.2 11.7 %query_grads.1 = (f32[1024,512]{1,0:T(8,128)}, f32[8,4,128,128]{3,2,1,0:T(8,128)}, f32[8,4,128,128]{3,2,1,0:T(8,128)}, f32[16,8,128]{2,1,0:T(8,128)}) custom-call(s32[2]{0:T(128)} %pad_add_fusion.place, bf16[1024,512]{1,0:T(8,128)(2,1)} %query.9, bf16[1024,512]{1,0:T(8,128)(2,1)} %key.7, bf16[1024,512]{1,0:T(8,128)(2,1)} %value.3, bf16[1024,512]{1,0:T(8,128)(2,1)} %grad.5, ...), custom_call_target="tpu_custom_call" | custom-call | tf_op jit(solution)/shard_map/query_grads/pallas_call | solution.py:511
  76.9 11.8 %all_to_all.21.sums = f32[16,8,128]{2,1,0:T(8,128)} all-to-all(f32[16,8,128]{2,1,0:T(8,128)} %get-tuple-element.40), channel_id=1, replica_groups=mesh['seq_0'=4,'seq_1'=2,'head_0'=4,'head_1'=4] {'head_0','head_1'}, dimensions={0} | all-to-all | bytes 131072 | tf_op jit(solution)/shard_map/all_to_all | solution.py:436
  88.7 3.4 %finish_queries.1.ready = bf16[1024,512]{1,0:T(8,128)(2,1)} custom-call(bf16[1024,512]{1,0:T(8,128)(2,1)} %query.9, f32[1024,512]{1,0:T(8,128)} %get-tuple-element.39.scaled, f32[1024,128]{1,0:T(8,128)} %get-tuple-element.38.norm_cols, f32[16,8,128]{2,1,0:T(8,128)} %all_to_all.21.sums), custom_call_target="tpu_custom_call" | custom-call | tf_op jit(solution)/shard_map/finish_queries/pallas_call | solution.py:539
  92.1 3.8 %all-to-all-start.2 = ((bf16[16,64,512]{2,1,0:T(8,128)(2,1)}), bf16[16,64,512]{2,1,0:T(8,128)(2,1)S(1)}, u32[]{:S(2)}, u32[]{:S(2)}) async-start(bf16[16,64,512]{2,1,0:T(8,128)(2,1)} %bitcast.16), calls=%async_computation.2 | async-start | bytes 2097152 | tf_op jit(solution)/shard_map/all_to_all | solution.py:436
  95.9 2.0 %collective-permute-start.8 = (f32[2,128,128]{2,1,0:T(8,128)S(1)}, f32[2,128,128]{2,1,0:T(8,128)S(1)}, u32[]{:S(2)}, u32[]{:S(2)}) collective-permute-start(f32[2,128,128]{2,1,0:T(8,128)S(1)} %copy-done.10), channel_id=1, source_target_pairs={{0,96},{32,0},{64,32},{96,64},{1,97},{33,1},{65,33},{97,65},{2,98}... | collective-permute-start | bytes 393224 | tf_op jit(solution)/shard_map/ppermute | solution.py:461
  98.0 2.3 %collective-permute-start.7 = (f32[2,128,128]{2,1,0:T(8,128)S(1)}, f32[2,128,128]{2,1,0:T(8,128)S(1)}, u32[]{:S(2)}, u32[]{:S(2)}) collective-permute-start(f32[2,128,128]{2,1,0:T(8,128)S(1)} %copy-done.10), channel_id=1, source_target_pairs={{0,64},{32,96},{64,0},{96,32},{1,65},{33,97},{65,1},{97,33},{2,66}... | collective-permute-start | bytes 393224 | tf_op jit(solution)/shard_map/ppermute | solution.py:461
  100.3 2.0 %collective-permute-done.8.three_back = f32[2,128,128]{2,1,0:T(8,128)S(1)} collective-permute-done((f32[2,128,128]{2,1,0:T(8,128)S(1)}, f32[2,128,128]{2,1,0:T(8,128)S(1)}, u32[]{:S(2)}, u32[]{:S(2)}) %collective-permute-start.8) | collective-permute-done | bytes 131104 | tf_op jit(solution)/shard_map/ppermute | solution.py:461
  102.3 2.8 %collective-permute-done.7.two_back = f32[2,128,128]{2,1,0:T(8,128)S(1)} collective-permute-done((f32[2,128,128]{2,1,0:T(8,128)S(1)}, f32[2,128,128]{2,1,0:T(8,128)S(1)}, u32[]{:S(2)}, u32[]{:S(2)}) %collective-permute-start.7) | collective-permute-done | bytes 131104 | tf_op jit(solution)/shard_map/ppermute | solution.py:461
  105.1 1.6 collective-permute-done.6.one_back
  106.8 0.7 copy-done.9
  107.4 3.0 %shard_map.87 = (f32[2,128,128]{2,1,0:T(8,128)}, f32[2,128,128]{2,1,0:T(8,128)}) custom-call(s32[2]{0:T(128)} %pad_add_fusion.place, f32[2,2,128,128]{3,2,1,0:T(8,128)} %get-tuple-element.26.mine, f32[2,2,128,128]{3,2,1,0:T(8,128)} %copy-done, f32[2,2,128,128]{3,2,1,0:T(8,128)} %copy-done.3, f32[2,2,128,128]{3,2,1,0:T(8,128)} %copy-done.2, ...), custom_call_target="tpu_custom_call" | custom-call | tf_op jit(solution)/shard_map/pallas_call | solution.py:466
  110.5 1.6 collective-permute-done.9.other
  112.0 0.7 copy-done.5
  112.7 15.4 %key_grads.1 = bf16[1024,1024]{1,0:T(8,128)(2,1)} custom-call(s32[2]{0:T(128)} %pad_add_fusion.place, bf16[1024,512]{1,0:T(8,128)(2,1)} %query.9, bf16[1024,512]{1,0:T(8,128)(2,1)} %key.7, bf16[1024,512]{1,0:T(8,128)(2,1)} %grad.5, f32[1,512]{1,0:T(1,128)} %bitcast.24, f32[2,128,128]{2,1,0:T(8,128)} %get-tuple-element.42.mine, f32[2,128,128]{2,1,0:T(8,128)} %copy-done.5, ...), custom_call_target="tpu_custom_call" | custom-call | tf_op jit(solution)/shard_map/key_grads/pallas_call | solution.py:551
  128.1 6.9 %all-to-all-start.3 = ((bf16[16,64,1024]{2,1,0:T(8,128)(2,1)}), bf16[16,64,1024]{2,1,0:T(8,128)(2,1)S(1)}, u32[]{:S(2)}, u32[]{:S(2)}) async-start(bf16[16,64,1024]{2,1,0:T(8,128)(2,1)} %bitcast.17), calls=%async_computation.3 | async-start | bytes 4194304 | tf_op jit(solution)/shard_map/all_to_all | solution.py:436
  135.0 1.1 copy.12
  136.1 30.1 %all-to-all-done.3 = bf16[16,64,1024]{2,1,0:T(8,128)(2,1)S(1)} async-done(((bf16[16,64,1024]{2,1,0:T(8,128)(2,1)}), bf16[16,64,1024]{2,1,0:T(8,128)(2,1)S(1)}, u32[]{:S(2)}, u32[]{:S(2)}) %all-to-all-start.3) | async-done | bytes 2097184 | tf_op jit(solution)/shard_map/all_to_all | solution.py:436
  166.4 1.1 copy.14
  167.5 1.1 copy.13
  (30 shorter events, 2.3 us)
Async XLA Ops:
  20.5 1.8 %collective-permute-start = (f32[2,2,128,128]{3,2,1,0:T(8,128)}, f32[2,2,128,128]{3,2,1,0:T(8,128)S(1)}, u32[]{:S(2)}, u32[]{:S(2)}) collective-permute-start(f32[2,2,128,128]{3,2,1,0:T(8,128)} %get-tuple-element.27), channel_id=1, source_target_pairs={{0,16},{16,0},{1,17},{17,1},{2,18},{18,2},{3,19},{19,3},{4,20},{20... | collective-permute-start | bytes 786440 | tf_op jit(solution)/shard_map/ppermute | solution.py:455
  22.3 0.7 copy-start
  25.1 33.9 %collective-permute-start.3 = (f32[2,2,128,128]{3,2,1,0:T(8,128)}, f32[2,2,128,128]{3,2,1,0:T(8,128)S(1)}, u32[]{:S(2)}, u32[]{:S(2)}) collective-permute-start(f32[2,2,128,128]{3,2,1,0:T(8,128)} %shard_map.85), channel_id=1, source_target_pairs={{0,96},{32,0},{64,32},{96,64},{1,97},{33,1},{65,33},{97,65},{2,98}... | collective-permute-start | bytes 786440 | tf_op jit(solution)/shard_map/ppermute | solution.py:461
  29.2 29.8 %collective-permute-start.2 = (f32[2,2,128,128]{3,2,1,0:T(8,128)}, f32[2,2,128,128]{3,2,1,0:T(8,128)S(1)}, u32[]{:S(2)}, u32[]{:S(2)}) collective-permute-start(f32[2,2,128,128]{3,2,1,0:T(8,128)} %shard_map.85), channel_id=1, source_target_pairs={{0,64},{32,96},{64,0},{96,32},{1,65},{33,97},{65,1},{97,33},{2,66}... | collective-permute-start | bytes 786440 | tf_op jit(solution)/shard_map/ppermute | solution.py:461
  29.2 29.8 %collective-permute-start.1 = (f32[2,2,128,128]{3,2,1,0:T(8,128)}, f32[2,2,128,128]{3,2,1,0:T(8,128)S(1)}, u32[]{:S(2)}, u32[]{:S(2)}) collective-permute-start(f32[2,2,128,128]{3,2,1,0:T(8,128)} %shard_map.85), channel_id=1, source_target_pairs={{0,32},{32,64},{64,96},{96,0},{1,33},{33,65},{65,97},{97,1},{2,34}... | collective-permute-start | bytes 786440 | tf_op jit(solution)/shard_map/ppermute | solution.py:461
  57.2 1.8 %collective-permute-start.4 = (f32[2,128,128]{2,1,0:T(8,128)}, f32[2,128,128]{2,1,0:T(8,128)S(1)}, u32[]{:S(2)}, u32[]{:S(2)}) collective-permute-start(f32[2,128,128]{2,1,0:T(8,128)} %get-tuple-element.33), channel_id=1, source_target_pairs={{0,16},{16,0},{1,17},{17,1},{2,18},{18,2},{3,19},{19,3},{4,20},{20... | collective-permute-start | bytes 393224 | tf_op jit(solution)/shard_map/ppermute | solution.py:455
  59.0 0.7 copy-start.4
  59.0 0.8 copy-start.1
  59.0 0.8 copy-start.2
  59.0 0.9 copy-start.3
  63.0 1.6 collective-permute-start.5
  64.6 0.6 copy-start.6
  92.1 3.8 %copy-start.10 = (f32[2,128,128]{2,1,0:T(8,128)S(1)}, f32[2,128,128]{2,1,0:T(8,128)}, u32[]{:S(2)}) copy-start(f32[2,128,128]{2,1,0:T(8,128)} %get-tuple-element.41) | copy-start | bytes 393220
  92.1 36.0 %all-to-all-start.2 = ((bf16[16,64,512]{2,1,0:T(8,128)(2,1)}), bf16[16,64,512]{2,1,0:T(8,128)(2,1)S(1)}, u32[]{:S(2)}, u32[]{:S(2)}) async-start(bf16[16,64,512]{2,1,0:T(8,128)(2,1)} %bitcast.16), calls=%async_computation.2 | async-start | bytes 2097152 | tf_op jit(solution)/shard_map/all_to_all | solution.py:436
  95.9 6.4 %collective-permute-start.8 = (f32[2,128,128]{2,1,0:T(8,128)S(1)}, f32[2,128,128]{2,1,0:T(8,128)S(1)}, u32[]{:S(2)}, u32[]{:S(2)}) collective-permute-start(f32[2,128,128]{2,1,0:T(8,128)S(1)} %copy-done.10), channel_id=1, source_target_pairs={{0,96},{32,0},{64,32},{96,64},{1,97},{33,1},{65,33},{97,65},{2,98}... | collective-permute-start | bytes 393224 | tf_op jit(solution)/shard_map/ppermute | solution.py:461
  98.0 7.1 %collective-permute-start.7 = (f32[2,128,128]{2,1,0:T(8,128)S(1)}, f32[2,128,128]{2,1,0:T(8,128)S(1)}, u32[]{:S(2)}, u32[]{:S(2)}) collective-permute-start(f32[2,128,128]{2,1,0:T(8,128)S(1)} %copy-done.10), channel_id=1, source_target_pairs={{0,64},{32,96},{64,0},{96,32},{1,65},{33,97},{65,1},{97,33},{2,66}... | collective-permute-start | bytes 393224 | tf_op jit(solution)/shard_map/ppermute | solution.py:461
  100.3 6.5 %collective-permute-start.6 = (f32[2,128,128]{2,1,0:T(8,128)S(1)}, f32[2,128,128]{2,1,0:T(8,128)S(1)}, u32[]{:S(2)}, u32[]{:S(2)}) collective-permute-start(f32[2,128,128]{2,1,0:T(8,128)S(1)} %copy-done.10), channel_id=1, source_target_pairs={{0,32},{32,64},{64,96},{96,0},{1,33},{33,65},{65,97},{97,1},{2,34}... | collective-permute-start | bytes 393224 | tf_op jit(solution)/shard_map/ppermute | solution.py:461
  102.3 4.5 %copy-start.7 = (f32[2,128,128]{2,1,0:T(8,128)}, f32[2,128,128]{2,1,0:T(8,128)S(1)}, u32[]{:S(2)}) copy-start(f32[2,128,128]{2,1,0:T(8,128)S(1)} %collective-permute-done.8.three_back) | copy-start | bytes 393220
  105.1 1.7 copy-start.8
  106.8 0.7 copy-start.9
  110.5 1.6 collective-permute-start.9
  112.0 0.7 copy-start.5
  128.1 38.1 %all-to-all-start.3 = ((bf16[16,64,1024]{2,1,0:T(8,128)(2,1)}), bf16[16,64,1024]{2,1,0:T(8,128)(2,1)S(1)}, u32[]{:S(2)}, u32[]{:S(2)}) async-start(bf16[16,64,1024]{2,1,0:T(8,128)(2,1)} %bitcast.17), calls=%async_computation.3 | async-start | bytes 4194304 | tf_op jit(solution)/shard_map/all_to_all | solution.py:436

commit v5 on v4

--- a/solution.py
+++ b/solution.py
@@ -16,6 +16,7 @@
 SEQ = ("seq_0", "seq_1")
 SEQ_HEAD = ("seq_0", "seq_1", "head_0", "head_1")
 EPS = 1e-06
+BASE = 16
 SCALE = C ** (-0.5)
 
 f32 = jnp.float32
@@ -72,17 +73,44 @@
     return ref[b * C : (b + 1) * C, h * C : (h + 1) * C]
 
 
-def square_sums(query, out):
+def square_sums(heads, query, out, lines):
+    step = pl.program_id(0)
     blocks = query.shape[0] // C
-    ones = jnp.full((out.shape[0], query.shape[1]), 1.0, bf16)
-    wide = query[...].astype(f32)
-    sums = mul_right(nt, ones, halves(wide * wide))
     for b in range(blocks):
-        out[:, b] = sums[:, b * C : (b + 1) * C]
+        total = jnp.zeros((C, C), f32)
+        for h in range(heads):
+            wide = tile(query, b, h).astype(f32)
+            total += wide * wide
+        lines[pl.ds(step * blocks + b, 1)] = jnp.sum(total.T, axis=0, keepdims=True)
+
+    @pl.when(step == pl.num_programs(0) - 1)
+    def _():
+        out[...] = jnp.broadcast_to(lines[...][None], out.shape)
+
+
+def placed(kernel, *settings):
+    def run(*refs):
+        kernel(*settings, (lax.axis_index("seq_0"), lax.axis_index("seq_1")), *refs)
+
+    return run
 
 
 def all_units(pair, heads):
     return [(b, h) for b in range(pair) for h in range(heads)]
+
+
+def block_inverses(lower):
+    row, col = iotas()
+    inside = (row // BASE) == (col // BASE)
+    packed = jnp.sum(jnp.where(inside, lower, 0.0).reshape(C // BASE, BASE, C), axis=0)
+    place_row = lax.broadcasted_iota(jnp.int32, (BASE, C), 0)
+    place_col = lax.broadcasted_iota(jnp.int32, (BASE, C), 1)
+    result = jnp.where(place_row == place_col % BASE, 1.0, 0.0)
+    for j in range(BASE - 1):
+        entry = (place_col // BASE) * BASE + j
+        factor = jnp.take_along_axis(packed, entry, axis=1, mode="promise_in_bounds")
+        result = result - factor * result[j : j + 1]
+    return jnp.where(inside, jnp.concatenate([result] * (C // BASE), axis=0), 0.0)
 
 
 def prep_keys(pair, heads, steps, place, key, value, decay, inv, weight, trans, shift, cols, rows, mine, other, whole, offset):
@@ -136,10 +164,8 @@
         )
 
     apart = row ^ col
-    result = [
-        jnp.where(row == col, 1.0, 0.0) - jnp.where(apart == 1, lower[u], 0.0) for u in range(count)
-    ]
-    size = 2
+    result = [block_inverses(lower[u]) for u in range(count)]
+    size = BASE
     while size < C:
         here = (apart >= size) & (apart < 2 * size)
         split = [halves(x) for x in result]
@@ -332,7 +358,7 @@
         part[...] = jnp.broadcast_to(sums_so_far[...][None], part.shape)
 
 
-def finish_queries(pair, query, scaled, norm_cols, sums, out, corrections):
+def finish_queries(pair, heads, query, scaled, norm_cols, sums, out, corrections):
     step = pl.program_id(0)
 
     @pl.when(step == 0)
@@ -343,9 +369,13 @@
     columns = columns_of(jnp.concatenate(lines, axis=0))
     for b in range(pair):
         part = slice(b * C, (b + 1) * C)
-        norm = norm_cols[part][:, :1]
+        norm = norm_cols[part]
         factor = norm * norm * columns[:, b : b + 1]
-        out[part] = (norm * scaled[part] - query[part].astype(f32) * factor).astype(bf16)
+        for h in range(heads):
+            side = slice(h * C, (h + 1) * C)
+            out[part, side] = (
+                norm * scaled[part, side] - query[part, side].astype(f32) * factor
+            ).astype(bf16)
 
 
 def key_grads(pair, heads, place, query, key, grad, gain, mine, other, inv, trans, adjoint, inner, fresh, starts, cols, rows, norm_rows, ready, out, state):
@@ -446,8 +476,6 @@
     chips = lax.axis_size("seq_0")
     assert (chips, cores) == (4, 2) and heads % 2 == 0
     some = heads // 2
-    place = jnp.stack([lax.axis_index("seq_0"), lax.axis_index("seq_1")]).astype(jnp.int32)
-    scalar = pl.BlockSpec(memory_space=pltpu.SMEM)
     pair_maps = shape((some, 2, C, C), f32)
     pair_states = shape((some, C, C), f32)
 
@@ -465,54 +493,61 @@
     def small(kernel, out_shape, *operands):
         return pl.pallas_call(
             kernel,
-            in_specs=[scalar] + [pl.BlockSpec(memory_space=pltpu.VMEM)] * (len(operands) - 1),
+            in_specs=[pl.BlockSpec(memory_space=pltpu.VMEM)] * len(operands),
             out_shape=out_shape,
         )(*operands)
 
     squares = exchange(
-        pl.pallas_call(square_sums, out_shape=sums, name="square_sums")(query_raw), HEAD
+        pl.pallas_call(
+            functools.partial(square_sums, heads),
+            grid=(2,),
+            in_specs=[pl.BlockSpec((rows // 2, width), lambda i: (i, 0))],
+            out_specs=fixed(group, blocks, C),
+            out_shape=sums,
+            scratch_shapes=[line_scratch],
+            name="square_sums",
+        )(query_raw),
+        HEAD,
     )
 
     steps, tokens, matrix, column, line = specs(PAIRS[0])
     inv, weight, trans, shift, cols, row_info, mine, other = pl.pallas_call(
-        functools.partial(prep_keys, PAIRS[0], heads, steps),
+        placed(prep_keys, PAIRS[0], heads, steps),
         grid=(steps,),
-        in_specs=[scalar, tokens, tokens, pl.BlockSpec((heads, PAIRS[0] * C), lambda i: (0, i))],
+        in_specs=[tokens, tokens, pl.BlockSpec((heads, PAIRS[0] * C), lambda i: (0, i))],
         out_specs=[matrix] * 4 + [column, line] + [fixed(some, 2, C, C)] * 2,
         out_shape=[matrices] * 4 + [columns, lines, pair_maps, pair_maps],
         scratch_shapes=[carry, carry],
         name="prep_keys",
-    )(place, key_raw, value_raw, log_decay)
+    )(key_raw, value_raw, log_decay)
     other = to_other_core(other)
-    behind = from_chips_behind(small(chip_maps, pair_maps, place, mine, other))
+    behind = from_chips_behind(small(placed(chip_maps), pair_maps, mine, other))
 
     steps, tokens, matrix, column, line = specs(PAIRS[1], reverse=True)
     inner, adjoint, norm_cols, norm_rows, mine_back, other_back = pl.pallas_call(
-        functools.partial(prep_queries, PAIRS[1], heads, steps),
+        placed(prep_queries, PAIRS[1], heads, steps),
         grid=(steps,),
-        in_specs=[scalar]
-        + [tokens] * 3
+        in_specs=[tokens] * 3
         + [fixed(1, width), fixed(group, blocks, C)]
         + [matrix, matrix, column, line],
         out_specs=[matrix, matrix, column, line] + [fixed(some, C, C)] * 2,
         out_shape=[matrices, matrices, columns, lines, pair_states, pair_states],
         scratch_shapes=[carry, line_scratch],
         name="prep_queries",
-    )(place, query_raw, key_raw, out_grad, gain, squares, weight, trans, cols, row_info)
+    )(query_raw, key_raw, out_grad, gain, squares, weight, trans, cols, row_info)
     other_back = to_other_core(other_back)
     stay, leave, back = small(
-        chip_states, [pair_states] * 3,
-        place, mine, other, *behind, mine_back, other_back,
+        placed(chip_states), [pair_states] * 3,
+        mine, other, *behind, mine_back, other_back,
     )
     arrived = to_other_core(leave)
     ahead = from_chips_behind(back)
 
     steps, tokens, matrix, column, line = specs(PAIRS[2])
     scaled, fresh, starts, part = pl.pallas_call(
-        functools.partial(query_grads, PAIRS[2], heads, steps),
+        placed(query_grads, PAIRS[2], heads, steps),
         grid=(steps,),
-        in_specs=[scalar]
-        + [tokens] * 4
+        in_specs=[tokens] * 4
         + [fixed(1, width), fixed(some, C, C), fixed(some, C, C)]
         + [matrix] * 4
         + [column, line, column],
@@ -521,14 +556,14 @@
         scratch_shapes=[carry, line_scratch],
         name="query_grads",
     )(
-        place, query_raw, key_raw, value_raw, out_grad, gain, stay, arrived,
+        query_raw, key_raw, value_raw, out_grad, gain, stay, arrived,
         inv, weight, trans, shift, cols, row_info, norm_cols,
     )
     corrections = exchange(part, HEAD)
 
     stay, leave = small(
-        functools.partial(chip_adjoints, chips - 1), [pair_states] * 2,
-        place, mine, other, *behind, *ahead, mine_back, other_back,
+        placed(chip_adjoints, chips - 1), [pair_states] * 2,
+        mine, other, *behind, *ahead, mine_back, other_back,
     )
     arrived = to_other_core(leave)
 
@@ -537,7 +572,7 @@
 
     steps, tokens, matrix, column, line = specs(PAIRS[3])
     query_raw_grad = pl.pallas_call(
-        functools.partial(finish_queries, PAIRS[3]),
+        functools.partial(finish_queries, PAIRS[3], heads),
         grid=(steps,),
         in_specs=[tokens, tokens, column, fixed(group, blocks, C)],
         out_specs=tokens,
@@ -549,10 +584,9 @@
 
     steps, tokens, matrix, column, line = specs(PAIRS[4], reverse=True)
     key_value = pl.pallas_call(
-        functools.partial(key_grads, PAIRS[4], heads),
+        placed(key_grads, PAIRS[4], heads),
         grid=(steps,),
-        in_specs=[scalar]
-        + [tokens] * 3
+        in_specs=[tokens] * 3
         + [fixed(1, width), fixed(some, C, C), fixed(some, C, C)]
         + [matrix] * 6
         + [column, line, line, pl.BlockSpec(memory_space=pl.ANY)],
@@ -561,7 +595,7 @@
         scratch_shapes=[carry],
         name="key_grads",
     )(
-        place, query_raw, key_raw, out_grad, gain, stay, arrived,
+        query_raw, key_raw, out_grad, gain, stay, arrived,
         inv, trans, adjoint, inner, fresh, starts, cols, row_info, norm_rows, query_raw_grad,
     )
     second = owned(key_value)

time: 169 us -> 166 us (0.982)
  Pallas kernels: 69.8 us -> 67.1 us
    pallas_call x9, Pallas kernels: 69.8 us -> 67.1 us  [the longest x1 17.4 us: per_device(): pl.pallas_call(placed(prep_keys, PAIRS[0], heads, steps), grid=(steps,),...]
where the time goes in v5:
time: 166 us; the launch traced here: 165 us
  Pallas kernels  67.1 us (40%)
  waiting for transfers between devices  42.8 us (26%)
  blocking collectives  26.6 us (16%)
  starting transfers between devices  20.8 us (13%)
  local copies, waits for them, and re-layouts  7.07 us (4%)
    all_to_all x2, waiting for transfers between devices, exchange(): return lax.all_to_all(value, axis, 0, 0, tiled=True)  30.1 us
    all_to_all x2, blocking collectives, exchange(): return lax.all_to_all(value, axis, 0, 0, tiled=True)  26.6 us
    pallas_call x1, Pallas kernels, per_device(): pl.pallas_call(placed(prep_keys, PAIRS[0], heads, steps), grid=(steps,),...  17.4 us
    pallas_call x1, Pallas kernels, per_device(): pl.pallas_call(placed(key_grads, PAIRS[4], heads), grid=(steps,), in_spec...  15.4 us
    pallas_call x1, Pallas kernels, per_device(): pl.pallas_call(placed(query_grads, PAIRS[2], heads, steps), grid=(steps,)...  11.7 us
    all_to_all x2, starting transfers between devices, exchange(): return lax.all_to_all(value, axis, 0, 0, tiled=True)  10.7 us
    ppermute x6, starting transfers between devices, from_chips_behind(): lax.ppermute(value, 'seq_0', [(i, (i + k) % chips) for i in range(chips)])  9.77 us
    pallas_call x1, Pallas kernels, per_device(): pl.pallas_call(placed(prep_queries, PAIRS[1], heads, steps), grid=(steps,...  9.27 us
  transfers between devices with their start and end apart: 12, of which 8 were waited for; matrix products, arithmetic and copies ran while one was open for 1% of the time, Pallas kernels for 18%

profile of v5, /device:TPU:0, one launch (start us, length us, event | category | flops | bytes accessed | tf_op | source)
XLA Modules:
  0.0 165.1 jit_solution(15808949650808702792)
XLA Ops:
  0.6 17.4 %prep_keys.1 = (f32[8,4,128,128]{3,2,1,0:T(8,128)}, f32[8,4,128,128]{3,2,1,0:T(8,128)}, f32[8,4,128,128]{3,2,1,0:T(8,128)}, f32[8,4,128,128]{3,2,1,0:T(8,128)}, ...) custom-call(bf16[1024,512]{1,0:T(8,128)(2,1)} %refs_1_.7, ...), custom_call_target="tpu_custom_call" | custom-call | tf_op jit(solution)/shard_map/prep_keys/pallas_call | solution.py:514
  18.1 1.7 %collective-permute-done.refs_1_ = f32[2,2,128,128]{3,2,1,0:T(8,128)S(1)} collective-permute-done((f32[2,2,128,128]{3,2,1,0:T(8,128)}, f32[2,2,128,128]{3,2,1,0:T(8,128)S(1)}, u32[]{:S(2)}, u32[]{:S(2)}) %collective-permute-start) | collective-permute-done | bytes 262176 | tf_op jit(solution)/shard_map/ppermute | solution.py:483
  19.9 0.7 copy-done
  20.6 2.0 %shard_map.85 = f32[2,2,128,128]{3,2,1,0:T(8,128)} custom-call(f32[2,2,128,128]{3,2,1,0:T(8,128)} %get-tuple-element.26.refs_0_, f32[2,2,128,128]{3,2,1,0:T(8,128)} %copy-done), custom_call_target="tpu_custom_call" | custom-call | tf_op jit(solution)/shard_map/pallas_call | solution.py:494
  22.6 4.1 %collective-permute-start.3 = (f32[2,2,128,128]{3,2,1,0:T(8,128)}, f32[2,2,128,128]{3,2,1,0:T(8,128)S(1)}, u32[]{:S(2)}, u32[]{:S(2)}) collective-permute-start(f32[2,2,128,128]{3,2,1,0:T(8,128)} %shard_map.85), channel_id=1, source_target_pairs={{0,96},{32,0},{64,32},{96,64},{1,97},{33,1},{65,33},{97,65},{2,98}... | collective-permute-start | bytes 786440 | tf_op jit(solution)/shard_map/ppermute | solution.py:489
  26.8 1.3 collective-permute-start.1
  28.0 2.0 %square_sums.1 = f32[16,8,128]{2,1,0:T(8,128)} custom-call(bf16[1024,512]{1,0:T(8,128)(2,1)} %refs_0_.7), custom_call_target="tpu_custom_call" | custom-call | tf_op jit(solution)/shard_map/square_sums/pallas_call | solution.py:501
  30.1 14.8 %all_to_all.20.refs_4_ = f32[16,8,128]{2,1,0:T(8,128)} all-to-all(f32[16,8,128]{2,1,0:T(8,128)} %square_sums.1), channel_id=1, replica_groups=mesh['seq_0'=4,'seq_1'=2,'head_0'=4,'head_1'=4] {'head_0','head_1'}, dimensions={0} | all-to-all | bytes 131072 | tf_op jit(solution)/shard_map/all_to_all | solution.py:466
  44.9 9.3 %prep_queries.1 = (f32[8,4,128,128]{3,2,1,0:T(8,128)}, f32[8,4,128,128]{3,2,1,0:T(8,128)}, f32[1024,128]{1,0:T(8,128)}, f32[8,8,128]{2,1,0:T(8,128)}, f32[2,128,128]{2,1,0:T(8,128)}, /*index=5*/f32[2,128,128]{2,1,0:T(8,128)}) custom-call(bf16[1024,512]{1,0:T(8,128)(2,1)} %refs_0_.7, bf16[1024,512]{1,0:T(8,128)(2,1)} %refs_1_.7, bf16[1024,512]{1,0:T(8,128)(2,1)} %refs_2_.7, ...), custom_call_target="tpu_custom_call" | custom-call | tf_op jit(solution)/shard_map/prep_queries/pallas_call | solution.py:527
  54.2 1.5 collective-permute-done.4.refs_6_.refs_9_
  56.7 3.1 %shard_map.86 = (f32[2,128,128]{2,1,0:T(8,128)}, f32[2,128,128]{2,1,0:T(8,128)}, f32[2,128,128]{2,1,0:T(8,128)}) custom-call(f32[2,2,128,128]{3,2,1,0:T(8,128)} %get-tuple-element.26.refs_0_, f32[2,2,128,128]{3,2,1,0:T(8,128)} %copy-done, f32[2,2,128,128]{3,2,1,0:T(8,128)} %copy-done.3, f32[2,2,128,128]{3,2,1,0:T(8,128)} %copy-done.2, ...), custom_call_target="tpu_custom_call" | custom-call | tf_op jit(solution)/shard_map/pallas_call | solution.py:494
  60.0 1.4 collective-permute-done.5.refs_6_
  61.4 0.6 copy-done.6
  62.0 11.7 %query_grads.1 = (f32[1024,512]{1,0:T(8,128)}, f32[8,4,128,128]{3,2,1,0:T(8,128)}, f32[8,4,128,128]{3,2,1,0:T(8,128)}, f32[16,8,128]{2,1,0:T(8,128)}) custom-call(bf16[1024,512]{1,0:T(8,128)(2,1)} %refs_0_.7, bf16[1024,512]{1,0:T(8,128)(2,1)} %refs_1_.7, bf16[1024,512]{1,0:T(8,128)(2,1)} %refs_2_.6, bf16[1024,512]{1,0:T(8,128)(2,1)} %refs_2_.7, ...), custom_call_target="tpu_custom_call" | custom-call | tf_op jit(solution)/shard_map/query_grads/pallas_call | solution.py:547
  73.7 11.8 %all_to_all.21.sums = f32[16,8,128]{2,1,0:T(8,128)} all-to-all(f32[16,8,128]{2,1,0:T(8,128)} %get-tuple-element.40), channel_id=1, replica_groups=mesh['seq_0'=4,'seq_1'=2,'head_0'=4,'head_1'=4] {'head_0','head_1'}, dimensions={0} | all-to-all | bytes 131072 | tf_op jit(solution)/shard_map/all_to_all | solution.py:466
  85.5 3.2 %finish_queries.1.refs_15_ = bf16[1024,512]{1,0:T(8,128)(2,1)} custom-call(bf16[1024,512]{1,0:T(8,128)(2,1)} %refs_0_.7, f32[1024,512]{1,0:T(8,128)} %get-tuple-element.39.scaled, f32[1024,128]{1,0:T(8,128)} %get-tuple-element.38.refs_13_.norm_cols, f32[16,8,128]{2,1,0:T(8,128)} %all_to_all.21.sums), custom_call_target="tpu_custom_call" | custom-call | tf_op jit(solution)/shard_map/finish_queries/pallas_call | solution.py:574
  88.7 3.8 %all-to-all-start.2 = ((bf16[16,64,512]{2,1,0:T(8,128)(2,1)}), bf16[16,64,512]{2,1,0:T(8,128)(2,1)S(1)}, u32[]{:S(2)}, u32[]{:S(2)}) async-start(bf16[16,64,512]{2,1,0:T(8,128)(2,1)} %bitcast.14), calls=%async_computation.2 | async-start | bytes 2097152 | tf_op jit(solution)/shard_map/all_to_all | solution.py:466
  92.5 2.0 %collective-permute-start.8 = (f32[2,128,128]{2,1,0:T(8,128)S(1)}, f32[2,128,128]{2,1,0:T(8,128)S(1)}, u32[]{:S(2)}, u32[]{:S(2)}) collective-permute-start(f32[2,128,128]{2,1,0:T(8,128)S(1)} %copy-done.10), channel_id=1, source_target_pairs={{0,96},{32,0},{64,32},{96,64},{1,97},{33,1},{65,33},{97,65},{2,98}... | collective-permute-start | bytes 393224 | tf_op jit(solution)/shard_map/ppermute | solution.py:489
  94.5 2.3 %collective-permute-start.7 = (f32[2,128,128]{2,1,0:T(8,128)S(1)}, f32[2,128,128]{2,1,0:T(8,128)S(1)}, u32[]{:S(2)}, u32[]{:S(2)}) collective-permute-start(f32[2,128,128]{2,1,0:T(8,128)S(1)} %copy-done.10), channel_id=1, source_target_pairs={{0,64},{32,96},{64,0},{96,32},{1,65},{33,97},{65,1},{97,33},{2,66}... | collective-permute-start | bytes 393224 | tf_op jit(solution)/shard_map/ppermute | solution.py:489
  96.9 2.0 %collective-permute-done.8.refs_7_ = f32[2,128,128]{2,1,0:T(8,128)S(1)} collective-permute-done((f32[2,128,128]{2,1,0:T(8,128)S(1)}, f32[2,128,128]{2,1,0:T(8,128)S(1)}, u32[]{:S(2)}, u32[]{:S(2)}) %collective-permute-start.8) | collective-permute-done | bytes 131104 | tf_op jit(solution)/shard_map/ppermute | solution.py:489
  98.9 2.8 %collective-permute-done.7.refs_6_ = f32[2,128,128]{2,1,0:T(8,128)S(1)} collective-permute-done((f32[2,128,128]{2,1,0:T(8,128)S(1)}, f32[2,128,128]{2,1,0:T(8,128)S(1)}, u32[]{:S(2)}, u32[]{:S(2)}) %collective-permute-start.7) | collective-permute-done | bytes 131104 | tf_op jit(solution)/shard_map/ppermute | solution.py:489
  101.7 1.6 collective-permute-done.6.refs_5_
  103.3 0.7 copy-done.9
  104.0 3.0 %shard_map.87 = (f32[2,128,128]{2,1,0:T(8,128)}, f32[2,128,128]{2,1,0:T(8,128)}) custom-call(f32[2,2,128,128]{3,2,1,0:T(8,128)} %get-tuple-element.26.refs_0_, f32[2,2,128,128]{3,2,1,0:T(8,128)} %copy-done, f32[2,2,128,128]{3,2,1,0:T(8,128)} %copy-done.3, f32[2,2,128,128]{3,2,1,0:T(8,128)} %copy-done.2, f32[2,2,128,128]{3,2,1,0:T(8,128)} %copy-done.1, ...), custom_call_target="tpu_custom_call" | custom-call | tf_op jit(solution)/shard_map/pallas_call | solution.py:494
  107.0 1.6 collective-permute-done.9.refs_5_
  108.6 0.7 copy-done.5
  109.2 15.4 %key_grads.1 = bf16[1024,1024]{1,0:T(8,128)(2,1)} custom-call(bf16[1024,512]{1,0:T(8,128)(2,1)} %refs_0_.7, bf16[1024,512]{1,0:T(8,128)(2,1)} %refs_1_.7, bf16[1024,512]{1,0:T(8,128)(2,1)} %refs_2_.7, f32[1,512]{1,0:T(1,128)} %bitcast.22, f32[2,128,128]{2,1,0:T(8,128)} %get-tuple-element.42.refs_4_, f32[2,128,128]{2,1,0:T(8,128)} %copy-done.5, ...), custom_call_target="tpu_custom_call" | custom-call | tf_op jit(solution)/shard_map/key_grads/pallas_call | solution.py:586
  124.6 6.9 %all-to-all-start.3 = ((bf16[16,64,1024]{2,1,0:T(8,128)(2,1)}), bf16[16,64,1024]{2,1,0:T(8,128)(2,1)S(1)}, u32[]{:S(2)}, u32[]{:S(2)}) async-start(bf16[16,64,1024]{2,1,0:T(8,128)(2,1)} %bitcast.15), calls=%async_computation.3 | async-start | bytes 4194304 | tf_op jit(solution)/shard_map/all_to_all | solution.py:466
  131.5 1.1 copy.12
  132.6 30.1 %all-to-all-done.3 = bf16[16,64,1024]{2,1,0:T(8,128)(2,1)S(1)} async-done(((bf16[16,64,1024]{2,1,0:T(8,128)(2,1)}), bf16[16,64,1024]{2,1,0:T(8,128)(2,1)S(1)}, u32[]{:S(2)}, u32[]{:S(2)}) %all-to-all-start.3) | async-done | bytes 2097184 | tf_op jit(solution)/shard_map/all_to_all | solution.py:466
  163.0 1.1 copy.14
  164.1 1.1 copy.13
  (29 shorter events, 1.5 us)
Async XLA Ops:
  18.1 1.8 %collective-permute-start = (f32[2,2,128,128]{3,2,1,0:T(8,128)}, f32[2,2,128,128]{3,2,1,0:T(8,128)S(1)}, u32[]{:S(2)}, u32[]{:S(2)}) collective-permute-start(f32[2,2,128,128]{3,2,1,0:T(8,128)} %get-tuple-element.27), channel_id=1, source_target_pairs={{0,16},{16,0},{1,17},{17,1},{2,18},{18,2},{3,19},{19,3},{4,20},{20... | collective-permute-start | bytes 786440 | tf_op jit(solution)/shard_map/ppermute | solution.py:483
  19.9 0.7 copy-start
  22.6 33.2 %collective-permute-start.3 = (f32[2,2,128,128]{3,2,1,0:T(8,128)}, f32[2,2,128,128]{3,2,1,0:T(8,128)S(1)}, u32[]{:S(2)}, u32[]{:S(2)}) collective-permute-start(f32[2,2,128,128]{3,2,1,0:T(8,128)} %shard_map.85), channel_id=1, source_target_pairs={{0,96},{32,0},{64,32},{96,64},{1,97},{33,1},{65,33},{97,65},{2,98}... | collective-permute-start | bytes 786440 | tf_op jit(solution)/shard_map/ppermute | solution.py:489
  26.8 29.0 %collective-permute-start.2 = (f32[2,2,128,128]{3,2,1,0:T(8,128)}, f32[2,2,128,128]{3,2,1,0:T(8,128)S(1)}, u32[]{:S(2)}, u32[]{:S(2)}) collective-permute-start(f32[2,2,128,128]{3,2,1,0:T(8,128)} %shard_map.85), channel_id=1, source_target_pairs={{0,64},{32,96},{64,0},{96,32},{1,65},{33,97},{65,1},{97,33},{2,66}... | collective-permute-start | bytes 786440 | tf_op jit(solution)/shard_map/ppermute | solution.py:489
  26.8 29.1 %collective-permute-start.1 = (f32[2,2,128,128]{3,2,1,0:T(8,128)}, f32[2,2,128,128]{3,2,1,0:T(8,128)S(1)}, u32[]{:S(2)}, u32[]{:S(2)}) collective-permute-start(f32[2,2,128,128]{3,2,1,0:T(8,128)} %shard_map.85), channel_id=1, source_target_pairs={{0,32},{32,64},{64,96},{96,0},{1,33},{33,65},{65,97},{97,1},{2,34}... | collective-permute-start | bytes 786440 | tf_op jit(solution)/shard_map/ppermute | solution.py:489
  54.1 1.6 collective-permute-start.4
  55.8 0.7 copy-start.4
  55.8 0.8 copy-start.1
  55.8 0.8 copy-start.2
  55.8 0.9 copy-start.3
  59.8 1.6 collective-permute-start.5
  61.4 0.6 copy-start.6
  88.7 3.8 %copy-start.10 = (f32[2,128,128]{2,1,0:T(8,128)S(1)}, f32[2,128,128]{2,1,0:T(8,128)}, u32[]{:S(2)}) copy-start(f32[2,128,128]{2,1,0:T(8,128)} %get-tuple-element.41) | copy-start | bytes 393220
  88.7 35.9 %all-to-all-start.2 = ((bf16[16,64,512]{2,1,0:T(8,128)(2,1)}), bf16[16,64,512]{2,1,0:T(8,128)(2,1)S(1)}, u32[]{:S(2)}, u32[]{:S(2)}) async-start(bf16[16,64,512]{2,1,0:T(8,128)(2,1)} %bitcast.14), calls=%async_computation.2 | async-start | bytes 2097152 | tf_op jit(solution)/shard_map/all_to_all | solution.py:466
  92.5 6.4 %collective-permute-start.8 = (f32[2,128,128]{2,1,0:T(8,128)S(1)}, f32[2,128,128]{2,1,0:T(8,128)S(1)}, u32[]{:S(2)}, u32[]{:S(2)}) collective-permute-start(f32[2,128,128]{2,1,0:T(8,128)S(1)} %copy-done.10), channel_id=1, source_target_pairs={{0,96},{32,0},{64,32},{96,64},{1,97},{33,1},{65,33},{97,65},{2,98}... | collective-permute-start | bytes 393224 | tf_op jit(solution)/shard_map/ppermute | solution.py:489
  94.5 7.1 %collective-permute-start.7 = (f32[2,128,128]{2,1,0:T(8,128)S(1)}, f32[2,128,128]{2,1,0:T(8,128)S(1)}, u32[]{:S(2)}, u32[]{:S(2)}) collective-permute-start(f32[2,128,128]{2,1,0:T(8,128)S(1)} %copy-done.10), channel_id=1, source_target_pairs={{0,64},{32,96},{64,0},{96,32},{1,65},{33,97},{65,1},{97,33},{2,66}... | collective-permute-start | bytes 393224 | tf_op jit(solution)/shard_map/ppermute | solution.py:489
  96.9 6.5 %collective-permute-start.6 = (f32[2,128,128]{2,1,0:T(8,128)S(1)}, f32[2,128,128]{2,1,0:T(8,128)S(1)}, u32[]{:S(2)}, u32[]{:S(2)}) collective-permute-start(f32[2,128,128]{2,1,0:T(8,128)S(1)} %copy-done.10), channel_id=1, source_target_pairs={{0,32},{32,64},{64,96},{96,0},{1,33},{33,65},{65,97},{97,1},{2,34}... | collective-permute-start | bytes 393224 | tf_op jit(solution)/shard_map/ppermute | solution.py:489
  98.9 4.5 %copy-start.7 = (f32[2,128,128]{2,1,0:T(8,128)}, f32[2,128,128]{2,1,0:T(8,128)S(1)}, u32[]{:S(2)}) copy-start(f32[2,128,128]{2,1,0:T(8,128)S(1)} %collective-permute-done.8.refs_7_) | copy-start | bytes 393220
  101.7 1.6 copy-start.8
  103.3 0.7 copy-start.9
  107.0 1.6 collective-permute-start.9
  108.6 0.7 copy-start.5
  124.6 38.1 %all-to-all-start.3 = ((bf16[16,64,1024]{2,1,0:T(8,128)(2,1)}), bf16[16,64,1024]{2,1,0:T(8,128)(2,1)S(1)}, u32[]{:S(2)}, u32[]{:S(2)}) async-start(bf16[16,64,1024]{2,1,0:T(8,128)(2,1)} %bitcast.15), calls=%async_computation.3 | async-start | bytes 4194304 | tf_op jit(solution)/shard_map/all_to_all | solution.py:466

commit v6 on v5

--- a/solution.py
+++ b/solution.py
@@ -11,7 +11,7 @@
 
 D = 8192
 C = 128
-PAIRS = (4, 2, 2, 4, 2)
+PAIRS = (8, 8, 2, 4, 2)
 HEAD = ("head_0", "head_1")
 SEQ = ("seq_0", "seq_1")
 SEQ_HEAD = ("seq_0", "seq_1", "head_0", "head_1")
@@ -113,6 +113,14 @@
     return jnp.where(inside, jnp.concatenate([result] * (C // BASE), axis=0), 0.0)
 
 
+def after(early, late):
+    step_map = halves(late[0])
+    return (
+        mul3(nn, step_map, halves(early[0])),
+        mul3(nt, halves(early[1]), step_map) + late[1],
+    )
+
+
 def prep_keys(pair, heads, steps, place, key, value, decay, inv, weight, trans, shift, cols, rows, mine, other, whole, offset):
     step = pl.program_id(0)
     units = all_units(pair, heads)
@@ -193,12 +201,14 @@
         maps.append(jnp.where(row == col, jnp.exp(last[u]), 0.0) - drop)
         trans[b, h] = maps[u]
 
-    for b in range(pair):
-        for h in range(heads):
-            u = b * heads + h
-            step_map = halves(maps[u])
-            whole[h] = mul3(nn, step_map, halves(whole[h]))
-            offset[h] = mul3(nt, halves(offset[h]), step_map) + moved[u]
+    runs = [[(maps[b * heads + h], moved[b * heads + h]) for h in range(heads)] for b in range(pair)]
+    while len(runs) > 1:
+        runs = [
+            [after(early, late) for early, late in zip(runs[i], runs[i + 1])]
+            for i in range(0, len(runs), 2)
+        ]
+    for h in range(heads):
+        whole[h], offset[h] = after((whole[h], offset[h]), runs[0][h])
 
     @pl.when(step == steps - 1)
     def _():
@@ -216,16 +226,14 @@
     for j in range(mine.shape[0]):
         early = [jnp.where(first, mine[j, i], other[j, i]) for i in range(2)]
         late = [jnp.where(first, other[j, i], mine[j, i]) for i in range(2)]
-        step_map = halves(late[0])
-        out[j, 0] = mul3(nn, step_map, halves(early[0]))
-        out[j, 1] = mul3(nt, halves(early[1]), step_map) + late[1]
+        out[j, 0], out[j, 1] = after(early, late)
 
 
 def chip_states(place, mine, other, one, two, three, mine_back, other_back, stay, leave, back):
     first = place[1] == 0
     for j in range(mine.shape[0]):
-        state = jnp.zeros((C, C), f32)
-        for k, behind in ((3, three), (2, two), (1, one)):
+        state = jnp.where(place[0] >= 3, three[j, 1], 0.0)
+        for k, behind in ((2, two), (1, one)):
             moved = mul3(nt, halves(state), halves(behind[j, 0])) + behind[j, 1]
             state = jnp.where(place[0] >= k, moved, state)
         early = [jnp.where(first, mine[j, i], other[j, i]) for i in range(2)]
@@ -241,8 +249,8 @@
 def chip_adjoints(last, place, mine, other, one, two, three, one_back, two_back, three_back, mine_back, other_back, stay, leave):
     first = place[1] == 0
     for j in range(mine.shape[0]):
-        state = jnp.zeros((C, C), f32)
-        for k, ahead, term in ((3, one, one_back), (2, two, two_back), (1, three, three_back)):
+        state = jnp.where(place[0] + 3 <= last, one_back[j], 0.0)
+        for k, ahead, term in ((2, two, two_back), (1, three, three_back)):
             moved = mul3(nn, halves(state), halves(ahead[j, 0])) + term[j]
             state = jnp.where(place[0] + k <= last, moved, state)
         late = jnp.where(first, other[j, 0], mine[j, 0])

time: 166 us -> 164 us (0.988)
  Pallas kernels: 67.1 us -> 65.3 us
where the time goes in v6:
time: 164 us; the launch traced here: 163 us
  Pallas kernels  65.3 us (40%)
  waiting for transfers between devices  42.8 us (26%)
  blocking collectives  26.6 us (16%)
  starting transfers between devices  20.6 us (13%)
  local copies, waits for them, and re-layouts  7.07 us (4%)
    all_to_all x2, waiting for transfers between devices, exchange(): return lax.all_to_all(value, axis, 0, 0, tiled=True)  30.1 us
    all_to_all x2, blocking collectives, exchange(): return lax.all_to_all(value, axis, 0, 0, tiled=True)  26.6 us
    pallas_call x1, Pallas kernels, per_device(): pl.pallas_call(placed(prep_keys, PAIRS[0], heads, steps), grid=(steps,),...  16.7 us
    pallas_call x1, Pallas kernels, per_device(): pl.pallas_call(placed(key_grads, PAIRS[4], heads), grid=(steps,), in_spec...  15.4 us
    pallas_call x1, Pallas kernels, per_device(): pl.pallas_call(placed(query_grads, PAIRS[2], heads, steps), grid=(steps,)...  11.7 us
    all_to_all x2, starting transfers between devices, exchange(): return lax.all_to_all(value, axis, 0, 0, tiled=True)  10.7 us
    ppermute x6, starting transfers between devices, from_chips_behind(): lax.ppermute(value, 'seq_0', [(i, (i + k) % chips) for i in range(chips)])  9.78 us
    pallas_call x1, Pallas kernels, per_device(): pl.pallas_call(placed(prep_queries, PAIRS[1], heads, steps), grid=(steps,...  8.76 us
  transfers between devices with their start and end apart: 12, of which 8 were waited for; matrix products, arithmetic and copies ran while one was open for 1% of the time, Pallas kernels for 18%

profile of v6, /device:TPU:0, one launch (start us, length us, event | category | flops | bytes accessed | tf_op | source)
XLA Modules:
  0.0 163.2 jit_solution(5186697149264282946)
XLA Ops:
  0.6 16.7 %prep_keys.1 = (f32[8,4,128,128]{3,2,1,0:T(8,128)}, f32[8,4,128,128]{3,2,1,0:T(8,128)}, f32[8,4,128,128]{3,2,1,0:T(8,128)}, f32[8,4,128,128]{3,2,1,0:T(8,128)}, ...) custom-call(bf16[1024,512]{1,0:T(8,128)(2,1)} %refs_1_.7, ...), custom_call_target="tpu_custom_call" | custom-call | tf_op jit(solution)/shard_map/prep_keys/pallas_call | solution.py:522
  17.3 1.7 %collective-permute-done.refs_1_ = f32[2,2,128,128]{3,2,1,0:T(8,128)S(1)} collective-permute-done((f32[2,2,128,128]{3,2,1,0:T(8,128)}, f32[2,2,128,128]{3,2,1,0:T(8,128)S(1)}, u32[]{:S(2)}, u32[]{:S(2)}) %collective-permute-start) | collective-permute-done | bytes 262176 | tf_op jit(solution)/shard_map/ppermute | solution.py:491
  19.1 0.7 copy-done
  19.8 2.0 %shard_map.85 = f32[2,2,128,128]{3,2,1,0:T(8,128)} custom-call(f32[2,2,128,128]{3,2,1,0:T(8,128)} %get-tuple-element.26.refs_0_, f32[2,2,128,128]{3,2,1,0:T(8,128)} %copy-done), custom_call_target="tpu_custom_call" | custom-call | tf_op jit(solution)/shard_map/pallas_call | solution.py:502
  21.8 4.2 %collective-permute-start.3 = (f32[2,2,128,128]{3,2,1,0:T(8,128)}, f32[2,2,128,128]{3,2,1,0:T(8,128)S(1)}, u32[]{:S(2)}, u32[]{:S(2)}) collective-permute-start(f32[2,2,128,128]{3,2,1,0:T(8,128)} %shard_map.85), channel_id=1, source_target_pairs={{0,96},{32,0},{64,32},{96,64},{1,97},{33,1},{65,33},{97,65},{2,98}... | collective-permute-start | bytes 786440 | tf_op jit(solution)/shard_map/ppermute | solution.py:497
  26.0 1.3 collective-permute-start.1
  27.2 2.0 %square_sums.1 = f32[16,8,128]{2,1,0:T(8,128)} custom-call(bf16[1024,512]{1,0:T(8,128)(2,1)} %refs_0_.7), custom_call_target="tpu_custom_call" | custom-call | tf_op jit(solution)/shard_map/square_sums/pallas_call | solution.py:509
  29.3 14.8 %all_to_all.20.refs_4_ = f32[16,8,128]{2,1,0:T(8,128)} all-to-all(f32[16,8,128]{2,1,0:T(8,128)} %square_sums.1), channel_id=1, replica_groups=mesh['seq_0'=4,'seq_1'=2,'head_0'=4,'head_1'=4] {'head_0','head_1'}, dimensions={0} | all-to-all | bytes 131072 | tf_op jit(solution)/shard_map/all_to_all | solution.py:474
  44.1 8.8 %prep_queries.1 = (f32[8,4,128,128]{3,2,1,0:T(8,128)}, f32[8,4,128,128]{3,2,1,0:T(8,128)}, f32[1024,128]{1,0:T(8,128)}, f32[8,8,128]{2,1,0:T(8,128)}, f32[2,128,128]{2,1,0:T(8,128)}, /*index=5*/f32[2,128,128]{2,1,0:T(8,128)}) custom-call(bf16[1024,512]{1,0:T(8,128)(2,1)} %refs_0_.7, bf16[1024,512]{1,0:T(8,128)(2,1)} %refs_1_.7, bf16[1024,512]{1,0:T(8,128)(2,1)} %refs_2_.7, ...), custom_call_target="tpu_custom_call" | custom-call | tf_op jit(solution)/shard_map/prep_queries/pallas_call | solution.py:535
  52.8 1.6 collective-permute-done.4.refs_6_.refs_9_
  55.3 2.8 %shard_map.86 = (f32[2,128,128]{2,1,0:T(8,128)}, f32[2,128,128]{2,1,0:T(8,128)}, f32[2,128,128]{2,1,0:T(8,128)}) custom-call(f32[2,2,128,128]{3,2,1,0:T(8,128)} %get-tuple-element.26.refs_0_, f32[2,2,128,128]{3,2,1,0:T(8,128)} %copy-done, f32[2,2,128,128]{3,2,1,0:T(8,128)} %copy-done.3, f32[2,2,128,128]{3,2,1,0:T(8,128)} %copy-done.2, ...), custom_call_target="tpu_custom_call" | custom-call | tf_op jit(solution)/shard_map/pallas_call | solution.py:502
  58.2 1.4 collective-permute-done.5.refs_6_
  59.6 0.6 copy-done.6
  60.3 11.7 %query_grads.1 = (f32[1024,512]{1,0:T(8,128)}, f32[8,4,128,128]{3,2,1,0:T(8,128)}, f32[8,4,128,128]{3,2,1,0:T(8,128)}, f32[16,8,128]{2,1,0:T(8,128)}) custom-call(bf16[1024,512]{1,0:T(8,128)(2,1)} %refs_0_.7, bf16[1024,512]{1,0:T(8,128)(2,1)} %refs_1_.7, bf16[1024,512]{1,0:T(8,128)(2,1)} %refs_2_.6, bf16[1024,512]{1,0:T(8,128)(2,1)} %refs_2_.7, ...), custom_call_target="tpu_custom_call" | custom-call | tf_op jit(solution)/shard_map/query_grads/pallas_call | solution.py:555
  72.0 11.8 %all_to_all.21.sums = f32[16,8,128]{2,1,0:T(8,128)} all-to-all(f32[16,8,128]{2,1,0:T(8,128)} %get-tuple-element.40), channel_id=1, replica_groups=mesh['seq_0'=4,'seq_1'=2,'head_0'=4,'head_1'=4] {'head_0','head_1'}, dimensions={0} | all-to-all | bytes 131072 | tf_op jit(solution)/shard_map/all_to_all | solution.py:474
  83.8 3.2 %finish_queries.1.refs_15_ = bf16[1024,512]{1,0:T(8,128)(2,1)} custom-call(bf16[1024,512]{1,0:T(8,128)(2,1)} %refs_0_.7, f32[1024,512]{1,0:T(8,128)} %get-tuple-element.39.scaled, f32[1024,128]{1,0:T(8,128)} %get-tuple-element.38.refs_13_.norm_cols, f32[16,8,128]{2,1,0:T(8,128)} %all_to_all.21.sums), custom_call_target="tpu_custom_call" | custom-call | tf_op jit(solution)/shard_map/finish_queries/pallas_call | solution.py:582
  87.0 3.8 %all-to-all-start.2 = ((bf16[16,64,512]{2,1,0:T(8,128)(2,1)}), bf16[16,64,512]{2,1,0:T(8,128)(2,1)S(1)}, u32[]{:S(2)}, u32[]{:S(2)}) async-start(bf16[16,64,512]{2,1,0:T(8,128)(2,1)} %bitcast.14), calls=%async_computation.2 | async-start | bytes 2097152 | tf_op jit(solution)/shard_map/all_to_all | solution.py:474
  90.8 2.0 %collective-permute-start.8 = (f32[2,128,128]{2,1,0:T(8,128)S(1)}, f32[2,128,128]{2,1,0:T(8,128)S(1)}, u32[]{:S(2)}, u32[]{:S(2)}) collective-permute-start(f32[2,128,128]{2,1,0:T(8,128)S(1)} %copy-done.10), channel_id=1, source_target_pairs={{0,96},{32,0},{64,32},{96,64},{1,97},{33,1},{65,33},{97,65},{2,98}... | collective-permute-start | bytes 393224 | tf_op jit(solution)/shard_map/ppermute | solution.py:497
  92.8 2.3 %collective-permute-start.7 = (f32[2,128,128]{2,1,0:T(8,128)S(1)}, f32[2,128,128]{2,1,0:T(8,128)S(1)}, u32[]{:S(2)}, u32[]{:S(2)}) collective-permute-start(f32[2,128,128]{2,1,0:T(8,128)S(1)} %copy-done.10), channel_id=1, source_target_pairs={{0,64},{32,96},{64,0},{96,32},{1,65},{33,97},{65,1},{97,33},{2,66}... | collective-permute-start | bytes 393224 | tf_op jit(solution)/shard_map/ppermute | solution.py:497
  95.1 2.0 %collective-permute-done.8.refs_7_ = f32[2,128,128]{2,1,0:T(8,128)S(1)} collective-permute-done((f32[2,128,128]{2,1,0:T(8,128)S(1)}, f32[2,128,128]{2,1,0:T(8,128)S(1)}, u32[]{:S(2)}, u32[]{:S(2)}) %collective-permute-start.8) | collective-permute-done | bytes 131104 | tf_op jit(solution)/shard_map/ppermute | solution.py:497
  97.1 2.8 %collective-permute-done.7.refs_6_ = f32[2,128,128]{2,1,0:T(8,128)S(1)} collective-permute-done((f32[2,128,128]{2,1,0:T(8,128)S(1)}, f32[2,128,128]{2,1,0:T(8,128)S(1)}, u32[]{:S(2)}, u32[]{:S(2)}) %collective-permute-start.7) | collective-permute-done | bytes 131104 | tf_op jit(solution)/shard_map/ppermute | solution.py:497
  99.9 1.6 %collective-permute-done.6.refs_5_ = f32[2,128,128]{2,1,0:T(8,128)S(1)} collective-permute-done((f32[2,128,128]{2,1,0:T(8,128)S(1)}, f32[2,128,128]{2,1,0:T(8,128)S(1)}, u32[]{:S(2)}, u32[]{:S(2)}) %collective-permute-start.6) | collective-permute-done | bytes 131104 | tf_op jit(solution)/shard_map/ppermute | solution.py:497
  101.6 0.7 copy-done.9
  102.2 2.8 %shard_map.87 = (f32[2,128,128]{2,1,0:T(8,128)}, f32[2,128,128]{2,1,0:T(8,128)}) custom-call(f32[2,2,128,128]{3,2,1,0:T(8,128)} %get-tuple-element.26.refs_0_, f32[2,2,128,128]{3,2,1,0:T(8,128)} %copy-done, f32[2,2,128,128]{3,2,1,0:T(8,128)} %copy-done.3, f32[2,2,128,128]{3,2,1,0:T(8,128)} %copy-done.2, f32[2,2,128,128]{3,2,1,0:T(8,128)} %copy-done.1, ...), custom_call_target="tpu_custom_call" | custom-call | tf_op jit(solution)/shard_map/pallas_call | solution.py:502
  105.0 1.6 collective-permute-done.9.refs_5_
  106.6 0.7 copy-done.5
  107.2 15.4 %key_grads.1 = bf16[1024,1024]{1,0:T(8,128)(2,1)} custom-call(bf16[1024,512]{1,0:T(8,128)(2,1)} %refs_0_.7, bf16[1024,512]{1,0:T(8,128)(2,1)} %refs_1_.7, bf16[1024,512]{1,0:T(8,128)(2,1)} %refs_2_.7, f32[1,512]{1,0:T(1,128)} %bitcast.22, f32[2,128,128]{2,1,0:T(8,128)} %get-tuple-element.42.refs_4_, f32[2,128,128]{2,1,0:T(8,128)} %copy-done.5, ...), custom_call_target="tpu_custom_call" | custom-call | tf_op jit(solution)/shard_map/key_grads/pallas_call | solution.py:594
  122.7 6.9 %all-to-all-start.3 = ((bf16[16,64,1024]{2,1,0:T(8,128)(2,1)}), bf16[16,64,1024]{2,1,0:T(8,128)(2,1)S(1)}, u32[]{:S(2)}, u32[]{:S(2)}) async-start(bf16[16,64,1024]{2,1,0:T(8,128)(2,1)} %bitcast.15), calls=%async_computation.3 | async-start | bytes 4194304 | tf_op jit(solution)/shard_map/all_to_all | solution.py:474
  129.6 1.1 copy.12
  130.6 30.1 %all-to-all-done.3 = bf16[16,64,1024]{2,1,0:T(8,128)(2,1)S(1)} async-done(((bf16[16,64,1024]{2,1,0:T(8,128)(2,1)}), bf16[16,64,1024]{2,1,0:T(8,128)(2,1)S(1)}, u32[]{:S(2)}, u32[]{:S(2)}) %all-to-all-start.3) | async-done | bytes 2097184 | tf_op jit(solution)/shard_map/all_to_all | solution.py:474
  161.0 1.1 copy.14
  162.1 1.1 copy.13
  (29 shorter events, 1.4 us)
Async XLA Ops:
  17.3 1.7 %collective-permute-start = (f32[2,2,128,128]{3,2,1,0:T(8,128)}, f32[2,2,128,128]{3,2,1,0:T(8,128)S(1)}, u32[]{:S(2)}, u32[]{:S(2)}) collective-permute-start(f32[2,2,128,128]{3,2,1,0:T(8,128)} %get-tuple-element.27), channel_id=1, source_target_pairs={{0,16},{16,0},{1,17},{17,1},{2,18},{18,2},{3,19},{19,3},{4,20},{20... | collective-permute-start | bytes 786440 | tf_op jit(solution)/shard_map/ppermute | solution.py:491
  19.1 0.7 copy-start
  21.8 32.6 %collective-permute-start.3 = (f32[2,2,128,128]{3,2,1,0:T(8,128)}, f32[2,2,128,128]{3,2,1,0:T(8,128)S(1)}, u32[]{:S(2)}, u32[]{:S(2)}) collective-permute-start(f32[2,2,128,128]{3,2,1,0:T(8,128)} %shard_map.85), channel_id=1, source_target_pairs={{0,96},{32,0},{64,32},{96,64},{1,97},{33,1},{65,33},{97,65},{2,98}... | collective-permute-start | bytes 786440 | tf_op jit(solution)/shard_map/ppermute | solution.py:497
  26.0 28.4 %collective-permute-start.2 = (f32[2,2,128,128]{3,2,1,0:T(8,128)}, f32[2,2,128,128]{3,2,1,0:T(8,128)S(1)}, u32[]{:S(2)}, u32[]{:S(2)}) collective-permute-start(f32[2,2,128,128]{3,2,1,0:T(8,128)} %shard_map.85), channel_id=1, source_target_pairs={{0,64},{32,96},{64,0},{96,32},{1,65},{33,97},{65,1},{97,33},{2,66}... | collective-permute-start | bytes 786440 | tf_op jit(solution)/shard_map/ppermute | solution.py:497
  26.0 28.4 %collective-permute-start.1 = (f32[2,2,128,128]{3,2,1,0:T(8,128)}, f32[2,2,128,128]{3,2,1,0:T(8,128)S(1)}, u32[]{:S(2)}, u32[]{:S(2)}) collective-permute-start(f32[2,2,128,128]{3,2,1,0:T(8,128)} %shard_map.85), channel_id=1, source_target_pairs={{0,32},{32,64},{64,96},{96,0},{1,33},{33,65},{65,97},{97,1},{2,34}... | collective-permute-start | bytes 786440 | tf_op jit(solution)/shard_map/ppermute | solution.py:497
  52.8 1.6 collective-permute-start.4
  54.4 0.7 copy-start.4
  54.4 0.8 copy-start.1
  54.4 0.8 copy-start.2
  54.4 0.9 copy-start.3
  58.1 1.6 collective-permute-start.5
  59.6 0.6 copy-start.6
  87.0 3.8 %copy-start.10 = (f32[2,128,128]{2,1,0:T(8,128)S(1)}, f32[2,128,128]{2,1,0:T(8,128)}, u32[]{:S(2)}) copy-start(f32[2,128,128]{2,1,0:T(8,128)} %get-tuple-element.41) | copy-start | bytes 393220
  87.0 35.7 %all-to-all-start.2 = ((bf16[16,64,512]{2,1,0:T(8,128)(2,1)}), bf16[16,64,512]{2,1,0:T(8,128)(2,1)S(1)}, u32[]{:S(2)}, u32[]{:S(2)}) async-start(bf16[16,64,512]{2,1,0:T(8,128)(2,1)} %bitcast.14), calls=%async_computation.2 | async-start | bytes 2097152 | tf_op jit(solution)/shard_map/all_to_all | solution.py:474
  90.8 6.4 %collective-permute-start.8 = (f32[2,128,128]{2,1,0:T(8,128)S(1)}, f32[2,128,128]{2,1,0:T(8,128)S(1)}, u32[]{:S(2)}, u32[]{:S(2)}) collective-permute-start(f32[2,128,128]{2,1,0:T(8,128)S(1)} %copy-done.10), channel_id=1, source_target_pairs={{0,96},{32,0},{64,32},{96,64},{1,97},{33,1},{65,33},{97,65},{2,98}... | collective-permute-start | bytes 393224 | tf_op jit(solution)/shard_map/ppermute | solution.py:497
  92.8 7.1 %collective-permute-start.7 = (f32[2,128,128]{2,1,0:T(8,128)S(1)}, f32[2,128,128]{2,1,0:T(8,128)S(1)}, u32[]{:S(2)}, u32[]{:S(2)}) collective-permute-start(f32[2,128,128]{2,1,0:T(8,128)S(1)} %copy-done.10), channel_id=1, source_target_pairs={{0,64},{32,96},{64,0},{96,32},{1,65},{33,97},{65,1},{97,33},{2,66}... | collective-permute-start | bytes 393224 | tf_op jit(solution)/shard_map/ppermute | solution.py:497
  95.1 6.5 %collective-permute-start.6 = (f32[2,128,128]{2,1,0:T(8,128)S(1)}, f32[2,128,128]{2,1,0:T(8,128)S(1)}, u32[]{:S(2)}, u32[]{:S(2)}) collective-permute-start(f32[2,128,128]{2,1,0:T(8,128)S(1)} %copy-done.10), channel_id=1, source_target_pairs={{0,32},{32,64},{64,96},{96,0},{1,33},{33,65},{65,97},{97,1},{2,34}... | collective-permute-start | bytes 393224 | tf_op jit(solution)/shard_map/ppermute | solution.py:497
  97.1 4.5 %copy-start.7 = (f32[2,128,128]{2,1,0:T(8,128)}, f32[2,128,128]{2,1,0:T(8,128)S(1)}, u32[]{:S(2)}) copy-start(f32[2,128,128]{2,1,0:T(8,128)S(1)} %collective-permute-done.8.refs_7_) | copy-start | bytes 393220
  99.9 1.7 %copy-start.8 = (f32[2,128,128]{2,1,0:T(8,128)}, f32[2,128,128]{2,1,0:T(8,128)S(1)}, u32[]{:S(2)}) copy-start(f32[2,128,128]{2,1,0:T(8,128)S(1)} %collective-permute-done.7.refs_6_) | copy-start | bytes 393220
  101.6 0.7 copy-start.9
  105.0 1.6 collective-permute-start.9
  106.6 0.7 copy-start.5
  122.7 38.1 %all-to-all-start.3 = ((bf16[16,64,1024]{2,1,0:T(8,128)(2,1)}), bf16[16,64,1024]{2,1,0:T(8,128)(2,1)S(1)}, u32[]{:S(2)}, u32[]{:S(2)}) async-start(bf16[16,64,1024]{2,1,0:T(8,128)(2,1)} %bitcast.15), calls=%async_computation.3 | async-start | bytes 4194304 | tf_op jit(solution)/shard_map/all_to_all | solution.py:474
